TPU v7x, 32 devices: a whole 2x2x4 slice. The times are simulated.
32 devices in a mesh: gx: 16 (over z, y, x), gy: 2 (over core).
Axes of the slice: x: 2, y: 2, z: 4, core: 2. Of those that a mesh axis runs over, the one named last changes fastest.
Arguments:
- features: bfloat16 [16, 2, 8, 128, 256], P('gx', 'gy'), may hold values from -6 to 6
- kernel_weight: bfloat16 [27, 256, 256], P(None, 'gy'), may hold values from -0.109375 to 0.109375
- channel_bias: float32 [256], replicated, may hold values from -3 to 3
- send_list: int32 [16, 2, 2], P('gx', 'gy'), may hold values from 0 to 7
- rule_source: int32 [16, 2, 27, 4], P('gx', 'gy'), may hold values from 0 to 23
- rule_target: int32 [16, 2, 27, 4], P('gx', 'gy'), may hold values from 0 to 7
- live_counts: int32 [16, 2, 27], P('gx', 'gy'), may hold values from 1 to 4, as said below
- out_grad: bfloat16 [16, 2, 8, 128, 256], P('gx', 'gy'), may hold values from -6 to 6
Outputs:
- outputs: bfloat16 [16, 2, 8, 128, 256], P('gx', 'gy')
- feat_grad: bfloat16 [16, 2, 8, 128, 256], P('gx', 'gy')
- weight_grad: float32 [27, 256, 256], P(None, 'gy')
Inputs may be any that keep to these rules, and one draw needn't show every extreme that they name: `rule_source`: index into the device's block table of its 8 own blocks followed by 2 blocks from each of the eight directions. `rule_target`: an own block of the device. `send_list`: an own block of the device; a block may appear more than once. `live_counts`: slots from this count up to 3 are padding whose indices carry no meaning.
All inputs are finite; a program needn't handle non-finite values.
Results may differ from a plain program's by a relative error of at most 0.007.
Values may be sent and summed in bfloat16 or wider, within the bound.
A program may use at most 128 MiB of HBM per device.

v0:
```python
import functools

import jax
import jax.numpy as jnp
from jax import lax
from jax.experimental import pallas as pl
from jax.experimental.pallas import tpu as pltpu
from jax.sharding import PartitionSpec as P

MESH = pl.DeviceIdType.MESH
VMEM = pltpu.VMEM
SMEM = pltpu.SMEM
LANES = 128
TILE = 16
KINDS = (2, 0, 1, 3, 0, 1, 0, 1, 0)
WAVES = (0,) * 9
STAGGER = 1
HALO_AT = 4
UNROLL = 9
VMEM_BYTES = 28 * 1024 * 1024
EXCHANGE_BYTES = 28 * 1024 * 1024


def greet_neighbours(barrier, me_x, me_y, nx, ny):
    total = 0
    for sx, sy in ((-1, 0), (1, 0), (0, -1), (0, 1)):
        x, y = me_x + sx, me_y + sy
        there = (x >= 0) & (x < nx) & (y >= 0) & (y < ny)

        @pl.when(there)
        def _():
            pl.semaphore_signal(barrier, inc=1, device_id=(x, y), device_id_type=MESH)

        total = total + there.astype(jnp.int32)
    return total


def greet_column(barrier, me_x, me_y, ny):
    for step in range(1, ny):
        pl.semaphore_signal(
            barrier, inc=1, device_id=(me_x, lax.rem(me_y + step, ny)), device_id_type=MESH
        )
    return ny - 1


def exists(index, count):
    return (index >= 0) & (index < count)


def exchange_kernel(
    nx, ny, send_ref, feats_ref, weight_ref, halo_ref, full_ref, feats, lsem, xsend, xrecv, hsend, hrecv, wsend, wrecv
):
    me_x, me_y = lax.axis_index("gx"), lax.axis_index("gy")
    barrier = pltpu.get_barrier_semaphore()
    expected = greet_neighbours(barrier, me_x, me_y, nx, ny) + greet_column(
        barrier, me_x, me_y, ny
    )
    load = pltpu.make_async_copy(feats_ref, feats, lsem.at[0])
    load.start()
    keep = pltpu.make_async_copy(weight_ref, full_ref.at[:, me_y], lsem.at[1])
    keep.start()
    load.wait()
    for s in range(halo_ref.shape[1]):
        halo_ref[4, s] = feats[send_ref[s]]
    pl.semaphore_wait(barrier, expected)

    def x_copy(a, device_x):
        return pltpu.make_async_remote_copy(
            src_ref=halo_ref.at[4],
            dst_ref=halo_ref.at[3 * a + 1],
            send_sem=xsend.at[a // 2],
            recv_sem=xrecv.at[a // 2],
            device_id=(device_x, me_y),
            device_id_type=MESH,
        )

    def y_copy(a, b, device_y):
        return pltpu.make_async_remote_copy(
            src_ref=halo_ref.at[3 * a + 1],
            dst_ref=halo_ref.at[3 * a + b],
            send_sem=hsend.at[a, b // 2],
            recv_sem=hrecv.at[a, b // 2],
            device_id=(me_x, device_y),
            device_id_type=MESH,
        )

    def weight_copy(step, owner):
        return pltpu.make_async_remote_copy(
            src_ref=weight_ref,
            dst_ref=full_ref.at[:, owner],
            send_sem=wsend.at[step],
            recv_sem=wrecv.at[step],
            device_id=(me_x, lax.rem(me_y + step, ny)),
            device_id_type=MESH,
        )

    def to_column(a, act):
        for b in (0, 2):
            target = me_y + 1 - b

            @pl.when(exists(target, ny))
            def _():
                act(y_copy(a, b, target))

    for a in (0, 2):
        target = me_x + 1 - a

        @pl.when(exists(target, nx))
        def _():
            x_copy(a, target).start()

    to_column(1, lambda copy: copy.start())
    for step in range(1, ny):
        weight_copy(step, me_y).start()
    blank = jnp.zeros(halo_ref.shape[1:], halo_ref.dtype)
    for a in (0, 2):
        here = exists(me_x + a - 1, nx)

        @pl.when(jnp.logical_not(here))
        def _():
            halo_ref[3 * a + 1] = blank

        @pl.when(here)
        def _():
            x_copy(a, me_x + a - 1).wait_recv()
            to_column(a, lambda copy: copy.start())

    for a in range(3):
        for b in (0, 2):
            there = exists(me_x + a - 1, nx) & exists(me_y + b - 1, ny)

            @pl.when(jnp.logical_not(there))
            def _():
                halo_ref[3 * a + b] = blank

            @pl.when(there)
            def _():
                y_copy(a, b, me_y + b - 1).wait_recv()

        @pl.when(exists(me_x + a - 1, nx))
        def _():
            to_column(a, lambda copy: copy.wait_send())

    for a in (0, 2):
        target = me_x + 1 - a

        @pl.when(exists(target, nx))
        def _():
            x_copy(a, target).wait_send()

    for step in range(1, ny):
        weight_copy(step, lax.rem(me_y - step + ny, ny)).wait_recv()
        weight_copy(step, me_y).wait_send()
    keep.wait()


def compute_kernel(
    source_ref,
    target_ref,
    count_ref,
    feats_ref,
    halo_ref,
    weight_ref,
    bias_ref,
    cot_ref,
    out_ref,
    own_ref,
    borrowed_ref,
    wpart_ref,
    table,
    turned,
    pre,
    dpre,
    grad,
):
    blocks, rows, width = feats_ref.shape
    slots = source_ref.shape[0]
    kvol = weight_ref.shape[0]
    total_blocks = grad.shape[0] - 1
    shared_count = halo_ref.shape[1]
    ny, tiles = wpart_ref.shape[:2]
    share = width // ny
    share_tiles = share // TILE
    places = [(b, feats_ref.at[b]) for b in range(blocks)]
    at = blocks
    for d in range(9):
        if d != 4:
            for s in range(shared_count):
                places.append((at, halo_ref.at[d, s]))
                at += 1
    for t, ref in places:
        value = ref[...]
        table[t] = value
        turned[t] = value.T
    for b in range(blocks):
        pre[b] = jnp.broadcast_to(bias_ref[...], (rows, width))
    for t in range(total_blocks):
        grad[t] = jnp.zeros((rows, width), jnp.float32)
    pre[blocks] = jnp.zeros((rows, width), jnp.float32)
    grad[total_blocks] = jnp.zeros((rows, width), jnp.float32)
    dpre[blocks] = jnp.zeros((rows, width), dpre.dtype)

    def rules(k):
        live = count_ref[k]
        sources = [source_ref[q, k] for q in range(slots)]
        targets = [target_ref[q, k] for q in range(slots)]
        reads = [jnp.where(q < live, v, 0) for q, v in enumerate(sources)]
        spread = [jnp.where(q < live, v, total_blocks) for q, v in enumerate(sources)]
        targets = [jnp.where(q < live, v, blocks) for q, v in enumerate(targets)]
        return reads, spread, targets

    def forward(k, carry):
        reads, _, targets = rules(k)
        taken = jnp.concatenate([table[s] for s in reads], axis=0)
        made = jnp.dot(taken, weight_ref[k], preferred_element_type=jnp.float32)
        for q, target in enumerate(targets):
            pre[target] += made[q * rows : (q + 1) * rows]
        return carry

    lax.fori_loop(0, kvol, forward, 0, unroll=UNROLL)

    def activate(b, carry):
        value = pre[b]
        sig = jax.nn.sigmoid(value)
        out_ref[b] = (value * sig).astype(out_ref.dtype)
        dpre[b] = (cot_ref[b].astype(jnp.float32) * sig * (1.0 + value * (1.0 - sig))).astype(
            dpre.dtype
        )
        return carry

    lax.fori_loop(0, blocks, activate, 0)

    filled = 2 * kvol * share_tiles
    if filled < tiles:
        for y in range(ny):
            wpart_ref[y, filled:] = jnp.zeros((tiles - filled, TILE, LANES), wpart_ref.dtype)

    def backward(k, carry):
        reads, spread, targets = rules(k)
        pulled = jnp.concatenate([dpre[t] for t in targets], axis=0)
        taken = jnp.concatenate([turned[s] for s in reads], axis=1)
        part = jnp.dot(taken, pulled, preferred_element_type=jnp.float32).astype(wpart_ref.dtype)
        for y in range(ny):
            for h in range(width // LANES):
                piece = part[y * share : (y + 1) * share, h * LANES : (h + 1) * LANES]
                wpart_ref[y, pl.ds((h * kvol + k) * share_tiles, share_tiles)] = piece.reshape(
                    share_tiles, TILE, LANES
                )
        back = lax.dot_general(
            pulled, weight_ref[k], (((1,), (1,)), ((), ())), preferred_element_type=jnp.float32
        )
        for q, source in enumerate(spread):
            grad[source] += back[q * rows : (q + 1) * rows]
        return carry

    lax.fori_loop(0, kvol, backward, 0, unroll=UNROLL)
    for b in range(blocks):
        own_ref[b] = grad[b]
    at = blocks
    for d in range(9):
        for s in range(shared_count):
            if d == 4:
                borrowed_ref[d, s] = jnp.zeros((rows, width), borrowed_ref.dtype)
            else:
                borrowed_ref[d, s] = grad[at].astype(borrowed_ref.dtype)
                at += 1


def reduce_kernel(
    nx,
    ny,
    wpart_ref,
    borrowed_ref,
    sum_ref,
    returned_ref,
    work,
    yland,
    xland,
    side_land,
    column,
    x_land,
    ysend,
    yrecv,
    rsend,
    rrecv,
    gsend,
    grecv,
    hsend,
    hrecv,
    bsend,
    brecv,
):
    me_x, me_y = lax.axis_index("gx"), lax.axis_index("gy")
    groups = work.shape[0]
    steps = nx.bit_length() - 1
    bits = [lax.rem(me_x // (1 << b), 2) for b in range(steps)]
    partners = [me_x + (1 - 2 * bits[b]) * (1 << b) for b in range(steps)]

    barrier = pltpu.get_barrier_semaphore()
    expected = greet_neighbours(barrier, me_x, me_y, nx, ny) + greet_column(
        barrier, me_x, me_y, ny
    )
    for b in range(steps):
        pl.semaphore_signal(barrier, inc=1, device_id=(partners[b], me_y), device_id_type=MESH)
    pl.semaphore_wait(barrier, expected + steps)

    def side_copy(a, b):
        return pltpu.make_async_remote_copy(
            src_ref=borrowed_ref.at[3 * a + b],
            dst_ref=side_land.at[a, b // 2],
            send_sem=hsend.at[a, b // 2],
            recv_sem=hrecv.at[a, b // 2],
            device_id=(me_x, me_y + b - 1),
            device_id_type=MESH,
        )

    def back_copy(a):
        return pltpu.make_async_remote_copy(
            src_ref=column.at[a // 2],
            dst_ref=x_land.at[a // 2],
            send_sem=bsend.at[a // 2],
            recv_sem=brecv.at[a // 2],
            device_id=(me_x + a - 1, me_y),
            device_id_type=MESH,
        )

    def sides(act, sign):
        for a in range(3):
            for b in (0, 2):

                @pl.when(exists(me_x + a - 1, nx) & exists(me_y + sign * (b - 1), ny))
                def _():
                    act(a, b)

    def column_copy(step, g):
        other = lax.rem(me_y + step, ny)
        return pltpu.make_async_remote_copy(
            src_ref=wpart_ref.at[other, g],
            dst_ref=yland.at[step - 1, g],
            send_sem=ysend.at[step - 1, g],
            recv_sem=yrecv.at[step - 1, g],
            device_id=(me_x, other),
            device_id_type=MESH,
        )

    late = list(range(2, steps))
    kinds = [[0, 1] + late, [1, 0] + late, late + [0, 1], late + [1, 0]]
    orders = [kinds[kind] for kind in KINDS]
    starts = []
    for g in range(groups):
        at = [0]
        for s in range(steps):
            at.append(at[-1] + bits[orders[g][s]] * (nx >> (s + 1)))
        starts.append(at)

    def scatter_copy(g, s):
        half = nx >> (s + 1)
        bit = bits[orders[g][s]]
        away = starts[g][s] + (1 - bit) * half
        return pltpu.make_async_remote_copy(
            src_ref=work.at[g, pl.ds(away, half)],
            dst_ref=xland.at[g, pl.ds(nx - 2 * half, half)],
            send_sem=rsend.at[s, g],
            recv_sem=rrecv.at[s, g],
            device_id=(partners[orders[g][s]], me_y),
            device_id_type=MESH,
        )

    def gather_copy(g, s, landing):
        half = nx >> (s + 1)
        bit = bits[orders[g][s]]
        mine = starts[g][s + 1]
        place = starts[g][s] + (1 - bit) * half if landing else mine
        return pltpu.make_async_remote_copy(
            src_ref=sum_ref.at[g, pl.ds(mine, half)],
            dst_ref=sum_ref.at[g, pl.ds(place, half)],
            send_sem=gsend.at[s, g],
            recv_sem=grecv.at[s, g],
            device_id=(partners[orders[g][s]], me_y),
            device_id_type=MESH,
        )

    for g in range(groups):
        for step in range(1, ny):
            column_copy(step, g).start()
    sides(lambda a, b: side_copy(a, b).start(), 1)

    def begin(g):
        value = wpart_ref[me_y, g].astype(jnp.float32)
        for step in range(1, ny):
            column_copy(step, g).wait_recv()
            value = value + yland[step - 1, g].astype(jnp.float32)
        work[g] = value.astype(work.dtype)
        scatter_copy(g, 0).start()

    def scatter(g, s):
        half = nx >> (s + 1)
        scatter_copy(g, s).wait_recv()
        keep = pl.ds(starts[g][s + 1], half)
        value = work[g, keep].astype(jnp.float32) + xland[g, pl.ds(nx - 2 * half, half)].astype(
            jnp.float32
        )
        if s < steps - 1:
            work[g, keep] = value.astype(work.dtype)
            scatter_copy(g, s + 1).start()
        else:
            sum_ref[g, keep] = value.astype(sum_ref.dtype)
            gather_copy(g, s, False).start()

    def gather(g, s):
        gather_copy(g, s, True).wait_recv()
        if s > 0:
            gather_copy(g, s - 1, False).start()

    events = []
    for g in range(groups):
        events.append((WAVES[g] * STAGGER, g, functools.partial(begin, g)))
        for s in range(steps):
            events.append((WAVES[g] * STAGGER + s + 1, g, functools.partial(scatter, g, s)))
            events.append(
                (WAVES[g] * STAGGER + 2 * steps - s, g, functools.partial(gather, g, s))
            )
    events.sort(key=lambda event: event[:2])
    first = [event[2] for event in events if event[0] < HALO_AT]
    rest = [event[2] for event in events if event[0] >= HALO_AT]
    for event in first:
        event()

    returned_ref[...] = jnp.zeros(returned_ref.shape, jnp.float32)
    for b in (0, 2):

        @pl.when(exists(me_y + 1 - b, ny))
        def _():
            side_copy(1, b).wait_recv()
            returned_ref[...] += side_land[1, b // 2].astype(jnp.float32)

    for a in (0, 2):

        @pl.when(exists(me_x + a - 1, nx))
        def _():
            for b in (0, 2):
                missing = jnp.logical_not(exists(me_y + 1 - b, ny))

                @pl.when(missing)
                def _():
                    side_land[a, b // 2] = jnp.zeros(side_land.shape[2:], side_land.dtype)

                @pl.when(jnp.logical_not(missing))
                def _():
                    side_copy(a, b).wait_recv()

            column[a // 2] = (
                borrowed_ref[3 * a + 1].astype(jnp.float32)
                + side_land[a, 0].astype(jnp.float32)
                + side_land[a, 1].astype(jnp.float32)
            ).astype(column.dtype)
            back_copy(a).start()

    for event in rest:
        event()

    for a in (0, 2):

        @pl.when(exists(me_x + 1 - a, nx))
        def _():
            back_copy(a).wait_recv()
            returned_ref[...] += x_land[a // 2].astype(jnp.float32)

    for g in range(groups):
        for step in range(1, ny):
            column_copy(step, g).wait_send()
        for s in range(steps):
            scatter_copy(g, s).wait_send()
            gather_copy(g, s, False).wait_send()
    sides(lambda a, b: side_copy(a, b).wait_send(), 1)
    for a in (0, 2):

        @pl.when(exists(me_x + a - 1, nx))
        def _():
            back_copy(a).wait_send()


def finish_kernel(
    send_ref, total_ref, own_ref, returned_ref, weight_ref, feat_ref, wide, feats, wsem, fsem
):
    chunks = wsem.shape[0]
    kvol, share, width = wide.shape
    per = kvol // chunks
    blocks, rows = own_ref.shape[:2]
    copies = []
    for c in range(chunks):
        at = pl.ds(c * per, per)
        for h in range(width // LANES):
            wide[at, :, h * LANES : (h + 1) * LANES] = total_ref[h, at].reshape(
                per, share, LANES
            ).astype(jnp.float32) * (1.0 / rows)
        copy = pltpu.make_async_copy(wide.at[at], weight_ref.at[at], wsem.at[c])
        copy.start()
        copies.append(copy)
    for b in range(blocks):
        value = own_ref[b]
        for s in range(returned_ref.shape[0]):
            value = value + jnp.where(send_ref[s] == b, returned_ref[s], 0.0)
        feats[b] = value.astype(feats.dtype)
        copy = pltpu.make_async_copy(feats.at[b], feat_ref.at[b], fsem.at[b])
        copy.start()
        copies.append(copy)
    for copy in copies:
        copy.wait()


def on_device(
    nx,
    ny,
    features,
    kernel_weight,
    channel_bias,
    send_list,
    rule_source,
    rule_target,
    live_counts,
    out_grad,
):
    feats = features[0, 0]
    blocks, rows, width = feats.shape
    shared = send_list[0, 0]
    shared_count = shared.shape[0]
    kvol, slots = rule_source.shape[2:]
    share = kernel_weight.shape[1]
    bf16, f32 = jnp.bfloat16, jnp.float32
    shape = jax.ShapeDtypeStruct
    vmem = pl.BlockSpec(memory_space=VMEM)
    smem = pl.BlockSpec(memory_space=SMEM)
    hbm = pl.BlockSpec(memory_space=pltpu.HBM)
    dma = pltpu.SemaphoreType.DMA
    squares = 9

    halo, full = pl.pallas_call(
        functools.partial(exchange_kernel, nx, ny),
        out_shape=(
            shape((squares, shared_count, rows, width), bf16),
            shape((kvol, ny, share, width), bf16),
        ),
        in_specs=[smem, hbm, hbm],
        out_specs=(vmem, vmem),
        scratch_shapes=[
            VMEM((blocks, rows, width), bf16),
            dma((2,)),
            dma((2,)),
            dma((2,)),
            dma((3, 2)),
            dma((3, 2)),
            dma((ny,)),
            dma((ny,)),
        ],
        compiler_params=pltpu.CompilerParams(
            collective_id=0, has_side_effects=True, vmem_limit_bytes=EXCHANGE_BYTES
        ),
    )(shared, feats, kernel_weight)

    total_blocks = blocks + (squares - 1) * shared_count
    used = (width // LANES) * kvol * (share // TILE)
    groups = len(KINDS)
    unit = groups * nx
    tiles = -(-used // unit) * unit
    depth = tiles // unit
    outputs, own, borrowed, wpart = pl.pallas_call(
        compute_kernel,
        out_shape=(
            shape((blocks, rows, width), bf16),
            shape((blocks, rows, width), f32),
            shape((squares, shared_count, rows, width), bf16),
            shape((ny, tiles, TILE, LANES), bf16),
        ),
        in_specs=[smem, smem, smem, vmem, vmem, vmem, vmem, vmem],
        out_specs=(vmem, vmem, vmem, vmem),
        scratch_shapes=[
            VMEM((total_blocks, rows, width), bf16),
            VMEM((total_blocks, width, rows), bf16),
            VMEM((blocks + 1, rows, width), f32),
            VMEM((blocks + 1, rows, width), bf16),
            VMEM((total_blocks + 1, rows, width), f32),
        ],
        compiler_params=pltpu.CompilerParams(vmem_limit_bytes=VMEM_BYTES),
    )(
        rule_source[0, 0].T,
        rule_target[0, 0].T,
        live_counts.reshape(-1),
        feats,
        halo,
        full.reshape(kvol, width, width),
        channel_bias.reshape(1, width),
        out_grad[0, 0],
    )

    steps = nx.bit_length() - 1
    block = (depth, TILE, LANES)
    boundary = (shared_count, rows, width)
    total, returned = pl.pallas_call(
        functools.partial(reduce_kernel, nx, ny),
        out_shape=(
            shape((groups, nx) + block, bf16),
            shape(boundary, f32),
        ),
        in_specs=[vmem, vmem],
        out_specs=(vmem, vmem),
        scratch_shapes=[
            VMEM((groups, nx) + block, bf16),
            VMEM((max(ny - 1, 1), groups, nx) + block, bf16),
            VMEM((groups, nx) + block, bf16),
            VMEM((3, 2) + boundary, bf16),
            VMEM((2,) + boundary, bf16),
            VMEM((2,) + boundary, bf16),
            dma((max(ny - 1, 1), groups)),
            dma((max(ny - 1, 1), groups)),
            dma((steps, groups)),
            dma((steps, groups)),
            dma((steps, groups)),
            dma((steps, groups)),
            dma((3, 2)),
            dma((3, 2)),
            dma((2,)),
            dma((2,)),
        ],
        compiler_params=pltpu.CompilerParams(
            collective_id=1, has_side_effects=True, vmem_limit_bytes=VMEM_BYTES
        ),
    )(wpart.reshape((ny, groups, nx) + block), borrowed)

    halves, share_tiles = width // LANES, share // TILE
    chunks = max(c for c in range(1, 10) if kvol % c == 0)
    weight_grad, feat_grad = pl.pallas_call(
        finish_kernel,
        out_shape=(shape((kvol, share, width), f32), shape((blocks, rows, width), bf16)),
        in_specs=[smem, vmem, vmem, vmem],
        out_specs=(hbm, hbm),
        scratch_shapes=[
            VMEM((kvol, share, width), f32),
            VMEM((blocks, rows, width), bf16),
            dma((chunks,)),
            dma((blocks,)),
        ],
        compiler_params=pltpu.CompilerParams(vmem_limit_bytes=VMEM_BYTES),
    )(
        shared,
        total.reshape(tiles, TILE, LANES)[:used].reshape(halves, kvol, share_tiles, TILE, LANES),
        own,
        returned,
    )
    return (outputs[None, None], feat_grad[None, None], weight_grad)


def solution(mesh):
    return jax.shard_map(
        functools.partial(on_device, mesh.shape["gx"], mesh.shape["gy"]),
        mesh=mesh,
        in_specs=(
            P("gx", "gy", None, None, None),
            P(None, "gy", None),
            P(),
            P("gx", "gy", None),
            P("gx", "gy", None, None),
            P("gx", "gy", None, None),
            P("gx", "gy", None),
            P("gx", "gy", None, None, None),
        ),
        out_specs=(
            P("gx", "gy", None, None, None),
            P("gx", "gy", None, None, None),
            P(None, "gy", None),
        ),
        check_vma=False,
    )
```

profile of v0, /device:TPU:0, one launch (start us, length us, event | category | flops | bytes accessed | tf_op | source)
XLA Modules:
  0.0 74.3 jit_solution(14464254750256536962)
XLA Ops:
  0.6 0.0 copy-start.8
  0.6 0.0 copy-start.5
  0.7 0.0 copy-start.4
  0.7 0.0 copy-start.7
  0.7 0.0 copy-start
  0.7 1.1 %copy-done = bf16[1,1,8,128,256]{4,3,2,1,0:T(8,128)(2,1)S(1)} copy-done((bf16[1,1,8,128,256]{4,3,2,1,0:T(8,128)(2,1)S(1)}, bf16[1,1,8,128,256]{4,3,2,1,0:T(8,128)(2,1)}, u32[]{:S(2)}) %copy-start) | copy-done | bytes 524312
  1.7 0.0 copy-start.2
  1.7 1.5 %copy-done.2 = bf16[27,128,256]{2,1,0:T(8,128)(2,1)S(1)} copy-done((bf16[27,128,256]{2,1,0:T(8,128)(2,1)S(1)}, bf16[27,128,256]{2,1,0:T(8,128)(2,1)}, u32[]{:S(2)}) %copy-start.2) | copy-done | bytes 1769496
  3.2 0.0 copy-start.6
  3.2 0.7 copy-done.6
  3.9 0.0 copy-start.1
  3.9 0.0 copy-start.3
  3.9 12.2 %shard_map.103 = (bf16[9,2,128,256]{3,2,1,0:T(8,128)(2,1)S(1)}, bf16[27,2,128,256]{3,2,1,0:T(8,128)(2,1)S(1)}) custom-call(s32[2]{0:T(128)S(1)} %bitcast.24, bf16[8,128,256]{2,1,0:T(8,128)(2,1)S(1)} %bitcast.18, bf16[27,128,256]{2,1,0:T(8,128)(2,1)S(1)} %copy-done.2), custom_call_target="tpu_custom_call" | custom-call | tf_op jit(solution)/shard_map/pallas_call | solution.py:538
  16.1 0.0 copy-done.8
  16.1 0.0 copy-done.5
  16.1 0.0 copy-done.4
  16.1 0.0 copy-done.7
  16.1 0.0 copy-done.1
  16.2 0.0 copy-done.3
  16.2 9.6 %shard_map.104 = (bf16[8,128,256]{2,1,0:T(8,128)(2,1)}, f32[8,128,256]{2,1,0:T(8,128)S(1)}, bf16[9,2,128,256]{3,2,1,0:T(8,128)(2,1)S(1)}, bf16[2,432,16,128]{3,2,1,0:T(8,128)(2,1)S(1)}) custom-call(s32[4,27]{1,0:T(4,128)S(1)} %bitcast.22, s32[4,27]{1,0:T(4,128)S(1)} %bitcast.23, s32[27]{0:T(128)S(1)} %bitcast.27, bf16[8,128,256]{2,1,0:T(8,128)(2,1)S(1)} %bitcast.19, ...), custom_call_target="tpu_custom_call" | custom-call | tf_op jit(solution)/shard_map/pallas_call | solution.py:567
  25.8 45.8 %shard_map.105 = (bf16[9,16,3,16,128]{4,3,2,1,0:T(8,128)(2,1)S(1)}, f32[2,128,256]{2,1,0:T(8,128)S(1)}) custom-call(bf16[2,9,16,3,16,128]{5,4,3,2,1,0:T(8,128)(2,1)S(1)} %bitcast.16, bf16[9,2,128,256]{3,2,1,0:T(8,128)(2,1)S(1)} %get-tuple-element.17.borrowed_ref), custom_call_target="tpu_custom_call" | custom-call | tf_op jit(solution)/shard_map/pallas_call | solution.py:599
  71.6 2.7 %shard_map.106 = (f32[27,128,256]{2,1,0:T(8,128)}, bf16[8,128,256]{2,1,0:T(8,128)(2,1)}) custom-call(s32[2]{0:T(128)S(1)} %bitcast.25, bf16[2,27,8,16,128]{4,3,2,1,0:T(8,128)(2,1)S(1)} %bitcast.20, f32[8,128,256]{2,1,0:T(8,128)S(1)} %get-tuple-element.19.own_ref, f32[2,128,256]{2,1,0:T(8,128)S(1)} %get-tuple-element.20.returned_ref), custom_call_target="tpu_custom_call" | custom-call | tf_op jit(solution)/shard_map/pallas_call | solution.py:632
Async XLA Ops:
  0.6 15.5 %copy-start.8 = (s32[1,1,27]{2,1,0:T(1,128)S(1)}, s32[1,1,27]{2,1,0:T(1,128)}, u32[]{:S(2)}) copy-start(s32[1,1,27]{2,1,0:T(1,128)} %param.14) | copy-start | bytes 328
  0.6 15.5 %copy-start.5 = (s32[1,1,27,4]{2,3,1,0:T(4,128)S(1)}, s32[1,1,27,4]{2,3,1,0:T(4,128)}, u32[]{:S(2)}) copy-start(s32[1,1,27,4]{2,3,1,0:T(4,128)} %param.13) | copy-start | bytes 1300
  0.7 15.5 %copy-start.4 = (s32[1,1,27,4]{2,3,1,0:T(4,128)S(1)}, s32[1,1,27,4]{2,3,1,0:T(4,128)}, u32[]{:S(2)}) copy-start(s32[1,1,27,4]{2,3,1,0:T(4,128)} %param.12) | copy-start | bytes 1300
  0.7 15.5 %copy-start.7 = (f32[256]{0:T(256)S(1)}, f32[256]{0:T(256)}, u32[]{:S(2)}) copy-start(f32[256]{0:T(256)} %param.10) | copy-start | bytes 3076
  0.7 1.1 %copy-start = (bf16[1,1,8,128,256]{4,3,2,1,0:T(8,128)(2,1)S(1)}, bf16[1,1,8,128,256]{4,3,2,1,0:T(8,128)(2,1)}, u32[]{:S(2)}) copy-start(bf16[1,1,8,128,256]{4,3,2,1,0:T(8,128)(2,1)} %param.8) | copy-start | bytes 1572868
  1.7 1.5 %copy-start.2 = (bf16[27,128,256]{2,1,0:T(8,128)(2,1)S(1)}, bf16[27,128,256]{2,1,0:T(8,128)(2,1)}, u32[]{:S(2)}) copy-start(bf16[27,128,256]{2,1,0:T(8,128)(2,1)} %weight_ref.1) | copy-start | bytes 5308420
  3.2 0.7 copy-start.6
  3.9 12.3 %copy-start.1 = (bf16[1,1,8,128,256]{4,3,2,1,0:T(8,128)(2,1)S(1)}, bf16[1,1,8,128,256]{4,3,2,1,0:T(8,128)(2,1)}, u32[]{:S(2)}) copy-start(bf16[1,1,8,128,256]{4,3,2,1,0:T(8,128)(2,1)} %param.8) | copy-start | bytes 1572868
  3.9 12.3 %copy-start.3 = (bf16[1,1,8,128,256]{4,3,2,1,0:T(8,128)(2,1)S(1)}, bf16[1,1,8,128,256]{4,3,2,1,0:T(8,128)(2,1)}, u32[]{:S(2)}) copy-start(bf16[1,1,8,128,256]{4,3,2,1,0:T(8,128)(2,1)} %param.15) | copy-start | bytes 1572868
where the time goes:
time: 74.4 us; the launch traced here: 74.3 us
  Pallas kernels  70.3 us (94%)
  local copies, waits for them, and re-layouts  3.21 us (4%)
    pallas_call x1, Pallas kernels, on_device(): pl.pallas_call(functools.partial(reduce_kernel, nx, ny), out_shape=(shape...  45.8 us
    pallas_call x1, Pallas kernels, on_device(): pl.pallas_call(functools.partial(exchange_kernel, nx, ny), out_shape=(sha...  12.2 us
    pallas_call x1, Pallas kernels, on_device(): pl.pallas_call(compute_kernel, out_shape=(shape((blocks, rows, width), bf...  9.64 us
    unnamed x18, local copies, waits for them, and re-layouts  3.21 us
    pallas_call x1, Pallas kernels, on_device(): pl.pallas_call(finish_kernel, out_shape=(shape((kvol, share, width), f32)...  2.66 us

commit v1 on v0

--- a/solution.py
+++ b/solution.py
@@ -19,6 +19,41 @@
 UNROLL = 9
 VMEM_BYTES = 28 * 1024 * 1024
 EXCHANGE_BYTES = 28 * 1024 * 1024
+
+LINE_KINDS = (
+    'Axrri', 'Ayrri', 'Axrri', 'Axrri', 'Byr', 'Axrri', 'Ayrri', 'Axrri',
+    'Byr', 'Axrri', 'Axrri', 'Axrri', 'Byr', 'Ayrri', 'Ayrri', 'Axrri',
+    'Axrri', 'Ayrri', 'Bxr', 'Byr', 'Axrri', 'Ayrri', 'Ayrri', 'Ayrri',
+    'Ayrri', 'Byr', 'Ayrri',
+)
+LINE_ORDERS = (
+(
+    0, 10, 20, 60, 30, 130, 50, 140, 70, 170, 90, 210, 100, 1, 41, 220,
+    110, 230, 150, 81, 21, 160, 240, 200, 31, 2, 121, 260, 11, 61, 51, 131,
+    71, 181, 141, 91, 22, 171, 101, 211, 111, 221, 151, 32, 191, 231, 161, 241,
+    201, 12, 261, 42, 62, 52, 270, 82, 132, 72, 251, 122, 142, 92, 172, 102,
+    3, 212, 112, 23, 222, 152, 232, 33, 162, 242, 202, 13, 262, 63, 53, 73,
+    192, 93, 252, 4, 103, 24, 113, 34, 133, 143, 14, 43, 153, 64, 83, 163,
+    54, 123, 173, 74, 182, 203, 94, 193, 213, 104, 253, 223, 114, 233, 134, 243,
+    271, 144, 263, 44, 154, 84, 164, 6, 124, 174, 183, 204, 194, 214, 254, 224,
+    234, 244, 264, 45, 16, 26, 85, 7, 66, 36, 125, 136, 184, 56, 195, 146,
+    76, 255, 176, 17, 96, 27, 216, 46, 67, 106, 37, 226, 86, 185, 137, 116,
+    236, 126, 57, 147, 156, 246, 77, 177, 166, 266, 196, 97, 217, 206, 256, 107,
+    227, 186, 117, 237, 157, 247, 167, 267, 207,
+),
+(
+    0, 10, 40, 20, 60, 30, 130, 80, 50, 140, 70, 170, 120, 90, 210, 100,
+    1, 180, 220, 110, 230, 150, 190, 21, 160, 240, 200, 31, 250, 260, 11, 61,
+    51, 131, 71, 141, 2, 91, 171, 22, 101, 211, 111, 221, 151, 32, 231, 161,
+    241, 201, 12, 261, 270, 62, 52, 72, 92, 102, 112, 132, 142, 152, 162, 172,
+    202, 212, 222, 232, 242, 262, 5, 25, 35, 271, 15, 65, 55, 75, 95, 6,
+    105, 115, 26, 135, 16, 145, 36, 155, 165, 175, 205, 215, 66, 7, 225, 235,
+    27, 245, 136, 265, 17, 56, 146, 46, 37, 76, 176, 86, 96, 216, 126, 67,
+    106, 226, 196, 137, 116, 236, 256, 57, 147, 156, 246, 47, 77, 177, 166, 266,
+    87, 97, 217, 206, 127, 107, 227, 186, 117, 237, 197, 157, 247, 257, 167, 267,
+    187, 207,
+),
+)
 
 
 def greet_neighbours(barrier, me_x, me_y, nx, ny):
@@ -230,8 +265,9 @@
 
     lax.fori_loop(0, blocks, activate, 0)
 
+    line = len(wpart_ref.shape) == 5
     filled = 2 * kvol * share_tiles
-    if filled < tiles:
+    if not line and filled < tiles:
         for y in range(ny):
             wpart_ref[y, filled:] = jnp.zeros((tiles - filled, TILE, LANES), wpart_ref.dtype)
 
@@ -240,12 +276,16 @@
         pulled = jnp.concatenate([dpre[t] for t in targets], axis=0)
         taken = jnp.concatenate([turned[s] for s in reads], axis=1)
         part = jnp.dot(taken, pulled, preferred_element_type=jnp.float32).astype(wpart_ref.dtype)
-        for y in range(ny):
-            for h in range(width // LANES):
-                piece = part[y * share : (y + 1) * share, h * LANES : (h + 1) * LANES]
-                wpart_ref[y, pl.ds((h * kvol + k) * share_tiles, share_tiles)] = piece.reshape(
-                    share_tiles, TILE, LANES
-                )
+        if line:
+            for y in range(ny):
+                wpart_ref[y, k] = part[y * share : (y + 1) * share].reshape(wpart_ref.shape[2:])
+        else:
+            for y in range(ny):
+                for h in range(width // LANES):
+                    piece = part[y * share : (y + 1) * share, h * LANES : (h + 1) * LANES]
+                    wpart_ref[y, pl.ds((h * kvol + k) * share_tiles, share_tiles)] = piece.reshape(
+                        share_tiles, TILE, LANES
+                    )
         back = lax.dot_general(
             pulled, weight_ref[k], (((1,), (1,)), ((), ())), preferred_element_type=jnp.float32
         )
@@ -480,6 +520,326 @@
             back_copy(a).wait_send()
 
 
+def line_kernel(
+    nx,
+    ny,
+    wpart_ref,
+    borrowed_ref,
+    sum_ref,
+    returned_ref,
+    work,
+    yland,
+    full_land,
+    half_land,
+    land,
+    side_land,
+    column,
+    x_land,
+    ysend,
+    yrecv,
+    csend,
+    crecv,
+    hsend,
+    hrecv,
+    bsend,
+    brecv,
+):
+    me_x, me_y = lax.axis_index("gx"), lax.axis_index("gy")
+    kvol = work.shape[0]
+    f32 = jnp.float32
+    bit_x, bit_y, z = lax.rem(me_x, 2), lax.rem(me_x // 2, 2), me_x // 4
+    low, high = lax.rem(z, 2), z // 2
+    beside = {"x": me_x + 1 - 2 * bit_x, "y": me_x + 2 - 4 * bit_y}
+    across = beside["y"] + 1 - 2 * bit_x
+    inner = exists(z - 1, 2)
+    near = jnp.where(inner, me_x - 4 + 8 * high, me_x + 4 - 8 * high)
+    middle = me_x + 4 - 8 * high
+    peers = (3 - z, z + 2 - 4 * high, z + 1 - 2 * low)
+
+    barrier = pltpu.get_barrier_semaphore()
+    expected = greet_neighbours(barrier, me_x, me_y, nx, ny) + greet_column(
+        barrier, me_x, me_y, ny
+    )
+    greeted = [beside["x"], beside["y"], across] + [me_x + 4 * (peer - z) for peer in peers]
+    for device in greeted:
+        pl.semaphore_signal(barrier, inc=1, device_id=(device, me_y), device_id_type=MESH)
+    pl.semaphore_wait(barrier, expected + len(greeted))
+
+    def side_copy(a, b):
+        return pltpu.make_async_remote_copy(
+            src_ref=borrowed_ref.at[3 * a + b],
+            dst_ref=side_land.at[a, b // 2],
+            send_sem=hsend.at[a, b // 2],
+            recv_sem=hrecv.at[a, b // 2],
+            device_id=(me_x, me_y + b - 1),
+            device_id_type=MESH,
+        )
+
+    def back_copy(a):
+        return pltpu.make_async_remote_copy(
+            src_ref=column.at[a // 2],
+            dst_ref=x_land.at[a // 2],
+            send_sem=bsend.at[a // 2],
+            recv_sem=brecv.at[a // 2],
+            device_id=(me_x + a - 1, me_y),
+            device_id_type=MESH,
+        )
+
+    def sides(act, sign):
+        for a in range(3):
+            for b in (0, 2):
+
+                @pl.when(exists(me_x + a - 1, nx) & exists(me_y + sign * (b - 1), ny))
+                def _():
+                    act(a, b)
+
+    def column_copy(step, g):
+        other = lax.rem(me_y + step, ny)
+        return pltpu.make_async_remote_copy(
+            src_ref=wpart_ref.at[other, g],
+            dst_ref=yland.at[step - 1, g],
+            send_sem=ysend.at[step - 1, g],
+            recv_sem=yrecv.at[step - 1, g],
+            device_id=(me_x, other),
+            device_id_type=MESH,
+        )
+
+    for g in range(kvol):
+        for step in range(1, ny):
+            column_copy(step, g).start()
+    sides(lambda a, b: side_copy(a, b).start(), 1)
+
+    def give_back():
+        returned_ref[...] = jnp.zeros(returned_ref.shape, f32)
+        for b in (0, 2):
+
+            @pl.when(exists(me_y + 1 - b, ny))
+            def _():
+                side_copy(1, b).wait_recv()
+                returned_ref[...] += side_land[1, b // 2].astype(f32)
+
+        for a in (0, 2):
+
+            @pl.when(exists(me_x + a - 1, nx))
+            def _():
+                for b in (0, 2):
+                    missing = jnp.logical_not(exists(me_y + 1 - b, ny))
+
+                    @pl.when(missing)
+                    def _():
+                        side_land[a, b // 2] = jnp.zeros(side_land.shape[2:], side_land.dtype)
+
+                    @pl.when(jnp.logical_not(missing))
+                    def _():
+                        side_copy(a, b).wait_recv()
+
+                column[a // 2] = (
+                    borrowed_ref[3 * a + 1].astype(f32)
+                    + side_land[a, 0].astype(f32)
+                    + side_land[a, 1].astype(f32)
+                ).astype(column.dtype)
+                back_copy(a).start()
+
+    def take_back():
+        for a in (0, 2):
+
+            @pl.when(exists(me_x + 1 - a, nx))
+            def _():
+                back_copy(a).wait_recv()
+                returned_ref[...] += x_land[a // 2].astype(f32)
+
+    def own_sum(g):
+        value = wpart_ref[me_y, g].astype(f32)
+        for step in range(1, ny):
+            column_copy(step, g).wait_recv()
+            value = value + yland[step - 1, g].astype(f32)
+        return value
+
+    def program(order, inside):
+        sent = []
+
+        def copy(g, src, dst, leave, arrive, device):
+            return pltpu.make_async_remote_copy(
+                src_ref=src,
+                dst_ref=dst,
+                send_sem=csend.at[leave, g],
+                recv_sem=crecv.at[arrive, g],
+                device_id=(device, me_y),
+                device_id_type=MESH,
+            )
+
+        def send(g, src, dst, leave, arrive, device):
+            made = copy(g, src, dst, leave, arrive, device)
+            made.start()
+            sent.append(made)
+
+        def recv(g, dst, arrive):
+            copy(g, dst, dst, 0, arrive, beside["x"]).wait_recv()
+
+        def along(g, k):
+            first, spread, gather, cross = LINE_KINDS[g][1:]
+            second = "y" if first == "x" else "x"
+            bits = {"x": bit_x, "y": bit_y}
+            hb, qb = bits[first], bits[second]
+            mine = 2 * hb + qb
+            beside_mine, over, corner = 2 * hb + 1 - qb, 2 - 2 * hb + qb, 3 - mine
+            kept, gone = pl.ds(2 * hb, 2), pl.ds(2 - 2 * hb, 2)
+            total, ours = sum_ref.at[g], work.at[g]
+
+            def spread_quarters():
+                send(g, total.at[mine], total.at[mine], 9, 9, across)
+                send(g, total.at[mine], total.at[mine], 8, 8, beside[first])
+                send(g, total.at[mine], total.at[mine], 7, 7, beside[second])
+
+            def gather_start():
+                if gather == "d":
+                    spread_quarters()
+                else:
+                    send(g, total.at[mine], total.at[mine], 7, 7, beside[second])
+
+            if k == 0:
+                work[g] = own_sum(g).astype(work.dtype)
+                if spread == "d":
+                    send(g, ours.at[corner], land.at[2, g], 2, 2, across)
+                    send(g, ours.at[over], land.at[1, g], 1, 1, beside[first])
+                    send(g, ours.at[beside_mine], land.at[0, g], 0, 0, beside[second])
+                else:
+                    send(g, ours.at[gone], half_land.at[g], 1, 1, beside[first])
+            elif k == 1:
+                if spread == "r":
+                    recv(g, half_land.at[g], 1)
+                    work[g, kept] = (
+                        work[g, kept].astype(f32) + half_land[g].astype(f32)
+                    ).astype(work.dtype)
+                    send(g, ours.at[beside_mine], land.at[0, g], 0, 0, beside[second])
+            elif k == 2:
+                value = work[g, mine].astype(f32)
+                for slot in range(3 if spread == "d" else 1):
+                    recv(g, land.at[slot, g], slot)
+                    value = value + land[slot, g].astype(f32)
+                work[g, mine] = value.astype(work.dtype)
+                if cross == "x":
+                    land[3 + z, g] = value.astype(work.dtype)
+                    for at, peer in enumerate(peers):
+                        send(g, ours.at[mine], land.at[3 + z, g], 3 + at, 3 + z, me_x + 4 * (peer - z))
+                elif not inside:
+                    send(g, ours.at[mine], land.at[3, g], 3, 3, near)
+            elif k == 3:
+                if cross == "i" and inside:
+                    recv(g, land.at[3, g], 3)
+                    work[g, mine] = (
+                        work[g, mine].astype(f32) + land[3, g].astype(f32)
+                    ).astype(work.dtype)
+                    send(g, ours.at[mine], land.at[4, g], 4, 4, middle)
+            elif k == 4:
+                if cross == "i" and inside:
+                    recv(g, land.at[4, g], 4)
+                    sum_ref[g, mine] = (
+                        work[g, mine].astype(f32) + land[4, g].astype(f32)
+                    ).astype(sum_ref.dtype)
+                    send(g, total.at[mine], total.at[mine], 5, 5, near)
+                    gather_start()
+            elif k == 5:
+                if cross == "x":
+                    for peer in peers:
+                        recv(g, land.at[3 + peer, g], 3 + peer)
+                    sum_ref[g, mine] = (
+                        (land[3, g].astype(f32) + land[4, g].astype(f32))
+                        + (land[5, g].astype(f32) + land[6, g].astype(f32))
+                    ).astype(sum_ref.dtype)
+                    gather_start()
+                elif not inside:
+                    recv(g, total.at[mine], 5)
+                    gather_start()
+            elif k == 6:
+                if gather == "r":
+                    recv(g, total.at[beside_mine], 7)
+                    send(g, total.at[kept], total.at[kept], 8, 8, beside[first])
+            elif k == 7:
+                if gather == "r":
+                    recv(g, total.at[gone], 8)
+                else:
+                    recv(g, total.at[beside_mine], 7)
+                    recv(g, total.at[over], 8)
+                    recv(g, total.at[corner], 9)
+
+        def fold(g, k):
+            first = LINE_KINDS[g][1]
+            second = "y" if first == "x" else "x"
+            bits = {"x": bit_x, "y": bit_y}
+            hb, qb = high, bits[first]
+            mine, other = 2 * hb + qb, 2 * hb + 1 - qb
+            kept, gone = pl.ds(2 * hb, 2), pl.ds(2 - 2 * hb, 2)
+            total, ours = sum_ref.at[g], work.at[g]
+            if not inside:
+                if k == 0:
+                    work[g] = own_sum(g).astype(work.dtype)
+                    send(g, ours, full_land.at[g], 3, 3, near)
+                elif k == 6:
+                    recv(g, total.at[kept], 6)
+                elif k == 7:
+                    recv(g, total.at[gone], 8)
+            elif k == 1:
+                value = own_sum(g)
+                recv(g, full_land.at[g], 3)
+                work[g] = (value + full_land[g].astype(f32)).astype(work.dtype)
+                send(g, ours.at[gone], half_land.at[g], 4, 4, middle)
+            elif k == 2:
+                recv(g, half_land.at[g], 4)
+                work[g, kept] = (
+                    work[g, kept].astype(f32) + half_land[g].astype(f32)
+                ).astype(work.dtype)
+                send(g, ours.at[other], land.at[0, g], 0, 0, beside[first])
+            elif k == 3:
+                recv(g, land.at[0, g], 0)
+                work[g, mine] = (
+                    work[g, mine].astype(f32) + land[0, g].astype(f32)
+                ).astype(work.dtype)
+                send(g, ours.at[mine], land.at[1, g], 1, 1, beside[second])
+            elif k == 4:
+                recv(g, land.at[1, g], 1)
+                sum_ref[g, mine] = (
+                    work[g, mine].astype(f32) + land[1, g].astype(f32)
+                ).astype(sum_ref.dtype)
+                send(g, total.at[mine], total.at[mine], 7, 7, beside[first])
+            elif k == 5:
+                recv(g, total.at[other], 7)
+                send(g, total.at[kept], total.at[kept], 5, 5, middle)
+                send(g, total.at[kept], total.at[kept], 6, 6, near)
+            elif k == 6:
+                recv(g, total.at[gone], 5)
+                send(g, total.at[gone], total.at[gone], 8, 8, near)
+
+        for event in order:
+            g, k = divmod(event, 10)
+            if g == kvol:
+                (give_back, take_back)[k]()
+            elif LINE_KINDS[g][0] == "B":
+                fold(g, k)
+            else:
+                along(g, k)
+        for made in sent:
+            made.wait_send()
+
+    @pl.when(inner)
+    def _():
+        program(LINE_ORDERS[0], True)
+
+    @pl.when(jnp.logical_not(inner))
+    def _():
+        program(LINE_ORDERS[1], False)
+
+    for g in range(kvol):
+        for step in range(1, ny):
+            column_copy(step, g).wait_send()
+    sides(lambda a, b: side_copy(a, b).wait_send(), 1)
+    for a in (0, 2):
+
+        @pl.when(exists(me_x + a - 1, nx))
+        def _():
+            back_copy(a).wait_send()
+
+
 def finish_kernel(
     send_ref, total_ref, own_ref, returned_ref, weight_ref, feat_ref, wide, feats, wsem, fsem
 ):
@@ -490,10 +850,13 @@
     copies = []
     for c in range(chunks):
         at = pl.ds(c * per, per)
-        for h in range(width // LANES):
-            wide[at, :, h * LANES : (h + 1) * LANES] = total_ref[h, at].reshape(
-                per, share, LANES
-            ).astype(jnp.float32) * (1.0 / rows)
+        if len(total_ref.shape) == 3:
+            wide[at] = total_ref[at].astype(jnp.float32) * (1.0 / rows)
+        else:
+            for h in range(width // LANES):
+                wide[at, :, h * LANES : (h + 1) * LANES] = total_ref[h, at].reshape(
+                    per, share, LANES
+                ).astype(jnp.float32) * (1.0 / rows)
         copy = pltpu.make_async_copy(wide.at[at], weight_ref.at[at], wsem.at[c])
         copy.start()
         copies.append(copy)
@@ -564,13 +927,15 @@
     unit = groups * nx
     tiles = -(-used // unit) * unit
     depth = tiles // unit
+    line = nx == 16 and kvol == len(LINE_KINDS)
+    quarters = (4, share // 4, width)
     outputs, own, borrowed, wpart = pl.pallas_call(
         compute_kernel,
         out_shape=(
             shape((blocks, rows, width), bf16),
             shape((blocks, rows, width), f32),
             shape((squares, shared_count, rows, width), bf16),
-            shape((ny, tiles, TILE, LANES), bf16),
+            shape((ny, kvol) + quarters if line else (ny, tiles, TILE, LANES), bf16),
         ),
         in_specs=[smem, smem, smem, vmem, vmem, vmem, vmem, vmem],
         out_specs=(vmem, vmem, vmem, vmem),
@@ -596,38 +961,70 @@
     steps = nx.bit_length() - 1
     block = (depth, TILE, LANES)
     boundary = (shared_count, rows, width)
-    total, returned = pl.pallas_call(
-        functools.partial(reduce_kernel, nx, ny),
-        out_shape=(
-            shape((groups, nx) + block, bf16),
-            shape(boundary, f32),
-        ),
-        in_specs=[vmem, vmem],
-        out_specs=(vmem, vmem),
-        scratch_shapes=[
-            VMEM((groups, nx) + block, bf16),
-            VMEM((max(ny - 1, 1), groups, nx) + block, bf16),
-            VMEM((groups, nx) + block, bf16),
-            VMEM((3, 2) + boundary, bf16),
-            VMEM((2,) + boundary, bf16),
-            VMEM((2,) + boundary, bf16),
-            dma((max(ny - 1, 1), groups)),
-            dma((max(ny - 1, 1), groups)),
-            dma((steps, groups)),
-            dma((steps, groups)),
-            dma((steps, groups)),
-            dma((steps, groups)),
-            dma((3, 2)),
-            dma((3, 2)),
-            dma((2,)),
-            dma((2,)),
-        ],
-        compiler_params=pltpu.CompilerParams(
-            collective_id=1, has_side_effects=True, vmem_limit_bytes=VMEM_BYTES
-        ),
-    )(wpart.reshape((ny, groups, nx) + block), borrowed)
-
-    halves, share_tiles = width // LANES, share // TILE
+    if line:
+        total, returned = pl.pallas_call(
+            functools.partial(line_kernel, nx, ny),
+            out_shape=(shape((kvol,) + quarters, bf16), shape(boundary, f32)),
+            in_specs=[vmem, vmem],
+            out_specs=(vmem, vmem),
+            scratch_shapes=[
+                VMEM((kvol,) + quarters, bf16),
+                VMEM((max(ny - 1, 1), kvol) + quarters, bf16),
+                VMEM((kvol,) + quarters, bf16),
+                VMEM((kvol, 2) + quarters[1:], bf16),
+                VMEM((7, kvol) + quarters[1:], bf16),
+                VMEM((3, 2) + boundary, bf16),
+                VMEM((2,) + boundary, bf16),
+                VMEM((2,) + boundary, bf16),
+                dma((max(ny - 1, 1), kvol)),
+                dma((max(ny - 1, 1), kvol)),
+                dma((10, kvol)),
+                dma((10, kvol)),
+                dma((3, 2)),
+                dma((3, 2)),
+                dma((2,)),
+                dma((2,)),
+            ],
+            compiler_params=pltpu.CompilerParams(
+                collective_id=1, has_side_effects=True, vmem_limit_bytes=VMEM_BYTES
+            ),
+        )(wpart, borrowed)
+        total = total.reshape(kvol, share, width)
+    else:
+        total, returned = pl.pallas_call(
+            functools.partial(reduce_kernel, nx, ny),
+            out_shape=(
+                shape((groups, nx) + block, bf16),
+                shape(boundary, f32),
+            ),
+            in_specs=[vmem, vmem],
+            out_specs=(vmem, vmem),
+            scratch_shapes=[
+                VMEM((groups, nx) + block, bf16),
+                VMEM((max(ny - 1, 1), groups, nx) + block, bf16),
+                VMEM((groups, nx) + block, bf16),
+                VMEM((3, 2) + boundary, bf16),
+                VMEM((2,) + boundary, bf16),
+                VMEM((2,) + boundary, bf16),
+                dma((max(ny - 1, 1), groups)),
+                dma((max(ny - 1, 1), groups)),
+                dma((steps, groups)),
+                dma((steps, groups)),
+                dma((steps, groups)),
+                dma((steps, groups)),
+                dma((3, 2)),
+                dma((3, 2)),
+                dma((2,)),
+                dma((2,)),
+            ],
+            compiler_params=pltpu.CompilerParams(
+                collective_id=1, has_side_effects=True, vmem_limit_bytes=VMEM_BYTES
+            ),
+        )(wpart.reshape((ny, groups, nx) + block), borrowed)
+        total = total.reshape(tiles, TILE, LANES)[:used].reshape(
+            width // LANES, kvol, share // TILE, TILE, LANES
+        )
+
     chunks = max(c for c in range(1, 10) if kvol % c == 0)
     weight_grad, feat_grad = pl.pallas_call(
         finish_kernel,
@@ -643,7 +1040,7 @@
         compiler_params=pltpu.CompilerParams(vmem_limit_bytes=VMEM_BYTES),
     )(
         shared,
-        total.reshape(tiles, TILE, LANES)[:used].reshape(halves, kvol, share_tiles, TILE, LANES),
+        total,
         own,
         returned,
     )

time: 74.4 us -> 74.9 us (level)
  no operation moved by 1% of the time
where the time goes in v1:
time: 74.9 us; the launch traced here: 74.7 us
  Pallas kernels  70.8 us (95%)
  local copies, waits for them, and re-layouts  3.21 us (4%)
    pallas_call x1, Pallas kernels, on_device(): pl.pallas_call(functools.partial(line_kernel, nx, ny), out_shape=(shape((...  46.3 us
    pallas_call x1, Pallas kernels, on_device(): pl.pallas_call(functools.partial(exchange_kernel, nx, ny), out_shape=(sha...  12.2 us
    pallas_call x1, Pallas kernels, on_device(): pl.pallas_call(compute_kernel, out_shape=(shape((blocks, rows, width), bf...  9.64 us
    unnamed x18, local copies, waits for them, and re-layouts  3.21 us
    pallas_call x1, Pallas kernels, on_device(): pl.pallas_call(finish_kernel, out_shape=(shape((kvol, share, width), f32)...  2.66 us

profile of v1, /device:TPU:0, one launch (start us, length us, event | category | flops | bytes accessed | tf_op | source)
XLA Modules:
  0.0 74.7 jit_solution(16535145484709796958)
XLA Ops:
  0.6 0.0 copy-start.8
  0.6 0.0 copy-start.5
  0.7 0.0 copy-start.4
  0.7 0.0 copy-start.7
  0.7 0.0 copy-start
  0.7 1.1 %copy-done = bf16[1,1,8,128,256]{4,3,2,1,0:T(8,128)(2,1)S(1)} copy-done((bf16[1,1,8,128,256]{4,3,2,1,0:T(8,128)(2,1)S(1)}, bf16[1,1,8,128,256]{4,3,2,1,0:T(8,128)(2,1)}, u32[]{:S(2)}) %copy-start) | copy-done | bytes 524312
  1.7 0.0 copy-start.2
  1.7 1.5 %copy-done.2 = bf16[27,128,256]{2,1,0:T(8,128)(2,1)S(1)} copy-done((bf16[27,128,256]{2,1,0:T(8,128)(2,1)S(1)}, bf16[27,128,256]{2,1,0:T(8,128)(2,1)}, u32[]{:S(2)}) %copy-start.2) | copy-done | bytes 1769496
  3.2 0.0 copy-start.6
  3.2 0.7 copy-done.6
  3.9 0.0 copy-start.1
  3.9 0.0 copy-start.3
  3.9 12.2 %shard_map.103 = (bf16[9,2,128,256]{3,2,1,0:T(8,128)(2,1)S(1)}, bf16[27,2,128,256]{3,2,1,0:T(8,128)(2,1)S(1)}) custom-call(s32[2]{0:T(128)S(1)} %bitcast.22, bf16[8,128,256]{2,1,0:T(8,128)(2,1)S(1)} %bitcast.16, bf16[27,128,256]{2,1,0:T(8,128)(2,1)S(1)} %copy-done.2), custom_call_target="tpu_custom_call" | custom-call | tf_op jit(solution)/shard_map/pallas_call | solution.py:901
  16.1 0.0 copy-done.8
  16.1 0.0 copy-done.5
  16.1 0.0 copy-done.4
  16.1 0.0 copy-done.7
  16.1 0.0 copy-done.1
  16.2 0.0 copy-done.3
  16.2 9.6 %shard_map.104 = (bf16[8,128,256]{2,1,0:T(8,128)(2,1)}, f32[8,128,256]{2,1,0:T(8,128)S(1)}, bf16[9,2,128,256]{3,2,1,0:T(8,128)(2,1)S(1)}, bf16[2,27,4,32,256]{4,3,2,1,0:T(8,128)(2,1)S(1)}) custom-call(s32[4,27]{1,0:T(4,128)S(1)} %bitcast.20, s32[4,27]{1,0:T(4,128)S(1)} %bitcast.21, s32[27]{0:T(128)S(1)} %bitcast.25, bf16[8,128,256]{2,1,0:T(8,128)(2,1)S(1)} %bitcast.17, ...), custom_call_target="tpu_custom_call" | custom-call | tf_op jit(solution)/shard_map/pallas_call | solution.py:932
  25.8 46.3 %shard_map.105 = (bf16[27,4,32,256]{3,2,1,0:T(8,128)(2,1)S(1)}, f32[2,128,256]{2,1,0:T(8,128)S(1)}) custom-call(bf16[2,27,4,32,256]{4,3,2,1,0:T(8,128)(2,1)S(1)} %get-tuple-element.16.wpart_ref, bf16[9,2,128,256]{3,2,1,0:T(8,128)(2,1)S(1)} %get-tuple-element.17.borrowed_ref), custom_call_target="tpu_custom_call" | custom-call | tf_op jit(solution)/shard_map/pallas_call | solution.py:965
  72.1 2.7 %shard_map.106 = (f32[27,128,256]{2,1,0:T(8,128)}, bf16[8,128,256]{2,1,0:T(8,128)(2,1)}) custom-call(s32[2]{0:T(128)S(1)} %bitcast.23, bf16[27,128,256]{2,1,0:T(8,128)(2,1)S(1)} %bitcast.18, f32[8,128,256]{2,1,0:T(8,128)S(1)} %get-tuple-element.19.own_ref, f32[2,128,256]{2,1,0:T(8,128)S(1)} %get-tuple-element.20.returned_ref), custom_call_target="tpu_custom_call" | custom-call | tf_op jit(solution)/shard_map/pallas_call | solution.py:1029
Async XLA Ops:
  0.6 15.5 %copy-start.8 = (s32[1,1,27]{2,1,0:T(1,128)S(1)}, s32[1,1,27]{2,1,0:T(1,128)}, u32[]{:S(2)}) copy-start(s32[1,1,27]{2,1,0:T(1,128)} %param.14) | copy-start | bytes 328
  0.6 15.5 %copy-start.5 = (s32[1,1,27,4]{2,3,1,0:T(4,128)S(1)}, s32[1,1,27,4]{2,3,1,0:T(4,128)}, u32[]{:S(2)}) copy-start(s32[1,1,27,4]{2,3,1,0:T(4,128)} %param.13) | copy-start | bytes 1300
  0.7 15.5 %copy-start.4 = (s32[1,1,27,4]{2,3,1,0:T(4,128)S(1)}, s32[1,1,27,4]{2,3,1,0:T(4,128)}, u32[]{:S(2)}) copy-start(s32[1,1,27,4]{2,3,1,0:T(4,128)} %param.12) | copy-start | bytes 1300
  0.7 15.5 %copy-start.7 = (f32[256]{0:T(256)S(1)}, f32[256]{0:T(256)}, u32[]{:S(2)}) copy-start(f32[256]{0:T(256)} %param.10) | copy-start | bytes 3076
  0.7 1.1 %copy-start = (bf16[1,1,8,128,256]{4,3,2,1,0:T(8,128)(2,1)S(1)}, bf16[1,1,8,128,256]{4,3,2,1,0:T(8,128)(2,1)}, u32[]{:S(2)}) copy-start(bf16[1,1,8,128,256]{4,3,2,1,0:T(8,128)(2,1)} %param.8) | copy-start | bytes 1572868
  1.7 1.5 %copy-start.2 = (bf16[27,128,256]{2,1,0:T(8,128)(2,1)S(1)}, bf16[27,128,256]{2,1,0:T(8,128)(2,1)}, u32[]{:S(2)}) copy-start(bf16[27,128,256]{2,1,0:T(8,128)(2,1)} %weight_ref.1) | copy-start | bytes 5308420
  3.2 0.7 copy-start.6
  3.9 12.3 %copy-start.1 = (bf16[1,1,8,128,256]{4,3,2,1,0:T(8,128)(2,1)S(1)}, bf16[1,1,8,128,256]{4,3,2,1,0:T(8,128)(2,1)}, u32[]{:S(2)}) copy-start(bf16[1,1,8,128,256]{4,3,2,1,0:T(8,128)(2,1)} %param.8) | copy-start | bytes 1572868
  3.9 12.3 %copy-start.3 = (bf16[1,1,8,128,256]{4,3,2,1,0:T(8,128)(2,1)S(1)}, bf16[1,1,8,128,256]{4,3,2,1,0:T(8,128)(2,1)}, u32[]{:S(2)}) copy-start(bf16[1,1,8,128,256]{4,3,2,1,0:T(8,128)(2,1)} %param.15) | copy-start | bytes 1572868

commit v2 on v1

--- a/solution.py
+++ b/solution.py
@@ -1,4 +1,5 @@
 import functools
+import math
 
 import jax
 import jax.numpy as jnp
@@ -532,6 +533,7 @@
     full_land,
     half_land,
     land,
+    spare,
     side_land,
     column,
     x_land,
@@ -548,22 +550,24 @@
     kvol = work.shape[0]
     f32 = jnp.float32
     bit_x, bit_y, z = lax.rem(me_x, 2), lax.rem(me_x // 2, 2), me_x // 4
-    low, high = lax.rem(z, 2), z // 2
+    high = z // 2
     beside = {"x": me_x + 1 - 2 * bit_x, "y": me_x + 2 - 4 * bit_y}
-    across = beside["y"] + 1 - 2 * bit_x
     inner = exists(z - 1, 2)
     near = jnp.where(inner, me_x - 4 + 8 * high, me_x + 4 - 8 * high)
     middle = me_x + 4 - 8 * high
-    peers = (3 - z, z + 2 - 4 * high, z + 1 - 2 * low)
 
     barrier = pltpu.get_barrier_semaphore()
     expected = greet_neighbours(barrier, me_x, me_y, nx, ny) + greet_column(
         barrier, me_x, me_y, ny
     )
-    greeted = [beside["x"], beside["y"], across] + [me_x + 4 * (peer - z) for peer in peers]
-    for device in greeted:
+    for device in (beside["x"], beside["y"], near):
         pl.semaphore_signal(barrier, inc=1, device_id=(device, me_y), device_id_type=MESH)
-    pl.semaphore_wait(barrier, expected + len(greeted))
+
+    @pl.when(inner)
+    def _():
+        pl.semaphore_signal(barrier, inc=1, device_id=(middle, me_y), device_id_type=MESH)
+
+    pl.semaphore_wait(barrier, expected + 3 + inner.astype(jnp.int32))
 
     def side_copy(a, b):
         return pltpu.make_async_remote_copy(
@@ -598,7 +602,7 @@
         return pltpu.make_async_remote_copy(
             src_ref=wpart_ref.at[other, g],
             dst_ref=yland.at[step - 1, g],
-            send_sem=ysend.at[step - 1, g],
+            send_sem=ysend.at[step - 1],
             recv_sem=yrecv.at[step - 1, g],
             device_id=(me_x, other),
             device_id_type=MESH,
@@ -656,112 +660,70 @@
         return value
 
     def program(order, inside):
-        sent = []
+        sent = {}
 
         def copy(g, src, dst, leave, arrive, device):
             return pltpu.make_async_remote_copy(
                 src_ref=src,
                 dst_ref=dst,
-                send_sem=csend.at[leave, g],
+                send_sem=csend.at[leave],
                 recv_sem=crecv.at[arrive, g],
                 device_id=(device, me_y),
                 device_id_type=MESH,
             )
 
         def send(g, src, dst, leave, arrive, device):
-            made = copy(g, src, dst, leave, arrive, device)
-            made.start()
-            sent.append(made)
+            copy(g, src, dst, leave, arrive, device).start()
+            sent[leave] = sent.get(leave, 0) + math.prod(src.shape[:-2])
 
         def recv(g, dst, arrive):
             copy(g, dst, dst, 0, arrive, beside["x"]).wait_recv()
 
         def along(g, k):
-            first, spread, gather, cross = LINE_KINDS[g][1:]
+            first = LINE_KINDS[g][1]
             second = "y" if first == "x" else "x"
             bits = {"x": bit_x, "y": bit_y}
             hb, qb = bits[first], bits[second]
-            mine = 2 * hb + qb
-            beside_mine, over, corner = 2 * hb + 1 - qb, 2 - 2 * hb + qb, 3 - mine
+            mine, other = 2 * hb + qb, 2 * hb + 1 - qb
             kept, gone = pl.ds(2 * hb, 2), pl.ds(2 - 2 * hb, 2)
             total, ours = sum_ref.at[g], work.at[g]
-
-            def spread_quarters():
-                send(g, total.at[mine], total.at[mine], 9, 9, across)
-                send(g, total.at[mine], total.at[mine], 8, 8, beside[first])
-                send(g, total.at[mine], total.at[mine], 7, 7, beside[second])
-
-            def gather_start():
-                if gather == "d":
-                    spread_quarters()
-                else:
-                    send(g, total.at[mine], total.at[mine], 7, 7, beside[second])
-
             if k == 0:
                 work[g] = own_sum(g).astype(work.dtype)
-                if spread == "d":
-                    send(g, ours.at[corner], land.at[2, g], 2, 2, across)
-                    send(g, ours.at[over], land.at[1, g], 1, 1, beside[first])
-                    send(g, ours.at[beside_mine], land.at[0, g], 0, 0, beside[second])
-                else:
-                    send(g, ours.at[gone], half_land.at[g], 1, 1, beside[first])
+                send(g, ours.at[gone], half_land.at[g], 0, 0, beside[first])
             elif k == 1:
-                if spread == "r":
-                    recv(g, half_land.at[g], 1)
-                    work[g, kept] = (
-                        work[g, kept].astype(f32) + half_land[g].astype(f32)
-                    ).astype(work.dtype)
-                    send(g, ours.at[beside_mine], land.at[0, g], 0, 0, beside[second])
+                recv(g, half_land.at[g], 0)
+                work[g, kept] = (
+                    work[g, kept].astype(f32) + half_land[g].astype(f32)
+                ).astype(work.dtype)
+                send(g, ours.at[other], land.at[0, g], 1, 1, beside[second])
             elif k == 2:
-                value = work[g, mine].astype(f32)
-                for slot in range(3 if spread == "d" else 1):
-                    recv(g, land.at[slot, g], slot)
-                    value = value + land[slot, g].astype(f32)
-                work[g, mine] = value.astype(work.dtype)
-                if cross == "x":
-                    land[3 + z, g] = value.astype(work.dtype)
-                    for at, peer in enumerate(peers):
-                        send(g, ours.at[mine], land.at[3 + z, g], 3 + at, 3 + z, me_x + 4 * (peer - z))
-                elif not inside:
-                    send(g, ours.at[mine], land.at[3, g], 3, 3, near)
+                recv(g, land.at[0, g], 1)
+                work[g, mine] = (
+                    work[g, mine].astype(f32) + land[0, g].astype(f32)
+                ).astype(work.dtype)
+                if not inside:
+                    send(g, ours.at[mine], land.at[1, g], 2, 2, near)
             elif k == 3:
-                if cross == "i" and inside:
-                    recv(g, land.at[3, g], 3)
-                    work[g, mine] = (
-                        work[g, mine].astype(f32) + land[3, g].astype(f32)
-                    ).astype(work.dtype)
-                    send(g, ours.at[mine], land.at[4, g], 4, 4, middle)
+                recv(g, land.at[1, g], 2)
+                work[g, mine] = (
+                    work[g, mine].astype(f32) + land[1, g].astype(f32)
+                ).astype(work.dtype)
+                send(g, ours.at[mine], land.at[2, g], 3, 3, middle)
             elif k == 4:
-                if cross == "i" and inside:
-                    recv(g, land.at[4, g], 4)
-                    sum_ref[g, mine] = (
-                        work[g, mine].astype(f32) + land[4, g].astype(f32)
-                    ).astype(sum_ref.dtype)
-                    send(g, total.at[mine], total.at[mine], 5, 5, near)
-                    gather_start()
+                recv(g, land.at[2, g], 3)
+                sum_ref[g, mine] = (
+                    work[g, mine].astype(f32) + land[2, g].astype(f32)
+                ).astype(sum_ref.dtype)
+                send(g, total.at[mine], total.at[mine], 2, 2, near)
+                send(g, total.at[mine], total.at[mine], 4, 0, beside[second])
             elif k == 5:
-                if cross == "x":
-                    for peer in peers:
-                        recv(g, land.at[3 + peer, g], 3 + peer)
-                    sum_ref[g, mine] = (
-                        (land[3, g].astype(f32) + land[4, g].astype(f32))
-                        + (land[5, g].astype(f32) + land[6, g].astype(f32))
-                    ).astype(sum_ref.dtype)
-                    gather_start()
-                elif not inside:
-                    recv(g, total.at[mine], 5)
-                    gather_start()
+                recv(g, total.at[mine], 2)
+                send(g, total.at[mine], total.at[mine], 4, 0, beside[second])
             elif k == 6:
-                if gather == "r":
-                    recv(g, total.at[beside_mine], 7)
-                    send(g, total.at[kept], total.at[kept], 8, 8, beside[first])
+                recv(g, total.at[other], 0)
+                send(g, total.at[kept], total.at[kept], 5, 4, beside[first])
             elif k == 7:
-                if gather == "r":
-                    recv(g, total.at[gone], 8)
-                else:
-                    recv(g, total.at[beside_mine], 7)
-                    recv(g, total.at[over], 8)
-                    recv(g, total.at[corner], 9)
+                recv(g, total.at[gone], 4)
 
         def fold(g, k):
             first = LINE_KINDS[g][1]
@@ -774,22 +736,22 @@
             if not inside:
                 if k == 0:
                     work[g] = own_sum(g).astype(work.dtype)
-                    send(g, ours, full_land.at[g], 3, 3, near)
+                    send(g, ours, full_land.at[g], 6, 2, near)
                 elif k == 6:
-                    recv(g, total.at[kept], 6)
+                    recv(g, total.at[kept], 2)
                 elif k == 7:
-                    recv(g, total.at[gone], 8)
+                    recv(g, total.at[gone], 3)
             elif k == 1:
                 value = own_sum(g)
-                recv(g, full_land.at[g], 3)
+                recv(g, full_land.at[g], 2)
                 work[g] = (value + full_land[g].astype(f32)).astype(work.dtype)
-                send(g, ours.at[gone], half_land.at[g], 4, 4, middle)
+                send(g, ours.at[gone], half_land.at[g], 7, 3, middle)
             elif k == 2:
-                recv(g, half_land.at[g], 4)
+                recv(g, half_land.at[g], 3)
                 work[g, kept] = (
                     work[g, kept].astype(f32) + half_land[g].astype(f32)
                 ).astype(work.dtype)
-                send(g, ours.at[other], land.at[0, g], 0, 0, beside[first])
+                send(g, ours.at[other], land.at[0, g], 1, 0, beside[first])
             elif k == 3:
                 recv(g, land.at[0, g], 0)
                 work[g, mine] = (
@@ -801,14 +763,14 @@
                 sum_ref[g, mine] = (
                     work[g, mine].astype(f32) + land[1, g].astype(f32)
                 ).astype(sum_ref.dtype)
-                send(g, total.at[mine], total.at[mine], 7, 7, beside[first])
+                send(g, total.at[mine], total.at[mine], 4, 4, beside[first])
             elif k == 5:
-                recv(g, total.at[other], 7)
-                send(g, total.at[kept], total.at[kept], 5, 5, middle)
-                send(g, total.at[kept], total.at[kept], 6, 6, near)
+                recv(g, total.at[other], 4)
+                send(g, total.at[kept], total.at[kept], 8, 2, middle)
+                send(g, total.at[kept], total.at[kept], 8, 2, near)
             elif k == 6:
-                recv(g, total.at[gone], 5)
-                send(g, total.at[gone], total.at[gone], 8, 8, near)
+                recv(g, total.at[gone], 2)
+                send(g, total.at[gone], total.at[gone], 8, 3, near)
 
         for event in order:
             g, k = divmod(event, 10)
@@ -818,8 +780,9 @@
                 fold(g, k)
             else:
                 along(g, k)
-        for made in sent:
-            made.wait_send()
+        for leave, pieces in sent.items():
+            gone = spare.at[pl.ds(0, pieces)]
+            copy(0, gone, gone, leave, 0, beside["x"]).wait_send()
 
     @pl.when(inner)
     def _():
@@ -829,9 +792,16 @@
     def _():
         program(LINE_ORDERS[1], False)
 
-    for g in range(kvol):
-        for step in range(1, ny):
-            column_copy(step, g).wait_send()
+    for step in range(1, ny):
+        other = lax.rem(me_y + step, ny)
+        pltpu.make_async_remote_copy(
+            src_ref=wpart_ref.at[other],
+            dst_ref=yland.at[step - 1],
+            send_sem=ysend.at[step - 1],
+            recv_sem=yrecv.at[step - 1, 0],
+            device_id=(me_x, other),
+            device_id_type=MESH,
+        ).wait_send()
     sides(lambda a, b: side_copy(a, b).wait_send(), 1)
     for a in (0, 2):
 
@@ -972,14 +942,15 @@
                 VMEM((max(ny - 1, 1), kvol) + quarters, bf16),
                 VMEM((kvol,) + quarters, bf16),
                 VMEM((kvol, 2) + quarters[1:], bf16),
-                VMEM((7, kvol) + quarters[1:], bf16),
+                VMEM((3, kvol) + quarters[1:], bf16),
+                VMEM((8 * kvol,) + quarters[1:], bf16),
                 VMEM((3, 2) + boundary, bf16),
                 VMEM((2,) + boundary, bf16),
                 VMEM((2,) + boundary, bf16),
+                dma((max(ny - 1, 1),)),
                 dma((max(ny - 1, 1), kvol)),
-                dma((max(ny - 1, 1), kvol)),
-                dma((10, kvol)),
-                dma((10, kvol)),
+                dma((9,)),
+                dma((5, kvol)),
                 dma((3, 2)),
                 dma((3, 2)),
                 dma((2,)),

time: 74.9 us -> 70.5 us (0.941)
  Pallas kernels: 70.8 us -> 66.4 us
    pallas_call x1, Pallas kernels: 46.3 us -> 41.9 us  [on_device(): pl.pallas_call(functools.partial(line_kernel, nx, ny), out_shape=(shape((...]
where the time goes in v2:
time: 70.5 us; the launch traced here: 70.3 us
  Pallas kernels  66.4 us (94%)
  local copies, waits for them, and re-layouts  3.21 us (5%)
  between operations  0.74 us (1%)
    pallas_call x1, Pallas kernels, on_device(): pl.pallas_call(functools.partial(line_kernel, nx, ny), out_shape=(shape((...  41.9 us
    pallas_call x1, Pallas kernels, on_device(): pl.pallas_call(functools.partial(exchange_kernel, nx, ny), out_shape=(sha...  12.2 us
    pallas_call x1, Pallas kernels, on_device(): pl.pallas_call(compute_kernel, out_shape=(shape((blocks, rows, width), bf...  9.64 us
    unnamed x18, local copies, waits for them, and re-layouts  3.21 us
    pallas_call x1, Pallas kernels, on_device(): pl.pallas_call(finish_kernel, out_shape=(shape((kvol, share, width), f32)...  2.66 us

profile of v2, /device:TPU:0, one launch (start us, length us, event | category | flops | bytes accessed | tf_op | source)
XLA Modules:
  0.0 70.3 jit_solution(12409962467439145970)
XLA Ops:
  0.6 0.0 copy-start.8
  0.6 0.0 copy-start.5
  0.7 0.0 copy-start.4
  0.7 0.0 copy-start.7
  0.7 0.0 copy-start
  0.7 1.1 %copy-done = bf16[1,1,8,128,256]{4,3,2,1,0:T(8,128)(2,1)S(1)} copy-done((bf16[1,1,8,128,256]{4,3,2,1,0:T(8,128)(2,1)S(1)}, bf16[1,1,8,128,256]{4,3,2,1,0:T(8,128)(2,1)}, u32[]{:S(2)}) %copy-start) | copy-done | bytes 524312
  1.7 0.0 copy-start.2
  1.7 1.5 %copy-done.2 = bf16[27,128,256]{2,1,0:T(8,128)(2,1)S(1)} copy-done((bf16[27,128,256]{2,1,0:T(8,128)(2,1)S(1)}, bf16[27,128,256]{2,1,0:T(8,128)(2,1)}, u32[]{:S(2)}) %copy-start.2) | copy-done | bytes 1769496
  3.2 0.0 copy-start.6
  3.2 0.7 copy-done.6
  3.9 0.0 copy-start.1
  3.9 0.0 copy-start.3
  3.9 12.2 %shard_map.103 = (bf16[9,2,128,256]{3,2,1,0:T(8,128)(2,1)S(1)}, bf16[27,2,128,256]{3,2,1,0:T(8,128)(2,1)S(1)}) custom-call(s32[2]{0:T(128)S(1)} %bitcast.22, bf16[8,128,256]{2,1,0:T(8,128)(2,1)S(1)} %bitcast.16, bf16[27,128,256]{2,1,0:T(8,128)(2,1)S(1)} %copy-done.2), custom_call_target="tpu_custom_call" | custom-call | tf_op jit(solution)/shard_map/pallas_call | solution.py:871
  16.1 0.0 copy-done.8
  16.1 0.0 copy-done.5
  16.1 0.0 copy-done.4
  16.1 0.0 copy-done.7
  16.1 0.0 copy-done.1
  16.2 0.0 copy-done.3
  16.2 9.6 %shard_map.104 = (bf16[8,128,256]{2,1,0:T(8,128)(2,1)}, f32[8,128,256]{2,1,0:T(8,128)S(1)}, bf16[9,2,128,256]{3,2,1,0:T(8,128)(2,1)S(1)}, bf16[2,27,4,32,256]{4,3,2,1,0:T(8,128)(2,1)S(1)}) custom-call(s32[4,27]{1,0:T(4,128)S(1)} %bitcast.20, s32[4,27]{1,0:T(4,128)S(1)} %bitcast.21, s32[27]{0:T(128)S(1)} %bitcast.25, bf16[8,128,256]{2,1,0:T(8,128)(2,1)S(1)} %bitcast.17, ...), custom_call_target="tpu_custom_call" | custom-call | tf_op jit(solution)/shard_map/pallas_call | solution.py:902
  25.8 41.9 %shard_map.105 = (bf16[27,4,32,256]{3,2,1,0:T(8,128)(2,1)S(1)}, f32[2,128,256]{2,1,0:T(8,128)S(1)}) custom-call(bf16[2,27,4,32,256]{4,3,2,1,0:T(8,128)(2,1)S(1)} %get-tuple-element.16.wpart_ref, bf16[9,2,128,256]{3,2,1,0:T(8,128)(2,1)S(1)} %get-tuple-element.17.borrowed_ref), custom_call_target="tpu_custom_call" | custom-call | tf_op jit(solution)/shard_map/pallas_call | solution.py:935
  67.7 2.7 %shard_map.106 = (f32[27,128,256]{2,1,0:T(8,128)}, bf16[8,128,256]{2,1,0:T(8,128)(2,1)}) custom-call(s32[2]{0:T(128)S(1)} %bitcast.23, bf16[27,128,256]{2,1,0:T(8,128)(2,1)S(1)} %bitcast.18, f32[8,128,256]{2,1,0:T(8,128)S(1)} %get-tuple-element.19.own_ref, f32[2,128,256]{2,1,0:T(8,128)S(1)} %get-tuple-element.20.returned_ref), custom_call_target="tpu_custom_call" | custom-call | tf_op jit(solution)/shard_map/pallas_call | solution.py:1000
Async XLA Ops:
  0.6 15.5 %copy-start.8 = (s32[1,1,27]{2,1,0:T(1,128)S(1)}, s32[1,1,27]{2,1,0:T(1,128)}, u32[]{:S(2)}) copy-start(s32[1,1,27]{2,1,0:T(1,128)} %param.14) | copy-start | bytes 328
  0.6 15.5 %copy-start.5 = (s32[1,1,27,4]{2,3,1,0:T(4,128)S(1)}, s32[1,1,27,4]{2,3,1,0:T(4,128)}, u32[]{:S(2)}) copy-start(s32[1,1,27,4]{2,3,1,0:T(4,128)} %param.13) | copy-start | bytes 1300
  0.7 15.5 %copy-start.4 = (s32[1,1,27,4]{2,3,1,0:T(4,128)S(1)}, s32[1,1,27,4]{2,3,1,0:T(4,128)}, u32[]{:S(2)}) copy-start(s32[1,1,27,4]{2,3,1,0:T(4,128)} %param.12) | copy-start | bytes 1300
  0.7 15.5 %copy-start.7 = (f32[256]{0:T(256)S(1)}, f32[256]{0:T(256)}, u32[]{:S(2)}) copy-start(f32[256]{0:T(256)} %param.10) | copy-start | bytes 3076
  0.7 1.1 %copy-start = (bf16[1,1,8,128,256]{4,3,2,1,0:T(8,128)(2,1)S(1)}, bf16[1,1,8,128,256]{4,3,2,1,0:T(8,128)(2,1)}, u32[]{:S(2)}) copy-start(bf16[1,1,8,128,256]{4,3,2,1,0:T(8,128)(2,1)} %param.8) | copy-start | bytes 1572868
  1.7 1.5 %copy-start.2 = (bf16[27,128,256]{2,1,0:T(8,128)(2,1)S(1)}, bf16[27,128,256]{2,1,0:T(8,128)(2,1)}, u32[]{:S(2)}) copy-start(bf16[27,128,256]{2,1,0:T(8,128)(2,1)} %weight_ref.1) | copy-start | bytes 5308420
  3.2 0.7 copy-start.6
  3.9 12.3 %copy-start.1 = (bf16[1,1,8,128,256]{4,3,2,1,0:T(8,128)(2,1)S(1)}, bf16[1,1,8,128,256]{4,3,2,1,0:T(8,128)(2,1)}, u32[]{:S(2)}) copy-start(bf16[1,1,8,128,256]{4,3,2,1,0:T(8,128)(2,1)} %param.8) | copy-start | bytes 1572868
  3.9 12.3 %copy-start.3 = (bf16[1,1,8,128,256]{4,3,2,1,0:T(8,128)(2,1)S(1)}, bf16[1,1,8,128,256]{4,3,2,1,0:T(8,128)(2,1)}, u32[]{:S(2)}) copy-start(bf16[1,1,8,128,256]{4,3,2,1,0:T(8,128)(2,1)} %param.15) | copy-start | bytes 1572868

commit v3 on v2

--- a/solution.py
+++ b/solution.py
@@ -20,39 +20,39 @@
 UNROLL = 9
 VMEM_BYTES = 28 * 1024 * 1024
 EXCHANGE_BYTES = 28 * 1024 * 1024
+LINE_BYTES = 28 * 1024 * 1024
+LINE_LENGTH = 4
+MAKE_AT = (4, 12, 27)
+MAKE_LEAD = 2
 
 LINE_KINDS = (
-    'Axrri', 'Ayrri', 'Axrri', 'Axrri', 'Byr', 'Axrri', 'Ayrri', 'Axrri',
-    'Byr', 'Axrri', 'Axrri', 'Axrri', 'Byr', 'Ayrri', 'Ayrri', 'Axrri',
-    'Axrri', 'Ayrri', 'Bxr', 'Byr', 'Axrri', 'Ayrri', 'Ayrri', 'Ayrri',
-    'Ayrri', 'Byr', 'Ayrri',
+    'Ax', 'Ay', 'Ax', 'By', 'Ay', 'Ax', 'Ay', 'Ax', 'By',
+    'Ay', 'Ax', 'Ay', 'Ax', 'Ay', 'Ax', 'By', 'Ay', 'Ax',
+    'Bx', 'Ay', 'Ax', 'Ax', 'By', 'Ay', 'Ax', 'Ay', 'By',
 )
 LINE_ORDERS = (
 (
-    0, 10, 20, 60, 30, 130, 50, 140, 70, 170, 90, 210, 100, 1, 41, 220,
-    110, 230, 150, 81, 21, 160, 240, 200, 31, 2, 121, 260, 11, 61, 51, 131,
-    71, 181, 141, 91, 22, 171, 101, 211, 111, 221, 151, 32, 191, 231, 161, 241,
-    201, 12, 261, 42, 62, 52, 270, 82, 132, 72, 251, 122, 142, 92, 172, 102,
-    3, 212, 112, 23, 222, 152, 232, 33, 162, 242, 202, 13, 262, 63, 53, 73,
-    192, 93, 252, 4, 103, 24, 113, 34, 133, 143, 14, 43, 153, 64, 83, 163,
-    54, 123, 173, 74, 182, 203, 94, 193, 213, 104, 253, 223, 114, 233, 134, 243,
-    271, 144, 263, 44, 154, 84, 164, 6, 124, 174, 183, 204, 194, 214, 254, 224,
-    234, 244, 264, 45, 16, 26, 85, 7, 66, 36, 125, 136, 184, 56, 195, 146,
-    76, 255, 176, 17, 96, 27, 216, 46, 67, 106, 37, 226, 86, 185, 137, 116,
-    236, 126, 57, 147, 156, 246, 77, 177, 166, 266, 196, 97, 217, 206, 256, 107,
-    227, 186, 117, 237, 157, 247, 167, 267, 207,
+    1, 31, 81, 21, 51, 2, 151, 11, 41, 71, 61, 101, 181, 91, 121, 22,
+    111, 141, 131, 171, 161, 201, 52, 221, 191, 211, 231, 241, 12, 251, 32, 42,
+    72, 270, 82, 62, 102, 261, 152, 92, 122, 112, 142, 3, 132, 172, 23, 162,
+    202, 192, 53, 212, 232, 242, 13, 252, 43, 73, 103, 222, 123, 262, 4, 143,
+    24, 173, 54, 63, 93, 14, 33, 203, 44, 83, 213, 74, 153, 113, 104, 182,
+    243, 124, 223, 133, 144, 263, 163, 174, 193, 64, 233, 271, 94, 253, 34, 204,
+    84, 214, 6, 154, 114, 183, 244, 224, 134, 264, 164, 194, 234, 254, 35, 16,
+    26, 85, 7, 46, 56, 155, 66, 184, 76, 225, 96, 106, 265, 116, 17, 126,
+    27, 136, 36, 47, 146, 57, 166, 86, 185, 67, 176, 196, 156, 77, 97, 206,
+    236, 107, 117, 216, 256, 226, 127, 137, 246, 266, 147, 167, 186, 177, 197, 207,
+    237, 217, 257, 247,
 ),
 (
-    0, 10, 40, 20, 60, 30, 130, 80, 50, 140, 70, 170, 120, 90, 210, 100,
-    1, 180, 220, 110, 230, 150, 190, 21, 160, 240, 200, 31, 250, 260, 11, 61,
-    51, 131, 71, 141, 2, 91, 171, 22, 101, 211, 111, 221, 151, 32, 231, 161,
-    241, 201, 12, 261, 270, 62, 52, 72, 92, 102, 112, 132, 142, 152, 162, 172,
-    202, 212, 222, 232, 242, 262, 5, 25, 35, 271, 15, 65, 55, 75, 95, 6,
-    105, 115, 26, 135, 16, 145, 36, 155, 165, 175, 205, 215, 66, 7, 225, 235,
-    27, 245, 136, 265, 17, 56, 146, 46, 37, 76, 176, 86, 96, 216, 126, 67,
-    106, 226, 196, 137, 116, 236, 256, 57, 147, 156, 246, 47, 77, 177, 166, 266,
-    87, 97, 217, 206, 127, 107, 227, 186, 117, 237, 197, 157, 247, 257, 167, 267,
-    187, 207,
+    1, 21, 51, 11, 41, 71, 61, 101, 91, 2, 121, 111, 22, 141, 131, 171,
+    161, 201, 52, 191, 211, 231, 241, 12, 251, 270, 42, 72, 102, 122, 142, 172,
+    62, 92, 202, 212, 112, 242, 132, 162, 192, 232, 252, 5, 25, 55, 271, 15,
+    45, 75, 105, 125, 6, 145, 175, 26, 65, 16, 95, 56, 205, 215, 115, 245,
+    135, 46, 7, 165, 195, 27, 235, 66, 255, 17, 76, 96, 36, 57, 106, 116,
+    86, 126, 136, 156, 47, 146, 166, 226, 67, 176, 196, 266, 77, 97, 206, 236,
+    37, 107, 117, 216, 256, 87, 127, 137, 246, 157, 147, 167, 186, 177, 197, 227,
+    207, 237, 267, 217, 257, 187, 247,
 ),
 )
 
@@ -266,9 +266,8 @@
 
     lax.fori_loop(0, blocks, activate, 0)
 
-    line = len(wpart_ref.shape) == 5
     filled = 2 * kvol * share_tiles
-    if not line and filled < tiles:
+    if filled < tiles:
         for y in range(ny):
             wpart_ref[y, filled:] = jnp.zeros((tiles - filled, TILE, LANES), wpart_ref.dtype)
 
@@ -277,16 +276,12 @@
         pulled = jnp.concatenate([dpre[t] for t in targets], axis=0)
         taken = jnp.concatenate([turned[s] for s in reads], axis=1)
         part = jnp.dot(taken, pulled, preferred_element_type=jnp.float32).astype(wpart_ref.dtype)
-        if line:
-            for y in range(ny):
-                wpart_ref[y, k] = part[y * share : (y + 1) * share].reshape(wpart_ref.shape[2:])
-        else:
-            for y in range(ny):
-                for h in range(width // LANES):
-                    piece = part[y * share : (y + 1) * share, h * LANES : (h + 1) * LANES]
-                    wpart_ref[y, pl.ds((h * kvol + k) * share_tiles, share_tiles)] = piece.reshape(
-                        share_tiles, TILE, LANES
-                    )
+        for y in range(ny):
+            for h in range(width // LANES):
+                piece = part[y * share : (y + 1) * share, h * LANES : (h + 1) * LANES]
+                wpart_ref[y, pl.ds((h * kvol + k) * share_tiles, share_tiles)] = piece.reshape(
+                    share_tiles, TILE, LANES
+                )
         back = lax.dot_general(
             pulled, weight_ref[k], (((1,), (1,)), ((), ())), preferred_element_type=jnp.float32
         )
@@ -521,13 +516,121 @@
             back_copy(a).wait_send()
 
 
+def layer_kernel(
+    source_ref,
+    target_ref,
+    count_ref,
+    feats_ref,
+    halo_ref,
+    weight_ref,
+    bias_ref,
+    cot_ref,
+    out_ref,
+    own_ref,
+    borrowed_ref,
+    dpre_ref,
+    turned_ref,
+    table,
+    pre,
+    grad,
+    out,
+    osem,
+):
+    blocks, rows, width = feats_ref.shape
+    slots = source_ref.shape[0]
+    kvol = weight_ref.shape[0]
+    total_blocks = table.shape[0]
+    shared_count = halo_ref.shape[1]
+    f32 = jnp.float32
+    places = [(b, feats_ref.at[b]) for b in range(blocks)]
+    at = blocks
+    for d in range(9):
+        if d != 4:
+            for s in range(shared_count):
+                places.append((at, halo_ref.at[d, s]))
+                at += 1
+    for t, ref in places:
+        value = ref[...]
+        table[t] = value
+        turned_ref[t] = value.T
+    for b in range(blocks):
+        pre[b] = jnp.broadcast_to(bias_ref[...], (rows, width))
+    for t in range(total_blocks):
+        grad[t] = jnp.zeros((rows, width), f32)
+    pre[blocks] = jnp.zeros((rows, width), f32)
+    grad[total_blocks] = jnp.zeros((rows, width), f32)
+    dpre_ref[blocks] = jnp.zeros((rows, width), dpre_ref.dtype)
+
+    def forward(k, carry):
+        live = count_ref[k]
+        taken, targets = [], []
+        for q in range(slots):
+            taken.append(table[jnp.where(q < live, source_ref[q, k], 0)])
+            targets.append(jnp.where(q < live, target_ref[q, k], blocks))
+        made = jnp.dot(jnp.concatenate(taken, axis=0), weight_ref[k], preferred_element_type=f32)
+        for q, target in enumerate(targets):
+            pre[target] += made[q * rows : (q + 1) * rows]
+        return carry
+
+    lax.fori_loop(0, kvol, forward, 0, unroll=UNROLL)
+
+    def activate(b, carry):
+        value = pre[b]
+        sig = jax.nn.sigmoid(value)
+        out[b] = (value * sig).astype(out.dtype)
+        dpre_ref[b] = (cot_ref[b].astype(f32) * sig * (1.0 + value * (1.0 - sig))).astype(
+            dpre_ref.dtype
+        )
+        return carry
+
+    lax.fori_loop(0, blocks, activate, 0)
+    keep = pltpu.make_async_copy(out, out_ref, osem)
+    keep.start()
+
+    def backward(k, carry):
+        live = count_ref[k]
+        pulled, spread = [], []
+        for q in range(slots):
+            pulled.append(dpre_ref[jnp.where(q < live, target_ref[q, k], blocks)])
+            spread.append(jnp.where(q < live, source_ref[q, k], total_blocks))
+        back = lax.dot_general(
+            jnp.concatenate(pulled, axis=0),
+            weight_ref[k],
+            (((1,), (1,)), ((), ())),
+            preferred_element_type=f32,
+        )
+        for q, source in enumerate(spread):
+            grad[source] += back[q * rows : (q + 1) * rows]
+        return carry
+
+    lax.fori_loop(0, kvol, backward, 0, unroll=UNROLL)
+    for b in range(blocks):
+        own_ref[b] = grad[b]
+    at = blocks
+    for d in range(9):
+        for s in range(shared_count):
+            if d != 4:
+                borrowed_ref[d, s] = grad[at].astype(borrowed_ref.dtype)
+                at += 1
+    keep.wait()
+
+
 def line_kernel(
     nx,
     ny,
-    wpart_ref,
+    source_ref,
+    target_ref,
+    count_ref,
+    send_ref,
+    turned_ref,
+    dpre_ref,
+    own_ref,
     borrowed_ref,
-    sum_ref,
-    returned_ref,
+    wide_ref,
+    feat_ref,
+    away,
+    sums,
+    back,
     work,
     yland,
     full_land,
@@ -547,7 +650,9 @@
     brecv,
 ):
     me_x, me_y = lax.axis_index("gx"), lax.axis_index("gy")
-    kvol = work.shape[0]
+    kvol, parts, deep, width = work.shape
+    slots = source_ref.shape[0]
+    blocks, rows = own_ref.shape[:2]
     f32 = jnp.float32
     bit_x, bit_y, z = lax.rem(me_x, 2), lax.rem(me_x // 2, 2), me_x // 4
     high = z // 2
@@ -600,7 +705,7 @@
     def column_copy(step, g):
         other = lax.rem(me_y + step, ny)
         return pltpu.make_async_remote_copy(
-            src_ref=wpart_ref.at[other, g],
+            src_ref=away.at[step - 1, g],
             dst_ref=yland.at[step - 1, g],
             send_sem=ysend.at[step - 1],
             recv_sem=yrecv.at[step - 1, g],
@@ -608,19 +713,42 @@
             device_id_type=MESH,
         )
 
-    for g in range(kvol):
+    def make(g, carry):
+        live = count_ref[g]
+        taken, pulled = [], []
+        for q in range(slots):
+            taken.append(turned_ref[jnp.where(q < live, source_ref[q, g], 0)])
+            pulled.append(dpre_ref[jnp.where(q < live, target_ref[q, g], blocks)])
+        part = jnp.dot(
+            jnp.concatenate(taken, axis=1),
+            jnp.concatenate(pulled, axis=0),
+            preferred_element_type=f32,
+        ).astype(work.dtype).reshape(ny, parts, deep, width)
+        for y in range(ny):
+            step = lax.rem(y - me_y + ny, ny)
+            for d in range(ny):
+
+                @pl.when(step == d)
+                def _():
+                    if d == 0:
+                        work[g] = part[y]
+                    else:
+                        away[d - 1, g] = part[y]
+
         for step in range(1, ny):
             column_copy(step, g).start()
+        return carry
+
     sides(lambda a, b: side_copy(a, b).start(), 1)
 
     def give_back():
-        returned_ref[...] = jnp.zeros(returned_ref.shape, f32)
+        back[...] = jnp.zeros(back.shape, f32)
         for b in (0, 2):
 
             @pl.when(exists(me_y + 1 - b, ny))
             def _():
                 side_copy(1, b).wait_recv()
-                returned_ref[...] += side_land[1, b // 2].astype(f32)
+                back[...] += side_land[1, b // 2].astype(f32)
 
         for a in (0, 2):
 
@@ -650,27 +778,54 @@
             @pl.when(exists(me_x + 1 - a, nx))
             def _():
                 back_copy(a).wait_recv()
-                returned_ref[...] += x_land[a // 2].astype(f32)
+                back[...] += x_land[a // 2].astype(f32)
+
+        for b in range(blocks):
+            value = own_ref[b]
+            for s in range(back.shape[0]):
+                value = value + jnp.where(send_ref[s] == b, back[s], 0.0)
+            feat_ref[b] = value.astype(feat_ref.dtype)
 
     def own_sum(g):
-        value = wpart_ref[me_y, g].astype(f32)
+        value = work[g].astype(f32)
         for step in range(1, ny):
             column_copy(step, g).wait_recv()
             value = value + yland[step - 1, g].astype(f32)
         return value
 
+    def first_send(g):
+        kind = LINE_KINDS[g]
+        if kind[0] == "B":
+
+            @pl.when(jnp.logical_not(inner))
+            def _():
+                work[g] = own_sum(g).astype(work.dtype)
+                copy(g, work.at[g], full_land.at[g], 6, 2, near).start()
+
+        else:
+            gone = 2 - 2 * (bit_x if kind[1] == "x" else bit_y)
+            work[g] = own_sum(g).astype(work.dtype)
+            copy(
+                g, work.at[g, pl.ds(gone, 2)], half_land.at[g], 0, 0, beside[kind[1]]
+            ).start()
+
+    def copy(g, src, dst, leave, arrive, device):
+        return pltpu.make_async_remote_copy(
+            src_ref=src,
+            dst_ref=dst,
+            send_sem=csend.at[leave],
+            recv_sem=crecv.at[arrive, g],
+            device_id=(device, me_y),
+            device_id_type=MESH,
+        )
+
     def program(order, inside):
         sent = {}
-
-        def copy(g, src, dst, leave, arrive, device):
-            return pltpu.make_async_remote_copy(
-                src_ref=src,
-                dst_ref=dst,
-                send_sem=csend.at[leave],
-                recv_sem=crecv.at[arrive, g],
-                device_id=(device, me_y),
-                device_id_type=MESH,
-            )
+        for kind in LINE_KINDS:
+            if kind[0] == "A":
+                sent[0] = sent.get(0, 0) + parts // 2
+            elif not inside:
+                sent[6] = sent.get(6, 0) + parts
 
         def send(g, src, dst, leave, arrive, device):
             copy(g, src, dst, leave, arrive, device).start()
@@ -678,6 +833,9 @@
 
         def recv(g, dst, arrive):
             copy(g, dst, dst, 0, arrive, beside["x"]).wait_recv()
+
+        def finish(g):
+            wide_ref[g] = sums[g].reshape(parts * deep, width).astype(f32) * (1.0 / rows)
 
         def along(g, k):
             first = LINE_KINDS[g][1]
@@ -686,11 +844,8 @@
             hb, qb = bits[first], bits[second]
             mine, other = 2 * hb + qb, 2 * hb + 1 - qb
             kept, gone = pl.ds(2 * hb, 2), pl.ds(2 - 2 * hb, 2)
-            total, ours = sum_ref.at[g], work.at[g]
-            if k == 0:
-                work[g] = own_sum(g).astype(work.dtype)
-                send(g, ours.at[gone], half_land.at[g], 0, 0, beside[first])
-            elif k == 1:
+            total, ours = sums.at[g], work.at[g]
+            if k == 1:
                 recv(g, half_land.at[g], 0)
                 work[g, kept] = (
                     work[g, kept].astype(f32) + half_land[g].astype(f32)
@@ -711,9 +866,9 @@
                 send(g, ours.at[mine], land.at[2, g], 3, 3, middle)
             elif k == 4:
                 recv(g, land.at[2, g], 3)
-                sum_ref[g, mine] = (
+                sums[g, mine] = (
                     work[g, mine].astype(f32) + land[2, g].astype(f32)
-                ).astype(sum_ref.dtype)
+                ).astype(sums.dtype)
                 send(g, total.at[mine], total.at[mine], 2, 2, near)
                 send(g, total.at[mine], total.at[mine], 4, 0, beside[second])
             elif k == 5:
@@ -724,6 +879,7 @@
                 send(g, total.at[kept], total.at[kept], 5, 4, beside[first])
             elif k == 7:
                 recv(g, total.at[gone], 4)
+                finish(g)
 
         def fold(g, k):
             first = LINE_KINDS[g][1]
@@ -732,15 +888,13 @@
             hb, qb = high, bits[first]
             mine, other = 2 * hb + qb, 2 * hb + 1 - qb
             kept, gone = pl.ds(2 * hb, 2), pl.ds(2 - 2 * hb, 2)
-            total, ours = sum_ref.at[g], work.at[g]
+            total, ours = sums.at[g], work.at[g]
             if not inside:
-                if k == 0:
-                    work[g] = own_sum(g).astype(work.dtype)
-                    send(g, ours, full_land.at[g], 6, 2, near)
-                elif k == 6:
+                if k == 6:
                     recv(g, total.at[kept], 2)
                 elif k == 7:
                     recv(g, total.at[gone], 3)
+                    finish(g)
             elif k == 1:
                 value = own_sum(g)
                 recv(g, full_land.at[g], 2)
@@ -760,9 +914,9 @@
                 send(g, ours.at[mine], land.at[1, g], 1, 1, beside[second])
             elif k == 4:
                 recv(g, land.at[1, g], 1)
-                sum_ref[g, mine] = (
+                sums[g, mine] = (
                     work[g, mine].astype(f32) + land[1, g].astype(f32)
-                ).astype(sum_ref.dtype)
+                ).astype(sums.dtype)
                 send(g, total.at[mine], total.at[mine], 4, 4, beside[first])
             elif k == 5:
                 recv(g, total.at[other], 4)
@@ -771,6 +925,7 @@
             elif k == 6:
                 recv(g, total.at[gone], 2)
                 send(g, total.at[gone], total.at[gone], 8, 3, near)
+                finish(g)
 
         for event in order:
             g, k = divmod(event, 10)
@@ -784,6 +939,13 @@
             gone = spare.at[pl.ds(0, pieces)]
             copy(0, gone, gone, leave, 0, beside["x"]).wait_send()
 
+    at = 0
+    for upto in MAKE_AT:
+        lax.fori_loop(at, upto, make, 0)
+        for g in range(max(at - MAKE_LEAD, 0), upto - MAKE_LEAD if upto < kvol else kvol):
+            first_send(g)
+        at = upto
+
     @pl.when(inner)
     def _():
         program(LINE_ORDERS[0], True)
@@ -795,7 +957,7 @@
     for step in range(1, ny):
         other = lax.rem(me_y + step, ny)
         pltpu.make_async_remote_copy(
-            src_ref=wpart_ref.at[other],
+            src_ref=away.at[step - 1],
             dst_ref=yland.at[step - 1],
             send_sem=ysend.at[step - 1],
             recv_sem=yrecv.at[step - 1, 0],
@@ -820,13 +982,10 @@
     copies = []
     for c in range(chunks):
         at = pl.ds(c * per, per)
-        if len(total_ref.shape) == 3:
-            wide[at] = total_ref[at].astype(jnp.float32) * (1.0 / rows)
-        else:
-            for h in range(width // LANES):
-                wide[at, :, h * LANES : (h + 1) * LANES] = total_ref[h, at].reshape(
-                    per, share, LANES
-                ).astype(jnp.float32) * (1.0 / rows)
+        for h in range(width // LANES):
+            wide[at, :, h * LANES : (h + 1) * LANES] = total_ref[h, at].reshape(
+                per, share, LANES
+            ).astype(jnp.float32) * (1.0 / rows)
         copy = pltpu.make_async_copy(wide.at[at], weight_ref.at[at], wsem.at[c])
         copy.start()
         copies.append(copy)
@@ -838,6 +997,19 @@
         copy = pltpu.make_async_copy(feats.at[b], feat_ref.at[b], fsem.at[b])
         copy.start()
         copies.append(copy)
+    for copy in copies:
+        copy.wait()
+
+
+def store_kernel(wide_ref, feat_ref, weight_out, feat_out, sem):
+    chunks = sem.shape[0] - 1
+    per = wide_ref.shape[0] // chunks
+    copies = [pltpu.make_async_copy(feat_ref, feat_out, sem.at[chunks])]
+    for c in range(chunks):
+        at = pl.ds(c * per, per)
+        copies.append(pltpu.make_async_copy(wide_ref.at[at], weight_out.at[at], sem.at[c]))
+    for copy in copies:
+        copy.start()
     for copy in copies:
         copy.wait()
 
@@ -892,20 +1064,91 @@
     )(shared, feats, kernel_weight)
 
     total_blocks = blocks + (squares - 1) * shared_count
+    if nx == 4 * LINE_LENGTH and kvol == len(LINE_KINDS):
+        rules = (rule_source[0, 0].T, rule_target[0, 0].T, live_counts.reshape(-1))
+        boundary = (shared_count, rows, width)
+        quarters = (4, share // 4, width)
+        outputs, own, borrowed, dpre, turned = pl.pallas_call(
+            layer_kernel,
+            out_shape=(
+                shape((blocks, rows, width), bf16),
+                shape((blocks, rows, width), f32),
+                shape((squares,) + boundary, bf16),
+                shape((blocks + 1, rows, width), bf16),
+                shape((total_blocks, width, rows), bf16),
+            ),
+            in_specs=[smem, smem, smem, vmem, vmem, vmem, vmem, vmem],
+            out_specs=(hbm, vmem, vmem, vmem, vmem),
+            scratch_shapes=[
+                VMEM((total_blocks, rows, width), bf16),
+                VMEM((blocks + 1, rows, width), f32),
+                VMEM((total_blocks + 1, rows, width), f32),
+                VMEM((blocks, rows, width), bf16),
+                dma(()),
+            ],
+            compiler_params=pltpu.CompilerParams(vmem_limit_bytes=VMEM_BYTES),
+        )(
+            *rules,
+            feats,
+            halo,
+            full.reshape(kvol, width, width),
+            channel_bias.reshape(1, width),
+            out_grad[0, 0],
+        )
+        wide, feat = pl.pallas_call(
+            functools.partial(line_kernel, nx, ny),
+            out_shape=(shape((kvol, share, width), f32), shape((blocks, rows, width), bf16)),
+            in_specs=[smem, smem, smem, smem, vmem, vmem, vmem, vmem],
+            out_specs=(vmem, vmem),
+            scratch_shapes=[
+                VMEM((max(ny - 1, 1), kvol) + quarters, bf16),
+                VMEM((kvol,) + quarters, bf16),
+                VMEM(boundary, f32),
+                VMEM((kvol,) + quarters, bf16),
+                VMEM((max(ny - 1, 1), kvol) + quarters, bf16),
+                VMEM((kvol,) + quarters, bf16),
+                VMEM((kvol, 2) + quarters[1:], bf16),
+                VMEM((3, kvol) + quarters[1:], bf16),
+                VMEM((8 * kvol,) + quarters[1:], bf16),
+                VMEM((3, 2) + boundary, bf16),
+                VMEM((2,) + boundary, bf16),
+                VMEM((2,) + boundary, bf16),
+                dma((max(ny - 1, 1),)),
+                dma((max(ny - 1, 1), kvol)),
+                dma((9,)),
+                dma((5, kvol)),
+                dma((3, 2)),
+                dma((3, 2)),
+                dma((2,)),
+                dma((2,)),
+            ],
+            compiler_params=pltpu.CompilerParams(
+                collective_id=2, has_side_effects=True, vmem_limit_bytes=LINE_BYTES
+            ),
+        )(*rules, shared, turned, dpre, own, borrowed)
+        chunks = max(c for c in range(1, 10) if kvol % c == 0)
+        weight_grad, feat_grad = pl.pallas_call(
+            store_kernel,
+            out_shape=(shape((kvol, share, width), f32), shape((blocks, rows, width), bf16)),
+            in_specs=[vmem, vmem],
+            out_specs=(hbm, hbm),
+            scratch_shapes=[dma((chunks + 1,))],
+            compiler_params=pltpu.CompilerParams(vmem_limit_bytes=VMEM_BYTES),
+        )(wide, feat)
+        return (outputs[None, None], feat_grad[None, None], weight_grad)
+
     used = (width // LANES) * kvol * (share // TILE)
     groups = len(KINDS)
     unit = groups * nx
     tiles = -(-used // unit) * unit
     depth = tiles // unit
-    line = nx == 16 and kvol == len(LINE_KINDS)
-    quarters = (4, share // 4, width)
     outputs, own, borrowed, wpart = pl.pallas_call(
         compute_kernel,
         out_shape=(
             shape((blocks, rows, width), bf16),
             shape((blocks, rows, width), f32),
             shape((squares, shared_count, rows, width), bf16),
-            shape((ny, kvol) + quarters if line else (ny, tiles, TILE, LANES), bf16),
+            shape((ny, tiles, TILE, LANES), bf16),
         ),
         in_specs=[smem, smem, smem, vmem, vmem, vmem, vmem, vmem],
         out_specs=(vmem, vmem, vmem, vmem),
@@ -931,71 +1174,38 @@
     steps = nx.bit_length() - 1
     block = (depth, TILE, LANES)
     boundary = (shared_count, rows, width)
-    if line:
-        total, returned = pl.pallas_call(
-            functools.partial(line_kernel, nx, ny),
-            out_shape=(shape((kvol,) + quarters, bf16), shape(boundary, f32)),
-            in_specs=[vmem, vmem],
-            out_specs=(vmem, vmem),
-            scratch_shapes=[
-                VMEM((kvol,) + quarters, bf16),
-                VMEM((max(ny - 1, 1), kvol) + quarters, bf16),
-                VMEM((kvol,) + quarters, bf16),
-                VMEM((kvol, 2) + quarters[1:], bf16),
-                VMEM((3, kvol) + quarters[1:], bf16),
-                VMEM((8 * kvol,) + quarters[1:], bf16),
-                VMEM((3, 2) + boundary, bf16),
-                VMEM((2,) + boundary, bf16),
-                VMEM((2,) + boundary, bf16),
-                dma((max(ny - 1, 1),)),
-                dma((max(ny - 1, 1), kvol)),
-                dma((9,)),
-                dma((5, kvol)),
-                dma((3, 2)),
-                dma((3, 2)),
-                dma((2,)),
-                dma((2,)),
-            ],
-            compiler_params=pltpu.CompilerParams(
-                collective_id=1, has_side_effects=True, vmem_limit_bytes=VMEM_BYTES
-            ),
-        )(wpart, borrowed)
-        total = total.reshape(kvol, share, width)
-    else:
-        total, returned = pl.pallas_call(
-            functools.partial(reduce_kernel, nx, ny),
-            out_shape=(
-                shape((groups, nx) + block, bf16),
-                shape(boundary, f32),
-            ),
-            in_specs=[vmem, vmem],
-            out_specs=(vmem, vmem),
-            scratch_shapes=[
-                VMEM((groups, nx) + block, bf16),
-                VMEM((max(ny - 1, 1), groups, nx) + block, bf16),
-                VMEM((groups, nx) + block, bf16),
-                VMEM((3, 2) + boundary, bf16),
-                VMEM((2,) + boundary, bf16),
-                VMEM((2,) + boundary, bf16),
-                dma((max(ny - 1, 1), groups)),
-                dma((max(ny - 1, 1), groups)),
-                dma((steps, groups)),
-                dma((steps, groups)),
-                dma((steps, groups)),
-                dma((steps, groups)),
-                dma((3, 2)),
-                dma((3, 2)),
-                dma((2,)),
-                dma((2,)),
-            ],
-            compiler_params=pltpu.CompilerParams(
-                collective_id=1, has_side_effects=True, vmem_limit_bytes=VMEM_BYTES
-            ),
-        )(wpart.reshape((ny, groups, nx) + block), borrowed)
-        total = total.reshape(tiles, TILE, LANES)[:used].reshape(
-            width // LANES, kvol, share // TILE, TILE, LANES
-        )
-
+    total, returned = pl.pallas_call(
+        functools.partial(reduce_kernel, nx, ny),
+        out_shape=(
+            shape((groups, nx) + block, bf16),
+            shape(boundary, f32),
+        ),
+        in_specs=[vmem, vmem],
+        out_specs=(vmem, vmem),
+        scratch_shapes=[
+            VMEM((groups, nx) + block, bf16),
+            VMEM((max(ny - 1, 1), groups, nx) + block, bf16),
+            VMEM((groups, nx) + block, bf16),
+            VMEM((3, 2) + boundary, bf16),
+            VMEM((2,) + boundary, bf16),
+            VMEM((2,) + boundary, bf16),
+            dma((max(ny - 1, 1), groups)),
+            dma((max(ny - 1, 1), groups)),
+            dma((steps, groups)),
+            dma((steps, groups)),
+            dma((steps, groups)),
+            dma((steps, groups)),
+            dma((3, 2)),
+            dma((3, 2)),
+            dma((2,)),
+            dma((2,)),
+        ],
+        compiler_params=pltpu.CompilerParams(
+            collective_id=1, has_side_effects=True, vmem_limit_bytes=VMEM_BYTES
+        ),
+    )(wpart.reshape((ny, groups, nx) + block), borrowed)
+
+    halves, share_tiles = width // LANES, share // TILE
     chunks = max(c for c in range(1, 10) if kvol % c == 0)
     weight_grad, feat_grad = pl.pallas_call(
         finish_kernel,
@@ -1011,7 +1221,7 @@
         compiler_params=pltpu.CompilerParams(vmem_limit_bytes=VMEM_BYTES),
     )(
         shared,
-        total,
+        total.reshape(tiles, TILE, LANES)[:used].reshape(halves, kvol, share_tiles, TILE, LANES),
         own,
         returned,
     )

time: 70.5 us -> 73.7 us (1.045)
  Pallas kernels: 66.4 us -> 69.6 us
    pallas_call x1, Pallas kernels: 41.9 us -> 47.8 us  [on_device(): pl.pallas_call(functools.partial(line_kernel, nx, ny), out_shape=(shape((...]
    pallas_call x2, Pallas kernels: 12.3 us -> 9.54 us  [the longest x1 7.5 us: on_device(): pl.pallas_call(layer_kernel, out_shape=(shape((blocks, rows, width), bf16...]
where the time goes in v3:
time: 73.7 us; the launch traced here: 73.6 us
  Pallas kernels  69.6 us (94%)
  local copies, waits for them, and re-layouts  3.21 us (4%)
  between operations  0.75 us (1%)
    pallas_call x1, Pallas kernels, on_device(): pl.pallas_call(functools.partial(line_kernel, nx, ny), out_shape=(shape((...  47.8 us
    pallas_call x1, Pallas kernels, on_device(): pl.pallas_call(functools.partial(exchange_kernel, nx, ny), out_shape=(sha...  12.2 us
    pallas_call x1, Pallas kernels, on_device(): pl.pallas_call(layer_kernel, out_shape=(shape((blocks, rows, width), bf16...  7.5 us
    unnamed x18, local copies, waits for them, and re-layouts  3.21 us
    pallas_call x1, Pallas kernels, on_device(): pl.pallas_call(store_kernel, out_shape=(shape((kvol, share, width), f32),...  2.04 us

profile of v3, /device:TPU:0, one launch (start us, length us, event | category | flops | bytes accessed | tf_op | source)
XLA Modules:
  0.0 73.6 jit_solution(3576159729663674648)
XLA Ops:
  0.6 0.0 copy-start.6
  0.6 0.0 copy-start.5
  0.7 0.0 copy-start.4
  0.7 0.0 copy-start.8
  0.7 0.0 copy-start
  0.7 1.1 %copy-done = bf16[1,1,8,128,256]{4,3,2,1,0:T(8,128)(2,1)S(1)} copy-done((bf16[1,1,8,128,256]{4,3,2,1,0:T(8,128)(2,1)S(1)}, bf16[1,1,8,128,256]{4,3,2,1,0:T(8,128)(2,1)}, u32[]{:S(2)}) %copy-start) | copy-done | bytes 524312
  1.7 0.0 copy-start.2
  1.7 1.5 %copy-done.2 = bf16[27,128,256]{2,1,0:T(8,128)(2,1)S(1)} copy-done((bf16[27,128,256]{2,1,0:T(8,128)(2,1)S(1)}, bf16[27,128,256]{2,1,0:T(8,128)(2,1)}, u32[]{:S(2)}) %copy-start.2) | copy-done | bytes 1769496
  3.2 0.0 copy-start.7
  3.2 0.7 copy-done.7
  3.9 0.0 copy-start.1
  3.9 0.0 copy-start.3
  3.9 12.2 %shard_map.103 = (bf16[9,2,128,256]{3,2,1,0:T(8,128)(2,1)S(1)}, bf16[27,2,128,256]{3,2,1,0:T(8,128)(2,1)S(1)}) custom-call(s32[2]{0:T(128)S(1)} %bitcast.24, bf16[8,128,256]{2,1,0:T(8,128)(2,1)S(1)} %bitcast.15, bf16[27,128,256]{2,1,0:T(8,128)(2,1)S(1)} %copy-done.2), custom_call_target="tpu_custom_call" | custom-call | tf_op jit(solution)/shard_map/pallas_call | solution.py:1043
  16.1 0.0 copy-done.6
  16.1 0.0 copy-done.5
  16.1 0.0 copy-done.4
  16.1 0.0 copy-done.8
  16.1 0.0 copy-done.1
  16.2 0.0 copy-done.3
  16.2 7.5 %shard_map.104 = (bf16[8,128,256]{2,1,0:T(8,128)(2,1)}, f32[8,128,256]{2,1,0:T(8,128)S(1)}, bf16[9,2,128,256]{3,2,1,0:T(8,128)(2,1)S(1)}, bf16[9,128,256]{2,1,0:T(8,128)(2,1)S(1)}, bf16[24,256,128]{2,1,0:T(8,128)(2,1)S(1)}) custom-call(s32[4,27]{1,0:T(4,128)S(1)} %bitcast.18, s32[4,27]{1,0:T(4,128)S(1)} %bitcast.20, s32[27]{0:T(128)S(1)} %bitcast.22, ...), custom_call_target="tpu_custom_call" | custom-call | tf_op jit(solution)/shard_map/pallas_call | solution.py:1071
  23.7 47.8 %shard_map.105 = (f32[27,128,256]{2,1,0:T(8,128)S(1)}, bf16[8,128,256]{2,1,0:T(8,128)(2,1)S(1)}) custom-call(s32[4,27]{1,0:T(4,128)S(1)} %bitcast.19, s32[4,27]{1,0:T(4,128)S(1)} %bitcast.21, s32[27]{0:T(128)S(1)} %bitcast.23, s32[2]{0:T(128)S(1)} %bitcast.25, bf16[24,256,128]{2,1,0:T(8,128)(2,1)S(1)} %get-tuple-element.17.turned_ref, ...), custom_call_target="tpu_custom_call" | custom-call | tf_op jit(solution)/shard_map/pallas_call | solution.py:1098
  71.5 2.0 %shard_map.106 = (f32[27,128,256]{2,1,0:T(8,128)}, bf16[8,128,256]{2,1,0:T(8,128)(2,1)}) custom-call(f32[27,128,256]{2,1,0:T(8,128)S(1)} %get-tuple-element.21.wide_ref, bf16[8,128,256]{2,1,0:T(8,128)(2,1)S(1)} %get-tuple-element.22.feat_ref), custom_call_target="tpu_custom_call" | custom-call | tf_op jit(solution)/shard_map/pallas_call | solution.py:1130
Async XLA Ops:
  0.6 15.5 %copy-start.6 = (s32[1,1,27]{2,1,0:T(1,128)S(1)}, s32[1,1,27]{2,1,0:T(1,128)}, u32[]{:S(2)}) copy-start(s32[1,1,27]{2,1,0:T(1,128)} %param.14) | copy-start | bytes 328
  0.6 15.5 %copy-start.5 = (s32[1,1,27,4]{2,3,1,0:T(4,128)S(1)}, s32[1,1,27,4]{2,3,1,0:T(4,128)}, u32[]{:S(2)}) copy-start(s32[1,1,27,4]{2,3,1,0:T(4,128)} %param.13) | copy-start | bytes 1300
  0.7 15.5 %copy-start.4 = (s32[1,1,27,4]{2,3,1,0:T(4,128)S(1)}, s32[1,1,27,4]{2,3,1,0:T(4,128)}, u32[]{:S(2)}) copy-start(s32[1,1,27,4]{2,3,1,0:T(4,128)} %param.12) | copy-start | bytes 1300
  0.7 15.5 %copy-start.8 = (f32[256]{0:T(256)S(1)}, f32[256]{0:T(256)}, u32[]{:S(2)}) copy-start(f32[256]{0:T(256)} %param.10) | copy-start | bytes 3076
  0.7 1.1 %copy-start = (bf16[1,1,8,128,256]{4,3,2,1,0:T(8,128)(2,1)S(1)}, bf16[1,1,8,128,256]{4,3,2,1,0:T(8,128)(2,1)}, u32[]{:S(2)}) copy-start(bf16[1,1,8,128,256]{4,3,2,1,0:T(8,128)(2,1)} %param.8) | copy-start | bytes 1572868
  1.7 1.5 %copy-start.2 = (bf16[27,128,256]{2,1,0:T(8,128)(2,1)S(1)}, bf16[27,128,256]{2,1,0:T(8,128)(2,1)}, u32[]{:S(2)}) copy-start(bf16[27,128,256]{2,1,0:T(8,128)(2,1)} %weight_ref.1) | copy-start | bytes 5308420
  3.2 0.7 copy-start.7
  3.9 12.3 %copy-start.1 = (bf16[1,1,8,128,256]{4,3,2,1,0:T(8,128)(2,1)S(1)}, bf16[1,1,8,128,256]{4,3,2,1,0:T(8,128)(2,1)}, u32[]{:S(2)}) copy-start(bf16[1,1,8,128,256]{4,3,2,1,0:T(8,128)(2,1)} %param.8) | copy-start | bytes 1572868
  3.9 12.3 %copy-start.3 = (bf16[1,1,8,128,256]{4,3,2,1,0:T(8,128)(2,1)S(1)}, bf16[1,1,8,128,256]{4,3,2,1,0:T(8,128)(2,1)}, u32[]{:S(2)}) copy-start(bf16[1,1,8,128,256]{4,3,2,1,0:T(8,128)(2,1)} %param.15) | copy-start | bytes 1572868

commit v4 on v3

--- a/solution.py
+++ b/solution.py
@@ -21,9 +21,11 @@
 VMEM_BYTES = 28 * 1024 * 1024
 EXCHANGE_BYTES = 28 * 1024 * 1024
 LINE_BYTES = 28 * 1024 * 1024
+GATHER_BYTES = 40 * 1024 * 1024
+LAYER_BYTES = 28 * 1024 * 1024
 LINE_LENGTH = 4
-MAKE_AT = (4, 12, 27)
-MAKE_LEAD = 2
+MAKE_STEP = 4
+MAKE_LEAD = 3
 
 LINE_KINDS = (
     'Ax', 'Ay', 'Ax', 'By', 'Ay', 'Ax', 'Ay', 'Ax', 'By',
@@ -32,27 +34,30 @@
 )
 LINE_ORDERS = (
 (
-    1, 31, 81, 21, 51, 2, 151, 11, 41, 71, 61, 101, 181, 91, 121, 22,
-    111, 141, 131, 171, 161, 201, 52, 221, 191, 211, 231, 241, 12, 251, 32, 42,
-    72, 270, 82, 62, 102, 261, 152, 92, 122, 112, 142, 3, 132, 172, 23, 162,
-    202, 192, 53, 212, 232, 242, 13, 252, 43, 73, 103, 222, 123, 262, 4, 143,
-    24, 173, 54, 63, 93, 14, 33, 203, 44, 83, 213, 74, 153, 113, 104, 182,
-    243, 124, 223, 133, 144, 263, 163, 174, 193, 64, 233, 271, 94, 253, 34, 204,
-    84, 214, 6, 154, 114, 183, 244, 224, 134, 264, 164, 194, 234, 254, 35, 16,
-    26, 85, 7, 46, 56, 155, 66, 184, 76, 225, 96, 106, 265, 116, 17, 126,
-    27, 136, 36, 47, 146, 57, 166, 86, 185, 67, 176, 196, 156, 77, 97, 206,
-    236, 107, 117, 216, 256, 226, 127, 137, 246, 266, 147, 167, 186, 177, 197, 207,
-    237, 217, 257, 247,
+    0, 10, 20, 40, 50, 60, 70, 90, 100, 110, 120, 130, 140, 1, 31, 160,
+    170, 190, 200, 81, 21, 210, 230, 240, 51, 2, 151, 250, 11, 41, 71, 61,
+    101, 181, 91, 121, 22, 111, 141, 131, 171, 161, 201, 52, 221, 191, 211, 231,
+    241, 12, 251, 32, 42, 72, 270, 82, 62, 102, 261, 152, 92, 122, 112, 142,
+    3, 132, 172, 23, 162, 202, 192, 53, 212, 232, 242, 13, 252, 43, 73, 103,
+    222, 123, 262, 4, 143, 24, 173, 54, 63, 93, 14, 33, 203, 44, 83, 213,
+    74, 153, 113, 104, 182, 243, 124, 223, 133, 144, 263, 163, 174, 193, 64, 233,
+    271, 94, 253, 34, 204, 84, 214, 6, 154, 114, 183, 244, 224, 134, 264, 164,
+    194, 234, 254, 35, 16, 26, 85, 7, 46, 56, 155, 66, 184, 76, 225, 96,
+    106, 265, 116, 17, 126, 27, 136, 36, 47, 146, 57, 166, 86, 185, 67, 176,
+    196, 156, 77, 97, 206, 236, 107, 117, 216, 256, 226, 127, 137, 246, 266, 147,
+    167, 186, 177, 197, 207, 237, 217, 257, 247,
 ),
 (
-    1, 21, 51, 11, 41, 71, 61, 101, 91, 2, 121, 111, 22, 141, 131, 171,
-    161, 201, 52, 191, 211, 231, 241, 12, 251, 270, 42, 72, 102, 122, 142, 172,
-    62, 92, 202, 212, 112, 242, 132, 162, 192, 232, 252, 5, 25, 55, 271, 15,
-    45, 75, 105, 125, 6, 145, 175, 26, 65, 16, 95, 56, 205, 215, 115, 245,
-    135, 46, 7, 165, 195, 27, 235, 66, 255, 17, 76, 96, 36, 57, 106, 116,
-    86, 126, 136, 156, 47, 146, 166, 226, 67, 176, 196, 266, 77, 97, 206, 236,
-    37, 107, 117, 216, 256, 87, 127, 137, 246, 157, 147, 167, 186, 177, 197, 227,
-    207, 237, 267, 217, 257, 187, 247,
+    0, 10, 30, 20, 40, 50, 60, 80, 70, 90, 100, 110, 150, 120, 130, 140,
+    1, 180, 160, 170, 190, 200, 220, 21, 210, 230, 240, 51, 260, 250, 11, 41,
+    71, 61, 101, 91, 2, 121, 111, 22, 141, 131, 171, 161, 201, 52, 191, 211,
+    231, 241, 12, 251, 270, 42, 72, 102, 122, 142, 172, 62, 92, 202, 212, 112,
+    242, 132, 162, 192, 232, 252, 5, 25, 55, 271, 15, 45, 75, 105, 125, 6,
+    145, 175, 26, 65, 16, 95, 56, 205, 215, 115, 245, 135, 46, 7, 165, 195,
+    27, 235, 66, 255, 17, 76, 96, 36, 57, 106, 116, 86, 126, 136, 156, 47,
+    146, 166, 226, 67, 176, 196, 266, 77, 97, 206, 236, 37, 107, 117, 216, 256,
+    87, 127, 137, 246, 157, 147, 167, 186, 177, 197, 227, 207, 237, 267, 217, 257,
+    187, 247,
 ),
 )
 
@@ -516,49 +521,211 @@
             back_copy(a).wait_send()
 
 
+def gather_kernel(
+    nx,
+    ny,
+    send_in,
+    feats_ref,
+    weight_ref,
+    bias_ref,
+    table_ref,
+    turned_ref,
+    full_ref,
+    pre_ref,
+    grad_ref,
+    send_ref,
+    own,
+    stage,
+    bias,
+    lsem,
+    xsend,
+    xrecv,
+    hsend,
+    hrecv,
+    wsend,
+    wrecv,
+):
+    me_x, me_y = lax.axis_index("gx"), lax.axis_index("gy")
+    blocks, rows, width = feats_ref.shape
+    shared_count = stage.shape[0]
+    f32 = jnp.float32
+    barrier = pltpu.get_barrier_semaphore()
+    expected = greet_neighbours(barrier, me_x, me_y, nx, ny) + greet_column(
+        barrier, me_x, me_y, ny
+    )
+    load = pltpu.make_async_copy(feats_ref, own, lsem.at[0])
+    load.start()
+    pick = pltpu.make_async_copy(send_in, send_ref, lsem.at[3])
+    pick.start()
+    file = pltpu.make_async_copy(feats_ref, table_ref.at[pl.ds(0, blocks)], lsem.at[4])
+    file.start()
+    shift = pltpu.make_async_copy(bias_ref, bias, lsem.at[2])
+    shift.start()
+    keep = pltpu.make_async_copy(weight_ref, full_ref.at[:, me_y], lsem.at[1])
+    keep.start()
+    pick.wait()
+    load.wait()
+    for s in range(shared_count):
+        stage[s] = own[send_ref[s]]
+    pl.semaphore_wait(barrier, expected)
+
+    def first(a, b):
+        d = 3 * a + b
+        return blocks + shared_count * (d - (d > 4))
+
+    def place(a, b):
+        return table_ref.at[pl.ds(first(a, b), shared_count)]
+
+    def x_copy(a, device_x):
+        return pltpu.make_async_remote_copy(
+            src_ref=stage,
+            dst_ref=place(a, 1),
+            send_sem=xsend.at[a // 2],
+            recv_sem=xrecv.at[a // 2],
+            device_id=(device_x, me_y),
+            device_id_type=MESH,
+        )
+
+    def y_copy(a, b, device_y):
+        return pltpu.make_async_remote_copy(
+            src_ref=stage if a == 1 else place(a, 1),
+            dst_ref=place(a, b),
+            send_sem=hsend.at[a, b // 2],
+            recv_sem=hrecv.at[a, b // 2],
+            device_id=(me_x, device_y),
+            device_id_type=MESH,
+        )
+
+    def weight_copy(step, owner):
+        return pltpu.make_async_remote_copy(
+            src_ref=weight_ref,
+            dst_ref=full_ref.at[:, owner],
+            send_sem=wsend.at[step],
+            recv_sem=wrecv.at[step],
+            device_id=(me_x, lax.rem(me_y + step, ny)),
+            device_id_type=MESH,
+        )
+
+    def to_column(a, act):
+        for b in (0, 2):
+            target = me_y + 1 - b
+
+            @pl.when(exists(target, ny))
+            def _():
+                act(y_copy(a, b, target))
+
+    def turn(t, count):
+        for at in range(t, t + count):
+            turned_ref[at] = table_ref[at].T
+
+    def clear(a, b):
+        for at in range(first(a, b), first(a, b) + shared_count):
+            table_ref[at] = jnp.zeros((rows, width), table_ref.dtype)
+
+    for a in (0, 2):
+        target = me_x + 1 - a
+
+        @pl.when(exists(target, nx))
+        def _():
+            x_copy(a, target).start()
+
+    to_column(1, lambda copy: copy.start())
+    for step in range(1, ny):
+        weight_copy(step, me_y).start()
+    for a in (0, 2):
+
+        @pl.when(jnp.logical_not(exists(me_x + a - 1, nx)))
+        def _():
+            clear(a, 1)
+
+        for b in (0, 2):
+
+            @pl.when(jnp.logical_not(exists(me_x + a - 1, nx) & exists(me_y + b - 1, ny)))
+            def _():
+                clear(a, b)
+
+    for b in (0, 2):
+
+        @pl.when(jnp.logical_not(exists(me_y + b - 1, ny)))
+        def _():
+            clear(1, b)
+
+    file.wait()
+    turn(0, blocks)
+    shift.wait()
+    for b in range(blocks):
+        pre_ref[b] = jnp.broadcast_to(bias[...], (rows, width))
+    pre_ref[blocks] = jnp.zeros((rows, width), f32)
+
+    def blank(t, carry):
+        grad_ref[t] = jnp.zeros((rows, width), f32)
+        return carry
+
+    lax.fori_loop(0, grad_ref.shape[0], blank, 0)
+
+    def arrive(a, b):
+        @pl.when(exists(me_x + a - 1, nx) & exists(me_y + b - 1, ny))
+        def _():
+            y_copy(a, b, me_y + b - 1).wait_recv()
+
+        turn(first(a, b), shared_count)
+
+    for b in (0, 2):
+        arrive(1, b)
+    for a in (0, 2):
+
+        @pl.when(exists(me_x + a - 1, nx))
+        def _():
+            x_copy(a, me_x + a - 1).wait_recv()
+            to_column(a, lambda copy: copy.start())
+
+        turn(first(a, 1), shared_count)
+    for a in (0, 2):
+        for b in (0, 2):
+            arrive(a, b)
+
+    for a in range(3):
+
+        @pl.when(exists(me_x + a - 1, nx))
+        def _():
+            to_column(a, lambda copy: copy.wait_send())
+
+    for a in (0, 2):
+        target = me_x + 1 - a
+
+        @pl.when(exists(target, nx))
+        def _():
+            x_copy(a, target).wait_send()
+
+    for step in range(1, ny):
+        weight_copy(step, lax.rem(me_y - step + ny, ny)).wait_recv()
+        weight_copy(step, me_y).wait_send()
+    keep.wait()
+
+
 def layer_kernel(
     source_ref,
     target_ref,
     count_ref,
-    feats_ref,
-    halo_ref,
+    table,
     weight_ref,
-    bias_ref,
     cot_ref,
+    pre_in,
+    grad_in,
     out_ref,
-    own_ref,
+    pre,
+    grad,
     borrowed_ref,
     dpre_ref,
-    turned_ref,
-    table,
-    pre,
-    grad,
     out,
     osem,
 ):
-    blocks, rows, width = feats_ref.shape
+    blocks, rows, width = cot_ref.shape
     slots = source_ref.shape[0]
     kvol = weight_ref.shape[0]
     total_blocks = table.shape[0]
-    shared_count = halo_ref.shape[1]
+    shared_count = borrowed_ref.shape[1]
     f32 = jnp.float32
-    places = [(b, feats_ref.at[b]) for b in range(blocks)]
-    at = blocks
-    for d in range(9):
-        if d != 4:
-            for s in range(shared_count):
-                places.append((at, halo_ref.at[d, s]))
-                at += 1
-    for t, ref in places:
-        value = ref[...]
-        table[t] = value
-        turned_ref[t] = value.T
-    for b in range(blocks):
-        pre[b] = jnp.broadcast_to(bias_ref[...], (rows, width))
-    for t in range(total_blocks):
-        grad[t] = jnp.zeros((rows, width), f32)
-    pre[blocks] = jnp.zeros((rows, width), f32)
-    grad[total_blocks] = jnp.zeros((rows, width), f32)
     dpre_ref[blocks] = jnp.zeros((rows, width), dpre_ref.dtype)
 
     def forward(k, carry):
@@ -604,8 +771,6 @@
         return carry
 
     lax.fori_loop(0, kvol, backward, 0, unroll=UNROLL)
-    for b in range(blocks):
-        own_ref[b] = grad[b]
     at = blocks
     for d in range(9):
         for s in range(shared_count):
@@ -621,13 +786,14 @@
     source_ref,
     target_ref,
     count_ref,
-    send_ref,
+    send_in,
     turned_ref,
     dpre_ref,
     own_ref,
     borrowed_ref,
     wide_ref,
     feat_ref,
+    send_ref,
     away,
     sums,
     back,
@@ -641,18 +807,18 @@
     column,
     x_land,
     ysend,
-    yrecv,
     csend,
     crecv,
     hsend,
     hrecv,
     bsend,
     brecv,
+    picksem,
 ):
     me_x, me_y = lax.axis_index("gx"), lax.axis_index("gy")
     kvol, parts, deep, width = work.shape
     slots = source_ref.shape[0]
-    blocks, rows = own_ref.shape[:2]
+    blocks, rows = feat_ref.shape[:2]
     f32 = jnp.float32
     bit_x, bit_y, z = lax.rem(me_x, 2), lax.rem(me_x // 2, 2), me_x // 4
     high = z // 2
@@ -661,6 +827,8 @@
     near = jnp.where(inner, me_x - 4 + 8 * high, me_x + 4 - 8 * high)
     middle = me_x + 4 - 8 * high
 
+    pick = pltpu.make_async_copy(send_in, send_ref, picksem)
+    pick.start()
     barrier = pltpu.get_barrier_semaphore()
     expected = greet_neighbours(barrier, me_x, me_y, nx, ny) + greet_column(
         barrier, me_x, me_y, ny
@@ -673,6 +841,8 @@
         pl.semaphore_signal(barrier, inc=1, device_id=(middle, me_y), device_id_type=MESH)
 
     pl.semaphore_wait(barrier, expected + 3 + inner.astype(jnp.int32))
+
+    pick.wait()
 
     def side_copy(a, b):
         return pltpu.make_async_remote_copy(
@@ -708,7 +878,7 @@
             src_ref=away.at[step - 1, g],
             dst_ref=yland.at[step - 1, g],
             send_sem=ysend.at[step - 1],
-            recv_sem=yrecv.at[step - 1, g],
+            recv_sem=crecv.at[4 + step - 1, g],
             device_id=(me_x, other),
             device_id_type=MESH,
         )
@@ -793,22 +963,6 @@
             value = value + yland[step - 1, g].astype(f32)
         return value
 
-    def first_send(g):
-        kind = LINE_KINDS[g]
-        if kind[0] == "B":
-
-            @pl.when(jnp.logical_not(inner))
-            def _():
-                work[g] = own_sum(g).astype(work.dtype)
-                copy(g, work.at[g], full_land.at[g], 6, 2, near).start()
-
-        else:
-            gone = 2 - 2 * (bit_x if kind[1] == "x" else bit_y)
-            work[g] = own_sum(g).astype(work.dtype)
-            copy(
-                g, work.at[g, pl.ds(gone, 2)], half_land.at[g], 0, 0, beside[kind[1]]
-            ).start()
-
     def copy(g, src, dst, leave, arrive, device):
         return pltpu.make_async_remote_copy(
             src_ref=src,
@@ -821,11 +975,7 @@
 
     def program(order, inside):
         sent = {}
-        for kind in LINE_KINDS:
-            if kind[0] == "A":
-                sent[0] = sent.get(0, 0) + parts // 2
-            elif not inside:
-                sent[6] = sent.get(6, 0) + parts
+        made = 0
 
         def send(g, src, dst, leave, arrive, device):
             copy(g, src, dst, leave, arrive, device).start()
@@ -845,7 +995,10 @@
             mine, other = 2 * hb + qb, 2 * hb + 1 - qb
             kept, gone = pl.ds(2 * hb, 2), pl.ds(2 - 2 * hb, 2)
             total, ours = sums.at[g], work.at[g]
-            if k == 1:
+            if k == 0:
+                work[g] = own_sum(g).astype(work.dtype)
+                send(g, ours.at[gone], half_land.at[g], 0, 0, beside[first])
+            elif k == 1:
                 recv(g, half_land.at[g], 0)
                 work[g, kept] = (
                     work[g, kept].astype(f32) + half_land[g].astype(f32)
@@ -890,7 +1043,10 @@
             kept, gone = pl.ds(2 * hb, 2), pl.ds(2 - 2 * hb, 2)
             total, ours = sums.at[g], work.at[g]
             if not inside:
-                if k == 6:
+                if k == 0:
+                    work[g] = own_sum(g).astype(work.dtype)
+                    send(g, ours, full_land.at[g], 6, 2, near)
+                elif k == 6:
                     recv(g, total.at[kept], 2)
                 elif k == 7:
                     recv(g, total.at[gone], 3)
@@ -929,6 +1085,10 @@
 
         for event in order:
             g, k = divmod(event, 10)
+            while made < kvol and g < kvol and made <= g + MAKE_LEAD:
+                upto = min(kvol, made + MAKE_STEP)
+                lax.fori_loop(made, upto, make, 0)
+                made = upto
             if g == kvol:
                 (give_back, take_back)[k]()
             elif LINE_KINDS[g][0] == "B":
@@ -939,13 +1099,6 @@
             gone = spare.at[pl.ds(0, pieces)]
             copy(0, gone, gone, leave, 0, beside["x"]).wait_send()
 
-    at = 0
-    for upto in MAKE_AT:
-        lax.fori_loop(at, upto, make, 0)
-        for g in range(max(at - MAKE_LEAD, 0), upto - MAKE_LEAD if upto < kvol else kvol):
-            first_send(g)
-        at = upto
-
     @pl.when(inner)
     def _():
         program(LINE_ORDERS[0], True)
@@ -960,7 +1113,7 @@
             src_ref=away.at[step - 1],
             dst_ref=yland.at[step - 1],
             send_sem=ysend.at[step - 1],
-            recv_sem=yrecv.at[step - 1, 0],
+            recv_sem=crecv.at[4 + step - 1, 0],
             device_id=(me_x, other),
             device_id_type=MESH,
         ).wait_send()
@@ -978,7 +1131,7 @@
     chunks = wsem.shape[0]
     kvol, share, width = wide.shape
     per = kvol // chunks
-    blocks, rows = own_ref.shape[:2]
+    blocks, rows = feat_ref.shape[:2]
     copies = []
     for c in range(chunks):
         at = pl.ds(c * per, per)
@@ -1040,6 +1193,105 @@
     dma = pltpu.SemaphoreType.DMA
     squares = 9
 
+    total_blocks = blocks + (squares - 1) * shared_count
+    if nx == 4 * LINE_LENGTH and kvol == len(LINE_KINDS):
+        stay = functools.partial(pltpu.with_memory_space_constraint, memory_space=pltpu.HBM)
+        rules = (rule_source[0, 0].T, rule_target[0, 0].T, live_counts.reshape(-1))
+        boundary = (shared_count, rows, width)
+        quarters = (4, share // 4, width)
+        table, turned, full, pre, grad = pl.pallas_call(
+            functools.partial(gather_kernel, nx, ny),
+            out_shape=(
+                shape((total_blocks, rows, width), bf16),
+                shape((total_blocks, width, rows), bf16),
+                shape((kvol, ny, share, width), bf16),
+                shape((blocks + 1, rows, width), f32),
+                shape((total_blocks + 1, rows, width), f32),
+            ),
+            in_specs=[hbm] * 4,
+            out_specs=(vmem,) * 5,
+            scratch_shapes=[
+                SMEM((shared_count,), jnp.int32),
+                VMEM((blocks, rows, width), bf16),
+                VMEM(boundary, bf16),
+                VMEM((1, width), f32),
+                dma((5,)),
+                dma((2,)),
+                dma((2,)),
+                dma((3, 2)),
+                dma((3, 2)),
+                dma((ny,)),
+                dma((ny,)),
+            ],
+            compiler_params=pltpu.CompilerParams(
+                collective_id=3, has_side_effects=True, vmem_limit_bytes=GATHER_BYTES
+            ),
+        )(*(stay(v) for v in (shared, feats, kernel_weight, channel_bias.reshape(1, width))))
+        outputs, _, grad, borrowed, dpre = pl.pallas_call(
+            layer_kernel,
+            out_shape=(
+                shape((blocks, rows, width), bf16),
+                shape((blocks + 1, rows, width), f32),
+                shape((total_blocks + 1, rows, width), f32),
+                shape((squares,) + boundary, bf16),
+                shape((blocks + 1, rows, width), bf16),
+            ),
+            in_specs=[smem, smem, smem, vmem, vmem, vmem, vmem, vmem],
+            out_specs=(hbm, vmem, vmem, vmem, vmem),
+            scratch_shapes=[VMEM((blocks, rows, width), bf16), dma(())],
+            input_output_aliases={6: 1, 7: 2},
+            compiler_params=pltpu.CompilerParams(vmem_limit_bytes=LAYER_BYTES),
+        )(
+            *rules,
+            table,
+            full.reshape(kvol, width, width),
+            out_grad[0, 0],
+            pre,
+            grad,
+        )
+        wide, feat = pl.pallas_call(
+            functools.partial(line_kernel, nx, ny),
+            out_shape=(shape((kvol, share, width), f32), shape((blocks, rows, width), bf16)),
+            in_specs=[smem, smem, smem, hbm, vmem, vmem, vmem, vmem],
+            out_specs=(vmem, vmem),
+            scratch_shapes=[
+                SMEM((shared_count,), jnp.int32),
+                VMEM((max(ny - 1, 1), kvol) + quarters, bf16),
+                VMEM((kvol,) + quarters, bf16),
+                VMEM(boundary, f32),
+                VMEM((kvol,) + quarters, bf16),
+                VMEM((max(ny - 1, 1), kvol) + quarters, bf16),
+                VMEM((kvol,) + quarters, bf16),
+                VMEM((kvol, 2) + quarters[1:], bf16),
+                VMEM((3, kvol) + quarters[1:], bf16),
+                VMEM((8 * kvol,) + quarters[1:], bf16),
+                VMEM((3, 2) + boundary, bf16),
+                VMEM((2,) + boundary, bf16),
+                VMEM((2,) + boundary, bf16),
+                dma((max(ny - 1, 1),)),
+                dma((9,)),
+                dma((4 + max(ny - 1, 1), kvol)),
+                dma((3, 2)),
+                dma((3, 2)),
+                dma((2,)),
+                dma((2,)),
+                dma(()),
+            ],
+            compiler_params=pltpu.CompilerParams(
+                collective_id=2, has_side_effects=True, vmem_limit_bytes=LINE_BYTES
+            ),
+        )(*rules, stay(shared), turned, dpre, grad, borrowed)
+        chunks = max(c for c in range(1, 10) if kvol % c == 0)
+        weight_grad, feat_grad = pl.pallas_call(
+            store_kernel,
+            out_shape=(shape((kvol, share, width), f32), shape((blocks, rows, width), bf16)),
+            in_specs=[vmem, vmem],
+            out_specs=(hbm, hbm),
+            scratch_shapes=[dma((chunks + 1,))],
+            compiler_params=pltpu.CompilerParams(vmem_limit_bytes=VMEM_BYTES),
+        )(wide, feat)
+        return (outputs[None, None], feat_grad[None, None], weight_grad)
+
     halo, full = pl.pallas_call(
         functools.partial(exchange_kernel, nx, ny),
         out_shape=(
@@ -1062,80 +1314,6 @@
             collective_id=0, has_side_effects=True, vmem_limit_bytes=EXCHANGE_BYTES
         ),
     )(shared, feats, kernel_weight)
-
-    total_blocks = blocks + (squares - 1) * shared_count
-    if nx == 4 * LINE_LENGTH and kvol == len(LINE_KINDS):
-        rules = (rule_source[0, 0].T, rule_target[0, 0].T, live_counts.reshape(-1))
-        boundary = (shared_count, rows, width)
-        quarters = (4, share // 4, width)
-        outputs, own, borrowed, dpre, turned = pl.pallas_call(
-            layer_kernel,
-            out_shape=(
-                shape((blocks, rows, width), bf16),
-                shape((blocks, rows, width), f32),
-                shape((squares,) + boundary, bf16),
-                shape((blocks + 1, rows, width), bf16),
-                shape((total_blocks, width, rows), bf16),
-            ),
-            in_specs=[smem, smem, smem, vmem, vmem, vmem, vmem, vmem],
-            out_specs=(hbm, vmem, vmem, vmem, vmem),
-            scratch_shapes=[
-                VMEM((total_blocks, rows, width), bf16),
-                VMEM((blocks + 1, rows, width), f32),
-                VMEM((total_blocks + 1, rows, width), f32),
-                VMEM((blocks, rows, width), bf16),
-                dma(()),
-            ],
-            compiler_params=pltpu.CompilerParams(vmem_limit_bytes=VMEM_BYTES),
-        )(
-            *rules,
-            feats,
-            halo,
-            full.reshape(kvol, width, width),
-            channel_bias.reshape(1, width),
-            out_grad[0, 0],
-        )
-        wide, feat = pl.pallas_call(
-            functools.partial(line_kernel, nx, ny),
-            out_shape=(shape((kvol, share, width), f32), shape((blocks, rows, width), bf16)),
-            in_specs=[smem, smem, smem, smem, vmem, vmem, vmem, vmem],
-            out_specs=(vmem, vmem),
-            scratch_shapes=[
-                VMEM((max(ny - 1, 1), kvol) + quarters, bf16),
-                VMEM((kvol,) + quarters, bf16),
-                VMEM(boundary, f32),
-                VMEM((kvol,) + quarters, bf16),
-                VMEM((max(ny - 1, 1), kvol) + quarters, bf16),
-                VMEM((kvol,) + quarters, bf16),
-                VMEM((kvol, 2) + quarters[1:], bf16),
-                VMEM((3, kvol) + quarters[1:], bf16),
-                VMEM((8 * kvol,) + quarters[1:], bf16),
-                VMEM((3, 2) + boundary, bf16),
-                VMEM((2,) + boundary, bf16),
-                VMEM((2,) + boundary, bf16),
-                dma((max(ny - 1, 1),)),
-                dma((max(ny - 1, 1), kvol)),
-                dma((9,)),
-                dma((5, kvol)),
-                dma((3, 2)),
-                dma((3, 2)),
-                dma((2,)),
-                dma((2,)),
-            ],
-            compiler_params=pltpu.CompilerParams(
-                collective_id=2, has_side_effects=True, vmem_limit_bytes=LINE_BYTES
-            ),
-        )(*rules, shared, turned, dpre, own, borrowed)
-        chunks = max(c for c in range(1, 10) if kvol % c == 0)
-        weight_grad, feat_grad = pl.pallas_call(
-            store_kernel,
-            out_shape=(shape((kvol, share, width), f32), shape((blocks, rows, width), bf16)),
-            in_specs=[vmem, vmem],
-            out_specs=(hbm, hbm),
-            scratch_shapes=[dma((chunks + 1,))],
-            compiler_params=pltpu.CompilerParams(vmem_limit_bytes=VMEM_BYTES),
-        )(wide, feat)
-        return (outputs[None, None], feat_grad[None, None], weight_grad)
 
     used = (width // LANES) * kvol * (share // TILE)
     groups = len(KINDS)

time: 73.7 us -> 65.8 us (0.89)
  Pallas kernels: 69.6 us -> 65 us
  local copies, waits for them, and re-layouts: 3.21 us -> 0.02 us
    pallas_call x1, Pallas kernels: 47.8 us -> 44.4 us  [on_device(): pl.pallas_call(functools.partial(line_kernel, nx, ny), out_shape=(shape((...]
    unnamed x18 -> x8, local copies, waits for them, and re-layouts: 3.21 us -> 0.02 us
where the time goes in v4:
time: 65.8 us; the launch traced here: 65.7 us
  Pallas kernels  65 us (99%)
  between operations  0.72 us (1%)
    pallas_call x1, Pallas kernels, on_device(): pl.pallas_call(functools.partial(line_kernel, nx, ny), out_shape=(shape((...  44.4 us
    pallas_call x1, Pallas kernels, on_device(): pl.pallas_call(functools.partial(gather_kernel, nx, ny), out_shape=(shape...  11.7 us
    pallas_call x1, Pallas kernels, on_device(): pl.pallas_call(layer_kernel, out_shape=(shape((blocks, rows, width), bf16...  6.84 us
    pallas_call x1, Pallas kernels, on_device(): pl.pallas_call(store_kernel, out_shape=(shape((kvol, share, width), f32),...  2.04 us

profile of v4, /device:TPU:0, one launch (start us, length us, event | category | flops | bytes accessed | tf_op | source)
XLA Modules:
  0.0 65.7 jit_solution(5141796710978031158)
XLA Ops:
  0.6 0.0 copy-start
  0.6 0.0 copy-start.3
  0.7 0.0 copy-start.2
  0.7 0.0 copy-start.1
  0.7 11.7 %shard_map.103 = (bf16[24,128,256]{2,1,0:T(8,128)(2,1)S(1)}, bf16[24,256,128]{2,1,0:T(8,128)(2,1)S(1)}, bf16[27,2,128,256]{3,2,1,0:T(8,128)(2,1)S(1)}, f32[9,128,256]{2,1,0:T(8,128)S(1)}, f32[25,128,256]{2,1,0:T(8,128)S(1)}) custom-call(s32[2]{0:T(128)} %bitcast.23, bf16[8,128,256]{2,1,0:T(8,128)(2,1)} %bitcast.22, bf16[27,128,256]{2,1,0:T(8,128)(2,1)} %weight_ref.1, ...), custom_call_target="tpu_custom_call" | custom-call | tf_op jit(solution)/shard_map/pallas_call | solution.py:1202
  12.4 0.0 copy-done
  12.4 0.0 copy-done.3
  12.4 0.0 copy-done.2
  12.4 0.0 copy-done.1
  12.4 6.8 %shard_map.104 = (bf16[8,128,256]{2,1,0:T(8,128)(2,1)}, f32[9,128,256]{2,1,0:T(8,128)S(1)}, f32[25,128,256]{2,1,0:T(8,128)S(1)}, bf16[9,2,128,256]{3,2,1,0:T(8,128)(2,1)S(1)}, bf16[9,128,256]{2,1,0:T(8,128)(2,1)S(1)}) custom-call(s32[4,27]{1,0:T(4,128)S(1)} %bitcast.16, s32[4,27]{1,0:T(4,128)S(1)} %bitcast.18, ...), custom_call_target="tpu_custom_call", output_to_operand_aliasing={{1}: (6, {}), {2}: (7, {})} | custom-call | tf_op jit(solution)/shard_map/pallas_call | solution.py:1230
  19.3 44.4 %shard_map.105 = (f32[27,128,256]{2,1,0:T(8,128)S(1)}, bf16[8,128,256]{2,1,0:T(8,128)(2,1)S(1)}) custom-call(s32[4,27]{1,0:T(4,128)S(1)} %bitcast.17, s32[4,27]{1,0:T(4,128)S(1)} %bitcast.19, s32[27]{0:T(128)S(1)} %bitcast.21, s32[2]{0:T(128)} %bitcast.24, bf16[24,256,128]{2,1,0:T(8,128)(2,1)S(1)} %get-tuple-element.21.turned_ref, ...), custom_call_target="tpu_custom_call" | custom-call | tf_op jit(solution)/shard_map/pallas_call | solution.py:1252
  63.7 2.0 %shard_map.106 = (f32[27,128,256]{2,1,0:T(8,128)}, bf16[8,128,256]{2,1,0:T(8,128)(2,1)}) custom-call(f32[27,128,256]{2,1,0:T(8,128)S(1)} %get-tuple-element.25.wide_ref, bf16[8,128,256]{2,1,0:T(8,128)(2,1)S(1)} %get-tuple-element.26.feat_ref), custom_call_target="tpu_custom_call" | custom-call | tf_op jit(solution)/shard_map/pallas_call | solution.py:1285
Async XLA Ops:
  0.6 11.8 %copy-start = (bf16[1,1,8,128,256]{4,3,2,1,0:T(8,128)(2,1)S(1)}, bf16[1,1,8,128,256]{4,3,2,1,0:T(8,128)(2,1)}, u32[]{:S(2)}) copy-start(bf16[1,1,8,128,256]{4,3,2,1,0:T(8,128)(2,1)} %param.15) | copy-start | bytes 1572868
  0.6 11.8 %copy-start.3 = (s32[1,1,27]{2,1,0:T(1,128)S(1)}, s32[1,1,27]{2,1,0:T(1,128)}, u32[]{:S(2)}) copy-start(s32[1,1,27]{2,1,0:T(1,128)} %param.14) | copy-start | bytes 328
  0.7 11.8 %copy-start.2 = (s32[1,1,27,4]{2,3,1,0:T(4,128)S(1)}, s32[1,1,27,4]{2,3,1,0:T(4,128)}, u32[]{:S(2)}) copy-start(s32[1,1,27,4]{2,3,1,0:T(4,128)} %param.13) | copy-start | bytes 1300
  0.7 11.8 %copy-start.1 = (s32[1,1,27,4]{2,3,1,0:T(4,128)S(1)}, s32[1,1,27,4]{2,3,1,0:T(4,128)}, u32[]{:S(2)}) copy-start(s32[1,1,27,4]{2,3,1,0:T(4,128)} %param.12) | copy-start | bytes 1300

commit v5 on v4

--- a/solution.py
+++ b/solution.py
@@ -24,40 +24,40 @@
 GATHER_BYTES = 40 * 1024 * 1024
 LAYER_BYTES = 28 * 1024 * 1024
 LINE_LENGTH = 4
-MAKE_STEP = 4
+MAKE_FIRST = 10
+MAKE_STEP = 3
 MAKE_LEAD = 3
 
 LINE_KINDS = (
-    'Ax', 'Ay', 'Ax', 'By', 'Ay', 'Ax', 'Ay', 'Ax', 'By',
-    'Ay', 'Ax', 'Ay', 'Ax', 'Ay', 'Ax', 'By', 'Ay', 'Ax',
-    'Bx', 'Ay', 'Ax', 'Ax', 'By', 'Ay', 'Ax', 'Ay', 'By',
+    'Cy', 'Ay', 'Ax', 'By', 'Ay', 'Ax', 'Ay', 'Ax', 'By',
+    'Cy', 'Ay', 'Ax', 'Ay', 'Ax', 'By', 'Cy', 'Ay', 'Ax',
+    'Ay', 'Ax', 'Ax', 'Ay', 'Ax', 'Ay', 'Ax', 'Ay', 'Ax',
 )
 LINE_ORDERS = (
 (
-    0, 10, 20, 40, 50, 60, 70, 90, 100, 110, 120, 130, 140, 1, 31, 160,
-    170, 190, 200, 81, 21, 210, 230, 240, 51, 2, 151, 250, 11, 41, 71, 61,
-    101, 181, 91, 121, 22, 111, 141, 131, 171, 161, 201, 52, 221, 191, 211, 231,
-    241, 12, 251, 32, 42, 72, 270, 82, 62, 102, 261, 152, 92, 122, 112, 142,
-    3, 132, 172, 23, 162, 202, 192, 53, 212, 232, 242, 13, 252, 43, 73, 103,
-    222, 123, 262, 4, 143, 24, 173, 54, 63, 93, 14, 33, 203, 44, 83, 213,
-    74, 153, 113, 104, 182, 243, 124, 223, 133, 144, 263, 163, 174, 193, 64, 233,
-    271, 94, 253, 34, 204, 84, 214, 6, 154, 114, 183, 244, 224, 134, 264, 164,
-    194, 234, 254, 35, 16, 26, 85, 7, 46, 56, 155, 66, 184, 76, 225, 96,
-    106, 265, 116, 17, 126, 27, 136, 36, 47, 146, 57, 166, 86, 185, 67, 176,
-    196, 156, 77, 97, 206, 236, 107, 117, 216, 256, 226, 127, 137, 246, 266, 147,
-    167, 186, 177, 197, 207, 237, 217, 257, 247,
+    0, 10, 20, 40, 50, 60, 70, 90, 100, 110, 120, 130, 150, 160, 170, 180,
+    190, 31, 21, 200, 210, 11, 51, 220, 81, 230, 41, 71, 240, 250, 141, 260,
+    22, 111, 131, 61, 12, 171, 101, 52, 191, 121, 201, 161, 42, 221, 181, 72,
+    32, 211, 241, 231, 82, 251, 112, 261, 270, 132, 23, 62, 142, 172, 13, 102,
+    192, 53, 122, 202, 162, 222, 43, 182, 73, 212, 242, 232, 252, 113, 262, 24,
+    133, 14, 63, 54, 103, 123, 44, 173, 74, 193, 163, 183, 33, 114, 203, 83,
+    134, 213, 143, 64, 233, 104, 253, 124, 223, 174, 243, 194, 263, 271, 164, 184,
+    34, 204, 84, 26, 214, 144, 234, 254, 16, 224, 244, 56, 264, 76, 35, 46,
+    116, 27, 66, 136, 106, 17, 85, 176, 126, 57, 196, 166, 77, 145, 47, 206,
+    186, 117, 6, 67, 226, 216, 137, 107, 246, 36, 236, 177, 96, 127, 266, 256,
+    86, 197, 167, 207, 156, 187, 146, 227, 7, 217, 247, 237, 267, 97, 257, 157,
 ),
 (
-    0, 10, 30, 20, 40, 50, 60, 80, 70, 90, 100, 110, 150, 120, 130, 140,
-    1, 180, 160, 170, 190, 200, 220, 21, 210, 230, 240, 51, 260, 250, 11, 41,
-    71, 61, 101, 91, 2, 121, 111, 22, 141, 131, 171, 161, 201, 52, 191, 211,
-    231, 241, 12, 251, 270, 42, 72, 102, 122, 142, 172, 62, 92, 202, 212, 112,
-    242, 132, 162, 192, 232, 252, 5, 25, 55, 271, 15, 45, 75, 105, 125, 6,
-    145, 175, 26, 65, 16, 95, 56, 205, 215, 115, 245, 135, 46, 7, 165, 195,
-    27, 235, 66, 255, 17, 76, 96, 36, 57, 106, 116, 86, 126, 136, 156, 47,
-    146, 166, 226, 67, 176, 196, 266, 77, 97, 206, 236, 37, 107, 117, 216, 256,
-    87, 127, 137, 246, 157, 147, 167, 186, 177, 197, 227, 207, 237, 267, 217, 257,
-    187, 247,
+    10, 20, 30, 40, 50, 60, 70, 80, 100, 110, 120, 130, 140, 160, 170, 180,
+    190, 1, 21, 200, 210, 11, 51, 220, 91, 230, 41, 71, 240, 250, 151, 260,
+    111, 22, 131, 61, 12, 171, 101, 52, 191, 121, 201, 161, 42, 221, 181, 72,
+    2, 211, 241, 231, 92, 251, 112, 261, 270, 132, 62, 102, 122, 172, 192, 162,
+    182, 202, 152, 212, 232, 252, 222, 242, 262, 3, 93, 25, 153, 15, 55, 45,
+    75, 271, 4, 94, 26, 154, 115, 65, 135, 105, 16, 125, 56, 175, 195, 165,
+    5, 46, 185, 76, 27, 205, 66, 215, 95, 235, 225, 255, 17, 245, 116, 57,
+    265, 155, 106, 136, 47, 126, 176, 77, 6, 166, 196, 67, 186, 206, 36, 117,
+    96, 216, 226, 107, 137, 236, 246, 127, 177, 156, 256, 266, 167, 197, 37, 187,
+    207, 217, 227, 86, 87, 237, 247, 257, 267, 146, 147,
 ),
 )
 
@@ -825,7 +825,7 @@
     beside = {"x": me_x + 1 - 2 * bit_x, "y": me_x + 2 - 4 * bit_y}
     inner = exists(z - 1, 2)
     near = jnp.where(inner, me_x - 4 + 8 * high, me_x + 4 - 8 * high)
-    middle = me_x + 4 - 8 * high
+    opposite = me_x + 12 - 8 * z
 
     pick = pltpu.make_async_copy(send_in, send_ref, picksem)
     pick.start()
@@ -833,57 +833,11 @@
     expected = greet_neighbours(barrier, me_x, me_y, nx, ny) + greet_column(
         barrier, me_x, me_y, ny
     )
-    for device in (beside["x"], beside["y"], near):
+    greeted = (beside["x"], beside["y"], near, opposite)
+    for device in greeted:
         pl.semaphore_signal(barrier, inc=1, device_id=(device, me_y), device_id_type=MESH)
 
-    @pl.when(inner)
-    def _():
-        pl.semaphore_signal(barrier, inc=1, device_id=(middle, me_y), device_id_type=MESH)
-
-    pl.semaphore_wait(barrier, expected + 3 + inner.astype(jnp.int32))
-
-    pick.wait()
-
-    def side_copy(a, b):
-        return pltpu.make_async_remote_copy(
-            src_ref=borrowed_ref.at[3 * a + b],
-            dst_ref=side_land.at[a, b // 2],
-            send_sem=hsend.at[a, b // 2],
-            recv_sem=hrecv.at[a, b // 2],
-            device_id=(me_x, me_y + b - 1),
-            device_id_type=MESH,
-        )
-
-    def back_copy(a):
-        return pltpu.make_async_remote_copy(
-            src_ref=column.at[a // 2],
-            dst_ref=x_land.at[a // 2],
-            send_sem=bsend.at[a // 2],
-            recv_sem=brecv.at[a // 2],
-            device_id=(me_x + a - 1, me_y),
-            device_id_type=MESH,
-        )
-
-    def sides(act, sign):
-        for a in range(3):
-            for b in (0, 2):
-
-                @pl.when(exists(me_x + a - 1, nx) & exists(me_y + sign * (b - 1), ny))
-                def _():
-                    act(a, b)
-
-    def column_copy(step, g):
-        other = lax.rem(me_y + step, ny)
-        return pltpu.make_async_remote_copy(
-            src_ref=away.at[step - 1, g],
-            dst_ref=yland.at[step - 1, g],
-            send_sem=ysend.at[step - 1],
-            recv_sem=crecv.at[4 + step - 1, g],
-            device_id=(me_x, other),
-            device_id_type=MESH,
-        )
-
-    def make(g, carry):
+    def multiply(g, carry):
         live = count_ref[g]
         taken, pulled = [], []
         for q in range(slots):
@@ -905,10 +859,62 @@
                     else:
                         away[d - 1, g] = part[y]
 
+        return carry
+
+    lax.fori_loop(0, MAKE_FIRST, multiply, 0)
+
+    pl.semaphore_wait(barrier, expected + len(greeted))
+
+    pick.wait()
+
+    def side_copy(a, b):
+        return pltpu.make_async_remote_copy(
+            src_ref=borrowed_ref.at[3 * a + b],
+            dst_ref=side_land.at[a, b // 2],
+            send_sem=hsend.at[a, b // 2],
+            recv_sem=hrecv.at[a, b // 2],
+            device_id=(me_x, me_y + b - 1),
+            device_id_type=MESH,
+        )
+
+    def back_copy(a):
+        return pltpu.make_async_remote_copy(
+            src_ref=column.at[a // 2],
+            dst_ref=x_land.at[a // 2],
+            send_sem=bsend.at[a // 2],
+            recv_sem=brecv.at[a // 2],
+            device_id=(me_x + a - 1, me_y),
+            device_id_type=MESH,
+        )
+
+    def sides(act, sign):
+        for a in range(3):
+            for b in (0, 2):
+
+                @pl.when(exists(me_x + a - 1, nx) & exists(me_y + sign * (b - 1), ny))
+                def _():
+                    act(a, b)
+
+    def column_copy(step, g):
+        other = lax.rem(me_y + step, ny)
+        return pltpu.make_async_remote_copy(
+            src_ref=away.at[step - 1, g],
+            dst_ref=yland.at[step - 1, g],
+            send_sem=ysend.at[step - 1],
+            recv_sem=crecv.at[4 + step - 1, g],
+            device_id=(me_x, other),
+            device_id_type=MESH,
+        )
+
+    def share(g, carry):
         for step in range(1, ny):
             column_copy(step, g).start()
         return carry
 
+    def make(g, carry):
+        return share(g, multiply(g, carry))
+
+    lax.fori_loop(0, MAKE_FIRST, share, 0)
     sides(lambda a, b: side_copy(a, b).start(), 1)
 
     def give_back():
@@ -975,7 +981,7 @@
 
     def program(order, inside):
         sent = {}
-        made = 0
+        made = MAKE_FIRST
 
         def send(g, src, dst, leave, arrive, device):
             copy(g, src, dst, leave, arrive, device).start()
@@ -1016,7 +1022,7 @@
                 work[g, mine] = (
                     work[g, mine].astype(f32) + land[1, g].astype(f32)
                 ).astype(work.dtype)
-                send(g, ours.at[mine], land.at[2, g], 3, 3, middle)
+                send(g, ours.at[mine], land.at[2, g], 3, 3, opposite)
             elif k == 4:
                 recv(g, land.at[2, g], 3)
                 sums[g, mine] = (
@@ -1042,7 +1048,8 @@
             mine, other = 2 * hb + qb, 2 * hb + 1 - qb
             kept, gone = pl.ds(2 * hb, 2), pl.ds(2 - 2 * hb, 2)
             total, ours = sums.at[g], work.at[g]
-            if not inside:
+            hub = inside if LINE_KINDS[g][0] == "B" else not inside
+            if not hub:
                 if k == 0:
                     work[g] = own_sum(g).astype(work.dtype)
                     send(g, ours, full_land.at[g], 6, 2, near)
@@ -1055,7 +1062,7 @@
                 value = own_sum(g)
                 recv(g, full_land.at[g], 2)
                 work[g] = (value + full_land[g].astype(f32)).astype(work.dtype)
-                send(g, ours.at[gone], half_land.at[g], 7, 3, middle)
+                send(g, ours.at[gone], half_land.at[g], 7, 3, opposite)
             elif k == 2:
                 recv(g, half_land.at[g], 3)
                 work[g, kept] = (
@@ -1076,7 +1083,7 @@
                 send(g, total.at[mine], total.at[mine], 4, 4, beside[first])
             elif k == 5:
                 recv(g, total.at[other], 4)
-                send(g, total.at[kept], total.at[kept], 8, 2, middle)
+                send(g, total.at[kept], total.at[kept], 8, 2, opposite)
                 send(g, total.at[kept], total.at[kept], 8, 2, near)
             elif k == 6:
                 recv(g, total.at[gone], 2)
@@ -1091,7 +1098,7 @@
                 made = upto
             if g == kvol:
                 (give_back, take_back)[k]()
-            elif LINE_KINDS[g][0] == "B":
+            elif LINE_KINDS[g][0] != "A":
                 fold(g, k)
             else:
                 along(g, k)

time: 65.8 us -> 64.7 us (0.983)
  Pallas kernels: 65 us -> 63.8 us
    pallas_call x1, Pallas kernels: 44.4 us -> 43.2 us  [on_device(): pl.pallas_call(functools.partial(line_kernel, nx, ny), out_shape=(shape((...]
where the time goes in v5:
time: 64.7 us; the launch traced here: 64.5 us
  Pallas kernels  63.8 us (99%)
  between operations  0.72 us (1%)
    pallas_call x1, Pallas kernels, on_device(): pl.pallas_call(functools.partial(line_kernel, nx, ny), out_shape=(shape((...  43.2 us
    pallas_call x1, Pallas kernels, on_device(): pl.pallas_call(functools.partial(gather_kernel, nx, ny), out_shape=(shape...  11.7 us
    pallas_call x1, Pallas kernels, on_device(): pl.pallas_call(layer_kernel, out_shape=(shape((blocks, rows, width), bf16...  6.84 us
    pallas_call x1, Pallas kernels, on_device(): pl.pallas_call(store_kernel, out_shape=(shape((kvol, share, width), f32),...  2.04 us

profile of v5, /device:TPU:0, one launch (start us, length us, event | category | flops | bytes accessed | tf_op | source)
XLA Modules:
  0.0 64.5 jit_solution(11555808634667048690)
XLA Ops:
  0.6 0.0 copy-start
  0.6 0.0 copy-start.3
  0.7 0.0 copy-start.2
  0.7 0.0 copy-start.1
  0.7 11.7 %shard_map.103 = (bf16[24,128,256]{2,1,0:T(8,128)(2,1)S(1)}, bf16[24,256,128]{2,1,0:T(8,128)(2,1)S(1)}, bf16[27,2,128,256]{3,2,1,0:T(8,128)(2,1)S(1)}, f32[9,128,256]{2,1,0:T(8,128)S(1)}, f32[25,128,256]{2,1,0:T(8,128)S(1)}) custom-call(s32[2]{0:T(128)} %bitcast.23, bf16[8,128,256]{2,1,0:T(8,128)(2,1)} %bitcast.22, bf16[27,128,256]{2,1,0:T(8,128)(2,1)} %weight_ref.1, ...), custom_call_target="tpu_custom_call" | custom-call | tf_op jit(solution)/shard_map/pallas_call | solution.py:1209
  12.4 0.0 copy-done
  12.4 0.0 copy-done.3
  12.4 0.0 copy-done.2
  12.4 0.0 copy-done.1
  12.4 6.8 %shard_map.104 = (bf16[8,128,256]{2,1,0:T(8,128)(2,1)}, f32[9,128,256]{2,1,0:T(8,128)S(1)}, f32[25,128,256]{2,1,0:T(8,128)S(1)}, bf16[9,2,128,256]{3,2,1,0:T(8,128)(2,1)S(1)}, bf16[9,128,256]{2,1,0:T(8,128)(2,1)S(1)}) custom-call(s32[4,27]{1,0:T(4,128)S(1)} %bitcast.16, s32[4,27]{1,0:T(4,128)S(1)} %bitcast.18, ...), custom_call_target="tpu_custom_call", output_to_operand_aliasing={{1}: (6, {}), {2}: (7, {})} | custom-call | tf_op jit(solution)/shard_map/pallas_call | solution.py:1237
  19.3 43.2 %shard_map.105 = (f32[27,128,256]{2,1,0:T(8,128)S(1)}, bf16[8,128,256]{2,1,0:T(8,128)(2,1)S(1)}) custom-call(s32[4,27]{1,0:T(4,128)S(1)} %bitcast.17, s32[4,27]{1,0:T(4,128)S(1)} %bitcast.19, s32[27]{0:T(128)S(1)} %bitcast.21, s32[2]{0:T(128)} %bitcast.24, bf16[24,256,128]{2,1,0:T(8,128)(2,1)S(1)} %get-tuple-element.21.turned_ref, ...), custom_call_target="tpu_custom_call" | custom-call | tf_op jit(solution)/shard_map/pallas_call | solution.py:1259
  62.5 2.0 %shard_map.106 = (f32[27,128,256]{2,1,0:T(8,128)}, bf16[8,128,256]{2,1,0:T(8,128)(2,1)}) custom-call(f32[27,128,256]{2,1,0:T(8,128)S(1)} %get-tuple-element.25.wide_ref, bf16[8,128,256]{2,1,0:T(8,128)(2,1)S(1)} %get-tuple-element.26.feat_ref), custom_call_target="tpu_custom_call" | custom-call | tf_op jit(solution)/shard_map/pallas_call | solution.py:1292
Async XLA Ops:
  0.6 11.8 %copy-start = (bf16[1,1,8,128,256]{4,3,2,1,0:T(8,128)(2,1)S(1)}, bf16[1,1,8,128,256]{4,3,2,1,0:T(8,128)(2,1)}, u32[]{:S(2)}) copy-start(bf16[1,1,8,128,256]{4,3,2,1,0:T(8,128)(2,1)} %param.15) | copy-start | bytes 1572868
  0.6 11.8 %copy-start.3 = (s32[1,1,27]{2,1,0:T(1,128)S(1)}, s32[1,1,27]{2,1,0:T(1,128)}, u32[]{:S(2)}) copy-start(s32[1,1,27]{2,1,0:T(1,128)} %param.14) | copy-start | bytes 328
  0.7 11.8 %copy-start.2 = (s32[1,1,27,4]{2,3,1,0:T(4,128)S(1)}, s32[1,1,27,4]{2,3,1,0:T(4,128)}, u32[]{:S(2)}) copy-start(s32[1,1,27,4]{2,3,1,0:T(4,128)} %param.13) | copy-start | bytes 1300
  0.7 11.8 %copy-start.1 = (s32[1,1,27,4]{2,3,1,0:T(4,128)S(1)}, s32[1,1,27,4]{2,3,1,0:T(4,128)}, u32[]{:S(2)}) copy-start(s32[1,1,27,4]{2,3,1,0:T(4,128)} %param.12) | copy-start | bytes 1300

commit v6 on v5

--- a/solution.py
+++ b/solution.py
@@ -20,19 +20,23 @@
 UNROLL = 9
 VMEM_BYTES = 28 * 1024 * 1024
 EXCHANGE_BYTES = 28 * 1024 * 1024
-LINE_BYTES = 28 * 1024 * 1024
+LINE_BYTES = 42 * 1024 * 1024
 GATHER_BYTES = 40 * 1024 * 1024
 LAYER_BYTES = 28 * 1024 * 1024
 LINE_LENGTH = 4
 MAKE_FIRST = 10
 MAKE_STEP = 3
 MAKE_LEAD = 3
+CHORES_FROM = 12
+PULL_STEP = 2
+PILE_STEP = 6
 
 LINE_KINDS = (
     'Cy', 'Ay', 'Ax', 'By', 'Ay', 'Ax', 'Ay', 'Ax', 'By',
     'Cy', 'Ay', 'Ax', 'Ay', 'Ax', 'By', 'Cy', 'Ay', 'Ax',
     'Ay', 'Ax', 'Ax', 'Ay', 'Ax', 'Ay', 'Ax', 'Ay', 'Ax',
 )
+LINE_FOLDED = [g for g, kind in enumerate(LINE_KINDS) if kind[0] != "A"]
 LINE_ORDERS = (
 (
     0, 10, 20, 40, 50, 60, 70, 90, 100, 110, 120, 130, 150, 160, 170, 180,
@@ -532,7 +536,6 @@
     turned_ref,
     full_ref,
     pre_ref,
-    grad_ref,
     send_ref,
     own,
     stage,
@@ -657,12 +660,6 @@
         pre_ref[b] = jnp.broadcast_to(bias[...], (rows, width))
     pre_ref[blocks] = jnp.zeros((rows, width), f32)
 
-    def blank(t, carry):
-        grad_ref[t] = jnp.zeros((rows, width), f32)
-        return carry
-
-    lax.fori_loop(0, grad_ref.shape[0], blank, 0)
-
     def arrive(a, b):
         @pl.when(exists(me_x + a - 1, nx) & exists(me_y + b - 1, ny))
         def _():
@@ -711,21 +708,21 @@
     weight_ref,
     cot_ref,
     pre_in,
-    grad_in,
     out_ref,
     pre,
-    grad,
-    borrowed_ref,
     dpre_ref,
+    plan_ref,
     out,
+    tally,
     osem,
 ):
     blocks, rows, width = cot_ref.shape
     slots = source_ref.shape[0]
     kvol = weight_ref.shape[0]
     total_blocks = table.shape[0]
-    shared_count = borrowed_ref.shape[1]
     f32 = jnp.float32
+    for t in range(total_blocks + 1):
+        tally[t] = 0
     dpre_ref[blocks] = jnp.zeros((rows, width), dpre_ref.dtype)
 
     def forward(k, carry):
@@ -734,12 +731,38 @@
         for q in range(slots):
             taken.append(table[jnp.where(q < live, source_ref[q, k], 0)])
             targets.append(jnp.where(q < live, target_ref[q, k], blocks))
+            key = jnp.where(q < live, source_ref[q, k], total_blocks)
+            tally[key] = tally[key] + 1
         made = jnp.dot(jnp.concatenate(taken, axis=0), weight_ref[k], preferred_element_type=f32)
         for q, target in enumerate(targets):
             pre[target] += made[q * rows : (q + 1) * rows]
         return carry
 
     lax.fori_loop(0, kvol, forward, 0, unroll=UNROLL)
+
+    def keep_on(i, carry):
+        plan_ref[1, i] = 1
+        return carry
+
+    lax.fori_loop(0, plan_ref.shape[1], keep_on, 0, unroll=16)
+    run = 0
+    for t in range(total_blocks + 1):
+        count = tally[t]
+        plan_ref[1, run] = 0
+        plan_ref[2, t] = jnp.where(count > 0, run + count - 1, -1)
+        tally[t] = run
+        run = run + count
+
+    def arrange(k, carry):
+        live = count_ref[k]
+        for q in range(slots):
+            key = jnp.where(q < live, source_ref[q, k], total_blocks)
+            place = tally[key]
+            tally[key] = place + 1
+            plan_ref[0, place] = slots * k + q
+        return carry
+
+    lax.fori_loop(0, kvol, arrange, 0, unroll=3)
 
     def activate(b, carry):
         value = pre[b]
@@ -754,29 +777,6 @@
     keep = pltpu.make_async_copy(out, out_ref, osem)
     keep.start()
 
-    def backward(k, carry):
-        live = count_ref[k]
-        pulled, spread = [], []
-        for q in range(slots):
-            pulled.append(dpre_ref[jnp.where(q < live, target_ref[q, k], blocks)])
-            spread.append(jnp.where(q < live, source_ref[q, k], total_blocks))
-        back = lax.dot_general(
-            jnp.concatenate(pulled, axis=0),
-            weight_ref[k],
-            (((1,), (1,)), ((), ())),
-            preferred_element_type=f32,
-        )
-        for q, source in enumerate(spread):
-            grad[source] += back[q * rows : (q + 1) * rows]
-        return carry
-
-    lax.fori_loop(0, kvol, backward, 0, unroll=UNROLL)
-    at = blocks
-    for d in range(9):
-        for s in range(shared_count):
-            if d != 4:
-                borrowed_ref[d, s] = grad[at].astype(borrowed_ref.dtype)
-                at += 1
     keep.wait()
 
 
@@ -789,8 +789,8 @@
     send_in,
     turned_ref,
     dpre_ref,
-    own_ref,
-    borrowed_ref,
+    weight_ref,
+    plan_in,
     wide_ref,
     feat_ref,
     send_ref,
@@ -803,6 +803,9 @@
     half_land,
     land,
     spare,
+    pulls,
+    piles,
+    borrowed_ref,
     side_land,
     column,
     x_land,
@@ -915,7 +918,53 @@
         return share(g, multiply(g, carry))
 
     lax.fori_loop(0, MAKE_FIRST, share, 0)
-    sides(lambda a, b: side_copy(a, b).start(), 1)
+    total_slots = kvol * slots
+
+    def pull(k, carry):
+        live = count_ref[k]
+        taken = [
+            dpre_ref[jnp.where(q < live, target_ref[q, k], blocks)] for q in range(slots)
+        ]
+        made = lax.dot_general(
+            jnp.concatenate(taken, axis=0),
+            weight_ref[k],
+            (((1,), (1,)), ((), ())),
+            preferred_element_type=f32,
+        )
+        pulls[pl.ds(slots * k, slots)] = made.reshape(slots, rows, width)
+        return carry
+
+    def pile(i, total):
+        total = jnp.where(plan_in[1, i] == 0, 0.0, total) + pulls[plan_in[0, i]]
+        piles[i] = total
+        return total
+
+    def table_grad(t):
+        place = plan_in[2, t]
+        return jnp.where(place >= 0, piles[jnp.maximum(place, 0)], 0.0)
+
+    def pull_some(k, upto):
+        lax.fori_loop(k, upto, pull, 0)
+
+    def pile_some(i, upto):
+        start = piles[i - 1] if i else jnp.zeros((rows, width), f32)
+        lax.fori_loop(i, upto, pile, start)
+
+    def lend():
+        at = blocks
+        for d in range(9):
+            for s in range(borrowed_ref.shape[1]):
+                if d != 4:
+                    borrowed_ref[d, s] = table_grad(at).astype(borrowed_ref.dtype)
+                    at += 1
+        sides(lambda a, b: side_copy(a, b).start(), 1)
+
+    chores = [functools.partial(pull_some, k, min(k + PULL_STEP, kvol)) for k in range(0, kvol, PULL_STEP)]
+    chores += [
+        functools.partial(pile_some, i, min(i + PILE_STEP, total_slots))
+        for i in range(0, total_slots, PILE_STEP)
+    ]
+    chores.append(lend)
 
     def give_back():
         back[...] = jnp.zeros(back.shape, f32)
@@ -957,7 +1006,7 @@
                 back[...] += x_land[a // 2].astype(f32)
 
         for b in range(blocks):
-            value = own_ref[b]
+            value = table_grad(b)
             for s in range(back.shape[0]):
                 value = value + jnp.where(send_ref[s] == b, back[s], 0.0)
             feat_ref[b] = value.astype(feat_ref.dtype)
@@ -1052,7 +1101,7 @@
             if not hub:
                 if k == 0:
                     work[g] = own_sum(g).astype(work.dtype)
-                    send(g, ours, full_land.at[g], 6, 2, near)
+                    send(g, ours, full_land.at[LINE_FOLDED.index(g)], 6, 2, near)
                 elif k == 6:
                     recv(g, total.at[kept], 2)
                 elif k == 7:
@@ -1060,8 +1109,8 @@
                     finish(g)
             elif k == 1:
                 value = own_sum(g)
-                recv(g, full_land.at[g], 2)
-                work[g] = (value + full_land[g].astype(f32)).astype(work.dtype)
+                recv(g, full_land.at[LINE_FOLDED.index(g)], 2)
+                work[g] = (value + full_land[LINE_FOLDED.index(g)].astype(f32)).astype(work.dtype)
                 send(g, ours.at[gone], half_land.at[g], 7, 3, opposite)
             elif k == 2:
                 recv(g, half_land.at[g], 3)
@@ -1090,8 +1139,14 @@
                 send(g, total.at[gone], total.at[gone], 8, 3, near)
                 finish(g)
 
-        for event in order:
+        waiting = list(chores)
+        for at, event in enumerate(order):
             g, k = divmod(event, 10)
+            if event == 10 * kvol:
+                while waiting:
+                    waiting.pop(0)()
+            elif at >= CHORES_FROM and waiting:
+                waiting.pop(0)()
             while made < kvol and g < kvol and made <= g + MAKE_LEAD:
                 upto = min(kvol, made + MAKE_STEP)
                 lax.fori_loop(made, upto, make, 0)
@@ -1206,17 +1261,16 @@
         rules = (rule_source[0, 0].T, rule_target[0, 0].T, live_counts.reshape(-1))
         boundary = (shared_count, rows, width)
         quarters = (4, share // 4, width)
-        table, turned, full, pre, grad = pl.pallas_call(
+        table, turned, full, pre = pl.pallas_call(
             functools.partial(gather_kernel, nx, ny),
             out_shape=(
                 shape((total_blocks, rows, width), bf16),
                 shape((total_blocks, width, rows), bf16),
                 shape((kvol, ny, share, width), bf16),
                 shape((blocks + 1, rows, width), f32),
-                shape((total_blocks + 1, rows, width), f32),
             ),
             in_specs=[hbm] * 4,
-            out_specs=(vmem,) * 5,
+            out_specs=(vmem,) * 4,
             scratch_shapes=[
                 SMEM((shared_count,), jnp.int32),
                 VMEM((blocks, rows, width), bf16),
@@ -1234,19 +1288,22 @@
                 collective_id=3, has_side_effects=True, vmem_limit_bytes=GATHER_BYTES
             ),
         )(*(stay(v) for v in (shared, feats, kernel_weight, channel_bias.reshape(1, width))))
-        outputs, _, grad, borrowed, dpre = pl.pallas_call(
+        outputs, _, dpre, plan = pl.pallas_call(
             layer_kernel,
             out_shape=(
                 shape((blocks, rows, width), bf16),
                 shape((blocks + 1, rows, width), f32),
-                shape((total_blocks + 1, rows, width), f32),
-                shape((squares,) + boundary, bf16),
                 shape((blocks + 1, rows, width), bf16),
+                shape((3, -(-(kvol * slots + 1) // LANES) * LANES), jnp.int32),
             ),
-            in_specs=[smem, smem, smem, vmem, vmem, vmem, vmem, vmem],
-            out_specs=(hbm, vmem, vmem, vmem, vmem),
-            scratch_shapes=[VMEM((blocks, rows, width), bf16), dma(())],
-            input_output_aliases={6: 1, 7: 2},
+            in_specs=[smem, smem, smem, vmem, vmem, vmem, vmem],
+            out_specs=(hbm, vmem, vmem, smem),
+            scratch_shapes=[
+                VMEM((blocks, rows, width), bf16),
+                SMEM((total_blocks + 1,), jnp.int32),
+                dma(()),
+            ],
+            input_output_aliases={6: 1},
             compiler_params=pltpu.CompilerParams(vmem_limit_bytes=LAYER_BYTES),
         )(
             *rules,
@@ -1254,12 +1311,11 @@
             full.reshape(kvol, width, width),
             out_grad[0, 0],
             pre,
-            grad,
         )
         wide, feat = pl.pallas_call(
             functools.partial(line_kernel, nx, ny),
             out_shape=(shape((kvol, share, width), f32), shape((blocks, rows, width), bf16)),
-            in_specs=[smem, smem, smem, hbm, vmem, vmem, vmem, vmem],
+            in_specs=[smem, smem, smem, hbm, vmem, vmem, vmem, smem],
             out_specs=(vmem, vmem),
             scratch_shapes=[
                 SMEM((shared_count,), jnp.int32),
@@ -1268,10 +1324,13 @@
                 VMEM(boundary, f32),
                 VMEM((kvol,) + quarters, bf16),
                 VMEM((max(ny - 1, 1), kvol) + quarters, bf16),
-                VMEM((kvol,) + quarters, bf16),
+                VMEM((len(LINE_FOLDED),) + quarters, bf16),
                 VMEM((kvol, 2) + quarters[1:], bf16),
                 VMEM((3, kvol) + quarters[1:], bf16),
-                VMEM((8 * kvol,) + quarters[1:], bf16),
+                VMEM((2 * kvol,) + quarters[1:], bf16),
+                VMEM((kvol * slots, rows, width), f32),
+                VMEM((kvol * slots, rows, width), f32),
+                VMEM((squares,) + boundary, bf16),
                 VMEM((3, 2) + boundary, bf16),
                 VMEM((2,) + boundary, bf16),
                 VMEM((2,) + boundary, bf16),
@@ -1287,7 +1346,7 @@
             compiler_params=pltpu.CompilerParams(
                 collective_id=2, has_side_effects=True, vmem_limit_bytes=LINE_BYTES
             ),
-        )(*rules, stay(shared), turned, dpre, grad, borrowed)
+        )(*rules, stay(shared), turned, dpre, full.reshape(kvol, width, width), plan)
         chunks = max(c for c in range(1, 10) if kvol % c == 0)
         weight_grad, feat_grad = pl.pallas_call(
             store_kernel,

time: 64.7 us -> 69.7 us (1.077)
  Pallas kernels: 63.8 us -> 68.9 us
    pallas_call x1, Pallas kernels: 43.2 us -> 48.8 us  [on_device(): pl.pallas_call(functools.partial(line_kernel, nx, ny), out_shape=(shape((...]
where the time goes in v6:
time: 69.7 us; the launch traced here: 69.6 us
  Pallas kernels  68.9 us (99%)
  between operations  0.72 us (1%)
    pallas_call x1, Pallas kernels, on_device(): pl.pallas_call(functools.partial(line_kernel, nx, ny), out_shape=(shape((...  48.8 us
    pallas_call x1, Pallas kernels, on_device(): pl.pallas_call(functools.partial(gather_kernel, nx, ny), out_shape=(shape...  11.7 us
    pallas_call x1, Pallas kernels, on_device(): pl.pallas_call(layer_kernel, out_shape=(shape((blocks, rows, width), bf16...  6.26 us
    pallas_call x1, Pallas kernels, on_device(): pl.pallas_call(store_kernel, out_shape=(shape((kvol, share, width), f32),...  2.04 us

profile of v6, /device:TPU:0, one launch (start us, length us, event | category | flops | bytes accessed | tf_op | source)
XLA Modules:
  0.0 69.6 jit_solution(17703477987892987315)
XLA Ops:
  0.6 0.0 copy-start
  0.6 0.0 copy-start.3
  0.7 0.0 copy-start.2
  0.7 0.0 copy-start.1
  0.7 11.7 %shard_map.103 = (bf16[24,128,256]{2,1,0:T(8,128)(2,1)S(1)}, bf16[24,256,128]{2,1,0:T(8,128)(2,1)S(1)}, bf16[27,2,128,256]{3,2,1,0:T(8,128)(2,1)S(1)}, f32[9,128,256]{2,1,0:T(8,128)S(1)}) custom-call(s32[2]{0:T(128)} %bitcast.24, bf16[8,128,256]{2,1,0:T(8,128)(2,1)} %bitcast.23, bf16[27,128,256]{2,1,0:T(8,128)(2,1)} %weight_ref.1, f32[1,256]{1,0:T(1,128)} %bitcast.26), custom_call_target="tpu_custom_call" | custom-call | tf_op jit(solution)/shard_map/pallas_call | solution.py:1264
  12.4 0.0 copy-done
  12.4 0.0 copy-done.3
  12.4 0.0 copy-done.2
  12.4 0.0 copy-done.1
  12.4 6.3 %shard_map.104 = (bf16[8,128,256]{2,1,0:T(8,128)(2,1)}, f32[9,128,256]{2,1,0:T(8,128)S(1)}, bf16[9,128,256]{2,1,0:T(8,128)(2,1)S(1)}, s32[3,128]{1,0:T(4,128)S(1)}) custom-call(s32[4,27]{1,0:T(4,128)S(1)} %bitcast.17, s32[4,27]{1,0:T(4,128)S(1)} %bitcast.19, s32[27]{0:T(128)S(1)} %bitcast.21, ...), custom_call_target="tpu_custom_call", output_to_operand_aliasing={{1}: (6, {})} | custom-call | tf_op jit(solution)/shard_map/pallas_call | solution.py:1291
  18.7 48.8 %shard_map.105 = (f32[27,128,256]{2,1,0:T(8,128)S(1)}, bf16[8,128,256]{2,1,0:T(8,128)(2,1)S(1)}) custom-call(s32[4,27]{1,0:T(4,128)S(1)} %bitcast.18, s32[4,27]{1,0:T(4,128)S(1)} %bitcast.20, s32[27]{0:T(128)S(1)} %bitcast.22, s32[2]{0:T(128)} %bitcast.25, bf16[24,256,128]{2,1,0:T(8,128)(2,1)S(1)} %get-tuple-element.18.turned_ref, ...), custom_call_target="tpu_custom_call" | custom-call | tf_op jit(solution)/shard_map/pallas_call | solution.py:1315
  67.6 2.0 %shard_map.106 = (f32[27,128,256]{2,1,0:T(8,128)}, bf16[8,128,256]{2,1,0:T(8,128)(2,1)}) custom-call(f32[27,128,256]{2,1,0:T(8,128)S(1)} %get-tuple-element.21.wide_ref, bf16[8,128,256]{2,1,0:T(8,128)(2,1)S(1)} %get-tuple-element.22.feat_ref), custom_call_target="tpu_custom_call" | custom-call | tf_op jit(solution)/shard_map/pallas_call | solution.py:1351
Async XLA Ops:
  0.6 11.8 %copy-start = (bf16[1,1,8,128,256]{4,3,2,1,0:T(8,128)(2,1)S(1)}, bf16[1,1,8,128,256]{4,3,2,1,0:T(8,128)(2,1)}, u32[]{:S(2)}) copy-start(bf16[1,1,8,128,256]{4,3,2,1,0:T(8,128)(2,1)} %param.15) | copy-start | bytes 1572868
  0.6 11.8 %copy-start.3 = (s32[1,1,27]{2,1,0:T(1,128)S(1)}, s32[1,1,27]{2,1,0:T(1,128)}, u32[]{:S(2)}) copy-start(s32[1,1,27]{2,1,0:T(1,128)} %param.14) | copy-start | bytes 328
  0.7 11.8 %copy-start.2 = (s32[1,1,27,4]{2,3,1,0:T(4,128)S(1)}, s32[1,1,27,4]{2,3,1,0:T(4,128)}, u32[]{:S(2)}) copy-start(s32[1,1,27,4]{2,3,1,0:T(4,128)} %param.13) | copy-start | bytes 1300
  0.7 11.8 %copy-start.1 = (s32[1,1,27,4]{2,3,1,0:T(4,128)S(1)}, s32[1,1,27,4]{2,3,1,0:T(4,128)}, u32[]{:S(2)}) copy-start(s32[1,1,27,4]{2,3,1,0:T(4,128)} %param.12) | copy-start | bytes 1300

commit v7 on v5

--- a/solution.py
+++ b/solution.py
@@ -38,8 +38,8 @@
     0, 10, 20, 40, 50, 60, 70, 90, 100, 110, 120, 130, 150, 160, 170, 180,
     190, 31, 21, 200, 210, 11, 51, 220, 81, 230, 41, 71, 240, 250, 141, 260,
     22, 111, 131, 61, 12, 171, 101, 52, 191, 121, 201, 161, 42, 221, 181, 72,
-    32, 211, 241, 231, 82, 251, 112, 261, 270, 132, 23, 62, 142, 172, 13, 102,
-    192, 53, 122, 202, 162, 222, 43, 182, 73, 212, 242, 232, 252, 113, 262, 24,
+    32, 211, 241, 231, 82, 251, 112, 261, 132, 23, 62, 142, 172, 13, 102, 192,
+    53, 122, 270, 202, 162, 222, 43, 182, 73, 212, 242, 232, 252, 113, 262, 24,
     133, 14, 63, 54, 103, 123, 44, 173, 74, 193, 163, 183, 33, 114, 203, 83,
     134, 213, 143, 64, 233, 104, 253, 124, 223, 174, 243, 194, 263, 271, 164, 184,
     34, 204, 84, 26, 214, 144, 234, 254, 16, 224, 244, 56, 264, 76, 35, 46,
@@ -51,8 +51,8 @@
     10, 20, 30, 40, 50, 60, 70, 80, 100, 110, 120, 130, 140, 160, 170, 180,
     190, 1, 21, 200, 210, 11, 51, 220, 91, 230, 41, 71, 240, 250, 151, 260,
     111, 22, 131, 61, 12, 171, 101, 52, 191, 121, 201, 161, 42, 221, 181, 72,
-    2, 211, 241, 231, 92, 251, 112, 261, 270, 132, 62, 102, 122, 172, 192, 162,
-    182, 202, 152, 212, 232, 252, 222, 242, 262, 3, 93, 25, 153, 15, 55, 45,
+    2, 211, 241, 231, 92, 251, 112, 261, 132, 62, 102, 122, 172, 192, 162, 182,
+    202, 152, 270, 212, 232, 252, 222, 242, 262, 3, 93, 25, 153, 15, 55, 45,
     75, 271, 4, 94, 26, 154, 115, 65, 135, 105, 16, 125, 56, 175, 195, 165,
     5, 46, 185, 76, 27, 205, 66, 215, 95, 235, 225, 255, 17, 245, 116, 57,
     265, 155, 106, 136, 47, 126, 176, 77, 6, 166, 196, 67, 186, 206, 36, 117,

time: 64.7 us -> 64.6 us (level)
  no operation moved by 1% of the time
where the time goes in v7:
time: 64.6 us; the launch traced here: 64.5 us
  Pallas kernels  63.8 us (99%)
  between operations  0.72 us (1%)
    pallas_call x1, Pallas kernels, on_device(): pl.pallas_call(functools.partial(line_kernel, nx, ny), out_shape=(shape((...  43.2 us
    pallas_call x1, Pallas kernels, on_device(): pl.pallas_call(functools.partial(gather_kernel, nx, ny), out_shape=(shape...  11.7 us
    pallas_call x1, Pallas kernels, on_device(): pl.pallas_call(layer_kernel, out_shape=(shape((blocks, rows, width), bf16...  6.84 us
    pallas_call x1, Pallas kernels, on_device(): pl.pallas_call(store_kernel, out_shape=(shape((kvol, share, width), f32),...  2.04 us

profile of v7, /device:TPU:0, one launch (start us, length us, event | category | flops | bytes accessed | tf_op | source)
XLA Modules:
  0.0 64.5 jit_solution(14112614633873422862)
XLA Ops:
  0.6 0.0 copy-start
  0.6 0.0 copy-start.3
  0.7 0.0 copy-start.2
  0.7 0.0 copy-start.1
  0.7 11.7 %shard_map.103 = (bf16[24,128,256]{2,1,0:T(8,128)(2,1)S(1)}, bf16[24,256,128]{2,1,0:T(8,128)(2,1)S(1)}, bf16[27,2,128,256]{3,2,1,0:T(8,128)(2,1)S(1)}, f32[9,128,256]{2,1,0:T(8,128)S(1)}, f32[25,128,256]{2,1,0:T(8,128)S(1)}) custom-call(s32[2]{0:T(128)} %bitcast.23, bf16[8,128,256]{2,1,0:T(8,128)(2,1)} %bitcast.22, bf16[27,128,256]{2,1,0:T(8,128)(2,1)} %weight_ref.1, ...), custom_call_target="tpu_custom_call" | custom-call | tf_op jit(solution)/shard_map/pallas_call | solution.py:1209
  12.4 0.0 copy-done
  12.4 0.0 copy-done.3
  12.4 0.0 copy-done.2
  12.4 0.0 copy-done.1
  12.4 6.8 %shard_map.104 = (bf16[8,128,256]{2,1,0:T(8,128)(2,1)}, f32[9,128,256]{2,1,0:T(8,128)S(1)}, f32[25,128,256]{2,1,0:T(8,128)S(1)}, bf16[9,2,128,256]{3,2,1,0:T(8,128)(2,1)S(1)}, bf16[9,128,256]{2,1,0:T(8,128)(2,1)S(1)}) custom-call(s32[4,27]{1,0:T(4,128)S(1)} %bitcast.16, s32[4,27]{1,0:T(4,128)S(1)} %bitcast.18, ...), custom_call_target="tpu_custom_call", output_to_operand_aliasing={{1}: (6, {}), {2}: (7, {})} | custom-call | tf_op jit(solution)/shard_map/pallas_call | solution.py:1237
  19.3 43.2 %shard_map.105 = (f32[27,128,256]{2,1,0:T(8,128)S(1)}, bf16[8,128,256]{2,1,0:T(8,128)(2,1)S(1)}) custom-call(s32[4,27]{1,0:T(4,128)S(1)} %bitcast.17, s32[4,27]{1,0:T(4,128)S(1)} %bitcast.19, s32[27]{0:T(128)S(1)} %bitcast.21, s32[2]{0:T(128)} %bitcast.24, bf16[24,256,128]{2,1,0:T(8,128)(2,1)S(1)} %get-tuple-element.21.turned_ref, ...), custom_call_target="tpu_custom_call" | custom-call | tf_op jit(solution)/shard_map/pallas_call | solution.py:1259
  62.5 2.0 %shard_map.106 = (f32[27,128,256]{2,1,0:T(8,128)}, bf16[8,128,256]{2,1,0:T(8,128)(2,1)}) custom-call(f32[27,128,256]{2,1,0:T(8,128)S(1)} %get-tuple-element.25.wide_ref, bf16[8,128,256]{2,1,0:T(8,128)(2,1)S(1)} %get-tuple-element.26.feat_ref), custom_call_target="tpu_custom_call" | custom-call | tf_op jit(solution)/shard_map/pallas_call | solution.py:1292
Async XLA Ops:
  0.6 11.8 %copy-start = (bf16[1,1,8,128,256]{4,3,2,1,0:T(8,128)(2,1)S(1)}, bf16[1,1,8,128,256]{4,3,2,1,0:T(8,128)(2,1)}, u32[]{:S(2)}) copy-start(bf16[1,1,8,128,256]{4,3,2,1,0:T(8,128)(2,1)} %param.15) | copy-start | bytes 1572868
  0.6 11.8 %copy-start.3 = (s32[1,1,27]{2,1,0:T(1,128)S(1)}, s32[1,1,27]{2,1,0:T(1,128)}, u32[]{:S(2)}) copy-start(s32[1,1,27]{2,1,0:T(1,128)} %param.14) | copy-start | bytes 328
  0.7 11.8 %copy-start.2 = (s32[1,1,27,4]{2,3,1,0:T(4,128)S(1)}, s32[1,1,27,4]{2,3,1,0:T(4,128)}, u32[]{:S(2)}) copy-start(s32[1,1,27,4]{2,3,1,0:T(4,128)} %param.13) | copy-start | bytes 1300
  0.7 11.8 %copy-start.1 = (s32[1,1,27,4]{2,3,1,0:T(4,128)S(1)}, s32[1,1,27,4]{2,3,1,0:T(4,128)}, u32[]{:S(2)}) copy-start(s32[1,1,27,4]{2,3,1,0:T(4,128)} %param.12) | copy-start | bytes 1300

commit v8 on v7

--- a/solution.py
+++ b/solution.py
@@ -679,6 +679,7 @@
             x_copy(a, me_x + a - 1).wait_recv()
             to_column(a, lambda copy: copy.start())
 
+    for a in (0, 2):
         turn(first(a, 1), shared_count)
     for a in (0, 2):
         for b in (0, 2):
@@ -750,7 +751,7 @@
         )
         return carry
 
-    lax.fori_loop(0, blocks, activate, 0)
+    lax.fori_loop(0, blocks, activate, 0, unroll=4)
     keep = pltpu.make_async_copy(out, out_ref, osem)
     keep.start()
 

time: 64.6 us -> 64.6 us (level)
  no operation moved by 1% of the time
where the time goes in v8:
time: 64.6 us; the launch traced here: 64.4 us
  Pallas kernels  63.7 us (99%)
  between operations  0.72 us (1%)
    pallas_call x1, Pallas kernels, on_device(): pl.pallas_call(functools.partial(line_kernel, nx, ny), out_shape=(shape((...  43.2 us
    pallas_call x1, Pallas kernels, on_device(): pl.pallas_call(functools.partial(gather_kernel, nx, ny), out_shape=(shape...  11.7 us
    pallas_call x1, Pallas kernels, on_device(): pl.pallas_call(layer_kernel, out_shape=(shape((blocks, rows, width), bf16...  6.77 us
    pallas_call x1, Pallas kernels, on_device(): pl.pallas_call(store_kernel, out_shape=(shape((kvol, share, width), f32),...  2.04 us

profile of v8, /device:TPU:0, one launch (start us, length us, event | category | flops | bytes accessed | tf_op | source)
XLA Modules:
  0.0 64.4 jit_solution(7283509073797995251)
XLA Ops:
  0.6 0.0 copy-start
  0.6 0.0 copy-start.3
  0.7 0.0 copy-start.2
  0.7 0.0 copy-start.1
  0.7 11.7 %shard_map.103 = (bf16[24,128,256]{2,1,0:T(8,128)(2,1)S(1)}, bf16[24,256,128]{2,1,0:T(8,128)(2,1)S(1)}, bf16[27,2,128,256]{3,2,1,0:T(8,128)(2,1)S(1)}, f32[9,128,256]{2,1,0:T(8,128)S(1)}, f32[25,128,256]{2,1,0:T(8,128)S(1)}) custom-call(s32[2]{0:T(128)} %bitcast.23, bf16[8,128,256]{2,1,0:T(8,128)(2,1)} %bitcast.22, bf16[27,128,256]{2,1,0:T(8,128)(2,1)} %weight_ref.1, ...), custom_call_target="tpu_custom_call" | custom-call | tf_op jit(solution)/shard_map/pallas_call | solution.py:1210
  12.4 0.0 copy-done
  12.4 0.0 copy-done.3
  12.4 0.0 copy-done.2
  12.4 0.0 copy-done.1
  12.4 6.8 %shard_map.104 = (bf16[8,128,256]{2,1,0:T(8,128)(2,1)}, f32[9,128,256]{2,1,0:T(8,128)S(1)}, f32[25,128,256]{2,1,0:T(8,128)S(1)}, bf16[9,2,128,256]{3,2,1,0:T(8,128)(2,1)S(1)}, bf16[9,128,256]{2,1,0:T(8,128)(2,1)S(1)}) custom-call(s32[4,27]{1,0:T(4,128)S(1)} %bitcast.16, s32[4,27]{1,0:T(4,128)S(1)} %bitcast.18, ...), custom_call_target="tpu_custom_call", output_to_operand_aliasing={{1}: (6, {}), {2}: (7, {})} | custom-call | tf_op jit(solution)/shard_map/pallas_call | solution.py:1238
  19.2 43.2 %shard_map.105 = (f32[27,128,256]{2,1,0:T(8,128)S(1)}, bf16[8,128,256]{2,1,0:T(8,128)(2,1)S(1)}) custom-call(s32[4,27]{1,0:T(4,128)S(1)} %bitcast.17, s32[4,27]{1,0:T(4,128)S(1)} %bitcast.19, s32[27]{0:T(128)S(1)} %bitcast.21, s32[2]{0:T(128)} %bitcast.24, bf16[24,256,128]{2,1,0:T(8,128)(2,1)S(1)} %get-tuple-element.21.turned_ref, ...), custom_call_target="tpu_custom_call" | custom-call | tf_op jit(solution)/shard_map/pallas_call | solution.py:1260
  62.4 2.0 %shard_map.106 = (f32[27,128,256]{2,1,0:T(8,128)}, bf16[8,128,256]{2,1,0:T(8,128)(2,1)}) custom-call(f32[27,128,256]{2,1,0:T(8,128)S(1)} %get-tuple-element.25.wide_ref, bf16[8,128,256]{2,1,0:T(8,128)(2,1)S(1)} %get-tuple-element.26.feat_ref), custom_call_target="tpu_custom_call" | custom-call | tf_op jit(solution)/shard_map/pallas_call | solution.py:1293
Async XLA Ops:
  0.6 11.8 %copy-start = (bf16[1,1,8,128,256]{4,3,2,1,0:T(8,128)(2,1)S(1)}, bf16[1,1,8,128,256]{4,3,2,1,0:T(8,128)(2,1)}, u32[]{:S(2)}) copy-start(bf16[1,1,8,128,256]{4,3,2,1,0:T(8,128)(2,1)} %param.15) | copy-start | bytes 1572868
  0.6 11.8 %copy-start.3 = (s32[1,1,27]{2,1,0:T(1,128)S(1)}, s32[1,1,27]{2,1,0:T(1,128)}, u32[]{:S(2)}) copy-start(s32[1,1,27]{2,1,0:T(1,128)} %param.14) | copy-start | bytes 328
  0.7 11.8 %copy-start.2 = (s32[1,1,27,4]{2,3,1,0:T(4,128)S(1)}, s32[1,1,27,4]{2,3,1,0:T(4,128)}, u32[]{:S(2)}) copy-start(s32[1,1,27,4]{2,3,1,0:T(4,128)} %param.13) | copy-start | bytes 1300
  0.7 11.8 %copy-start.1 = (s32[1,1,27,4]{2,3,1,0:T(4,128)S(1)}, s32[1,1,27,4]{2,3,1,0:T(4,128)}, u32[]{:S(2)}) copy-start(s32[1,1,27,4]{2,3,1,0:T(4,128)} %param.12) | copy-start | bytes 1300
